TPU v7x, 512 devices: a whole 4x4x16 slice. The times are simulated.
512 devices in a mesh: src: 128 (over y, z, core), seg: 4 (over x).
Axes of the slice: x: 4, y: 4, z: 16, core: 2. Of those that a mesh axis runs over, the one named last changes fastest.
Arguments:
- residual: float32 [8388608], P(('src', 'seg')), may hold values from -24 to 24
- obs_weight: float32 [8388608], P(('src', 'seg')), may hold values from 0.25 to 4
- time_frac: float32 [8388608], P(('src', 'seg')), may hold values from 0 to 0.99
- src_partials: float32 [5, 8388608], P(None, ('src', 'seg')), may hold values from -6 to 6
- att_dir: float32 [3, 8388608], P(None, ('src', 'seg')), may hold values from -6 to 6
- src_prior: float32 [5, 262144], P(None, 'src'), may hold values from 4 to 40
- att_prior: float32 [3, 32768], P(None, ('src', 'seg')), may hold values from 16 to 128
- obs_source: int32 [8388608], P(('src', 'seg')), may hold values from 0 to 2047, as said below
- obs_interval: int32 [8388608], P(('src', 'seg')), may hold values from 0 to 32767, as said below
- obs_count: int32 [512, 128], P(('src', 'seg')), may hold values from 16 to 128, as said below
Outputs:
- src_update: float32 [5, 262144], P(None, 'src')
- att_update: float32 [3, 32768], P(None, ('src', 'seg'))
- residual_out: float32 [8388608], P(('src', 'seg'))
Inputs may be any that keep to these rules, and one draw needn't show every extreme that they name: obs_source of a slot on row r of obs_count (slot i with r = i // 16384) is the index of its source within the src block r // 4. A slot of row r in block b has an interval owned by knot block t = b * 4 + (r mod 4): obs_interval lies in t * 64 to (t + 1) * 64 - 1. `obs_count`: row r counts the live slots, from the start, of the 128 blocks of device r; for every seg index one block index is full (128) on every row of that seg index.
All inputs are finite; a program needn't handle non-finite values.
Results may differ from a plain program's by a relative error of at most 0.0003.
Values sent between devices are 32-bit elements; how exact they have to be, the bound alone decides.
No kernel may reach another device: no remote copies, remote signals or barrier semaphores. Data moves between devices by JAX's collectives and lax.ppermute only.
A program may use at most 128 MiB of HBM per device.

v0:
```python
import jax
import jax.numpy as jnp
from jax import lax
from jax.sharding import PartitionSpec as P

ITERS_ATT = 6


param_pairs = [
    (0, 0),
    (0, 1),
    (0, 2),
    (0, 3),
    (0, 4),
    (1, 1),
    (1, 2),
    (1, 3),
    (1, 4),
    (2, 2),
    (2, 3),
    (2, 4),
    (3, 3),
    (3, 4),
    (4, 4),
]
sym_pairs = [(0, 0), (0, 1), (0, 2), (1, 1), (1, 2), (2, 2)]
damping = 0.5


def with_halo(cells, sides, width):
    for axis, dim in sides:
        count = lax.axis_size(axis)
        ends = count - 1
        head = lax.slice_in_dim(cells, 0, width, axis=dim)
        tail = lax.slice_in_dim(cells, cells.shape[dim] - width, cells.shape[dim], axis=dim)
        cells = jnp.concatenate(
            [
                lax.ppermute(tail, axis, [(i, (i + 1) % count) for i in range(ends)]),
                cells,
                lax.ppermute(head, axis, [((i + 1) % count, i) for i in range(ends)]),
            ],
            axis=dim,
        )
    return cells


def from_behind(array, axis, by):
    size = lax.axis_size(axis)
    pairs = [(i, i + by) for i in range(size) if 0 <= i + by < size]
    return lax.ppermute(array, axis, pairs)


def cholesky_solve5(normal, rhs_terms, prior_diag):
    matrix = {}
    for number, pair_at in enumerate(param_pairs):
        matrix[pair_at] = normal[number]
        matrix[pair_at[1], pair_at[0]] = normal[number]
    for number in range(5):
        matrix[number, number] = matrix[number, number] + prior_diag[number]
    factor = {}
    for row_at in range(5):
        for col_at in range(row_at + 1):
            running = matrix[row_at, col_at]
            for inner_k in range(col_at):
                running = running - factor[row_at, inner_k] * factor[col_at, inner_k]
            if row_at == col_at:
                factor[row_at, row_at] = jnp.sqrt(running)
            else:
                factor[row_at, col_at] = running / factor[col_at, col_at]
    forward = []
    for row_at in range(5):
        running = rhs_terms[row_at]
        for inner_k in range(row_at):
            running = running - factor[row_at, inner_k] * forward[inner_k]
        forward.append(running / factor[row_at, row_at])
    backward = [None] * 5
    for row_at in reversed(range(5)):
        running = forward[row_at]
        for inner_k in range(row_at + 1, 5):
            running = running - factor[inner_k, row_at] * backward[inner_k]
        backward[row_at] = running / factor[row_at, row_at]
    return jnp.stack(backward)


def spline_basis(local_time):
    floor_part = jnp.floor(local_time)
    frac_part = local_time - floor_part
    square = frac_part * frac_part
    cube_term = square * frac_part
    rest = 1.0 - frac_part
    splines = [
        rest * rest * rest / 6.0,
        (3.0 * cube_term - 6.0 * square + 4.0) / 6.0,
        (-3.0 * cube_term + 3.0 * square + 3.0 * frac_part + 1.0) / 6.0,
        cube_term / 6.0,
    ]
    return (floor_part.astype(jnp.int32), splines)


def band_sums(direction, pair_weight, rhs_vec, local_time, knots):
    floor_at, splines = spline_basis(local_time)
    knot_ids = jnp.arange(knots + 3, dtype=jnp.int32)
    outer_terms = []
    for left_at, right_at in sym_pairs:
        entry_term = direction[left_at] * direction[right_at]
        entry_term = pair_weight * entry_term
        outer_terms.append(entry_term)
    total = None
    for spline_at in range(4):
        choice_mask = (floor_at[..., None] + spline_at == knot_ids).astype(jnp.float32)
        column_list = []
        for offset in range(4 - spline_at):
            coeff_pair = splines[spline_at] * splines[spline_at + offset]
            for entry_term in outer_terms:
                column_list.append(coeff_pair * entry_term)
        scaled = rhs_vec * splines[spline_at]
        for axis_at in range(3):
            column_list.append(scaled * direction[axis_at])
        accumulated_sum = jnp.einsum(
            "gyf,yfm->gym", jnp.stack(column_list), choice_mask, precision=lax.Precision.HIGHEST
        )
        lead = 6 * (4 - spline_at)
        blank = jnp.zeros((6 * spline_at,) + accumulated_sum.shape[1:], jnp.float32)
        filled = jnp.concatenate([accumulated_sum[:lead], blank, accumulated_sum[lead:]], 0)
        total = filled if total is None else total + filled
    return (total, floor_at, splines)


def sym_apply(entries, vector):
    first_row = entries[0] * vector[0] + entries[1] * vector[1] + entries[2] * vector[2]
    middle_row_entries = entries[1] * vector[0] + entries[3] * vector[1] + entries[4] * vector[2]
    third_row = entries[2] * vector[0] + entries[4] * vector[1] + entries[5] * vector[2]
    return jnp.stack([first_row, middle_row_entries, third_row])


def symmetric_inverse(entries):
    cof_00 = entries[3] * entries[5] - entries[4] * entries[4]
    cof_01 = entries[2] * entries[4] - entries[1] * entries[5]
    cof_02 = entries[1] * entries[4] - entries[2] * entries[3]
    cof_11 = entries[0] * entries[5] - entries[2] * entries[2]
    cof_12 = entries[1] * entries[2] - entries[0] * entries[4]
    cof_22 = entries[0] * entries[3] - entries[1] * entries[1]
    determinant = entries[0] * cof_00 + entries[1] * cof_01 + entries[2] * cof_02
    return jnp.stack([cof_00, cof_01, cof_02, cof_11, cof_12, cof_22]) / determinant


def add_prior(diag_sums, prior_diag):
    return jnp.stack(
        [
            diag_sums[0] + prior_diag[0],
            diag_sums[1],
            diag_sums[2],
            diag_sums[3] + prior_diag[1],
            diag_sums[4],
            diag_sums[5] + prior_diag[2],
        ]
    )


def apply_operator(diag_block, upper_triangle_filled, vector_padded, knot_count):
    applied = sym_apply(diag_block, vector_padded[:, 3 : 3 + knot_count])
    for offset in range(1, 4):
        upper_here = upper_triangle_filled[6 * (offset - 1) : 6 * offset, 3 : 3 + knot_count]
        upper_left = upper_triangle_filled[
            6 * (offset - 1) : 6 * offset, 3 - offset : 3 - offset + knot_count
        ]
        applied = applied + sym_apply(
            upper_here, vector_padded[:, 3 + offset : 3 + offset + knot_count]
        )
        applied = applied + sym_apply(
            upper_left, vector_padded[:, 3 - offset : 3 - offset + knot_count]
        )
    return applied


def body(
    residual,
    obs_weight,
    time_frac,
    src_partials,
    att_dir,
    src_prior,
    att_prior,
    obs_source,
    obs_interval,
    obs_count,
):
    src_count = lax.axis_size("src")
    obs_local = residual.shape[0]
    capacity = obs_local // src_count
    sources = src_prior.shape[1]
    knots = att_prior.shape[1]
    slot_ok = jnp.arange(capacity, dtype=jnp.int32)[None, :] < obs_count[0][:, None]
    live_mask = slot_ok.reshape(-1).astype(jnp.float32)
    weight = obs_weight * live_mask
    features = []
    for left_at, right_at in param_pairs:
        features.append(weight * src_partials[left_at] * src_partials[right_at])
    for axis_at in range(5):
        features.append(weight * src_partials[axis_at] * residual)
    src_sums = jax.ops.segment_sum(jnp.stack(features, 1), obs_source, num_segments=sources).T
    full_sums = lax.psum(src_sums, "seg")
    src_update = cholesky_solve5(full_sums[:15], full_sums[15:], src_prior)
    src_corr = jnp.sum(src_partials * jnp.take(src_update, obs_source, axis=1), 0)
    first_pass = residual - src_corr
    local_time = (obs_interval % knots).astype(jnp.float32) + time_frac
    packed = jnp.stack(
        [first_pass, weight, local_time, att_dir[0], att_dir[1], att_dir[2]]
    ).reshape(6, src_count, capacity)
    incoming_values = lax.all_to_all(packed, "src", split_axis=1, concat_axis=1, tiled=True)
    arrived = incoming_values.reshape(6, 1, obs_local)
    band_total, arrived_floor, arrived_splines = band_sums(
        arrived[3:6], arrived[1], arrived[1] * arrived[0], arrived[2], knots
    )
    ext_sums = band_total[:, 0, :]
    zero_col = jnp.zeros((27,), jnp.float32)
    edge_cols = jnp.stack(
        [ext_sums[:, 0], zero_col, ext_sums[:, knots + 1], ext_sums[:, knots + 2]], 1
    )
    edge_rims = with_halo(edge_cols, ((("src", "seg"), 1),), 2)
    own_sums = ext_sums[:, 1 : knots + 1]
    own_sums = own_sums.at[:, 0:2].add(edge_rims[:, 0:2])
    own_sums = own_sums.at[:, knots - 1].add(edge_rims[:, 6])
    diag_block = add_prior(own_sums[:6], att_prior)
    inverse = symmetric_inverse(diag_block)
    att_rhs = own_sums[24:27]
    lower_rim = from_behind(own_sums[6:24, knots - 3 : knots], ("src", "seg"), 1)
    upper_triangle_filled = jnp.concatenate([lower_rim, own_sums[6:24]], 1)
    att_update = damping * sym_apply(inverse, att_rhs)
    for sweep_at in range(1, ITERS_ATT):
        vector_padded = with_halo(att_update, ((("src", "seg"), 1),), 3)
        att_update = att_update + damping * sym_apply(
            inverse,
            att_rhs - apply_operator(diag_block, upper_triangle_filled, vector_padded, knots),
        )
    final_padded = with_halo(att_update, ((("src", "seg"), 1),), 3)
    arrived_dir = arrived[3:6, 0]
    correction = jnp.zeros((obs_local,), jnp.float32)
    for spline_at in range(4):
        looked = jnp.take(final_padded, arrived_floor[0] + spline_at + 2, axis=1)
        correction = correction + arrived_splines[spline_at][0] * jnp.sum(arrived_dir * looked, 0)
    returned = lax.all_to_all(
        correction.reshape(src_count, capacity), "src", split_axis=0, concat_axis=0, tiled=True
    )
    att_corr = returned.reshape(-1)
    residual_out = residual - live_mask * (src_corr + att_corr)
    return (src_update, att_update, residual_out)


def solution(mesh):
    in_specs = (
        P(("src", "seg")),
        P(("src", "seg")),
        P(("src", "seg")),
        P(None, ("src", "seg")),
        P(None, ("src", "seg")),
        P(None, "src"),
        P(None, ("src", "seg")),
        P(("src", "seg")),
        P(("src", "seg")),
        P(("src", "seg"), None),
    )
    out_specs = (P(None, "src"), P(None, ("src", "seg")), P(("src", "seg")))
    return jax.shard_map(body, mesh=mesh, in_specs=in_specs, out_specs=out_specs, check_vma=False)
```

profile of v0, /device:TPU:1, one launch (start us, length us, event | category | flops | bytes accessed | tf_op | source)
XLA Modules:
  0.0 673.1 jit_solution(11265447645809301933)
XLA Ops:
  13.7 4.7 copy.225
  18.5 87.9 %scatter_custom_fusion = f32[2048,20]{1,0:T(8,128)S(1)} fusion(s32[16384]{0:T(1024)S(1)} %copy-done.2, f32[16384,20]{1,0:T(8,128)} %copy.225, f32[]{:T(128)} %constant.116.clone.1), kind=kCustom, calls=%fused_computation.49 | custom fusion | flops 327680 | bytes 164352 | tf_op jit(solution)/shard_map/scatter-add | solution.py:201
  107.6 5.3 copy.228
  113.0 54.9 %all-reduce.2.cloned.1.call-done = f32[20,2048]{1,0:T(8,128)} async-done(((f32[20,2048]{1,0:T(8,128)}), f32[20,2048]{1,0:T(8,128)}) %all-reduce.2.cloned.1.call-update) | async-done | bytes 163856 | tf_op jit(solution)/shard_map/psum | solution.py:202
  172.1 54.5 %gather_fusion = f32[16384,5]{1,0:T(8,128)} fusion(f32[5,2048]{0,1:T(8,128)S(1)} %copy.227, s32[16384]{0:T(1024)S(1)} %fusion.89), kind=kCustom, calls=%fused_computation.4 | custom fusion | bytes 720896 | tf_op jit(solution)/shard_map/jit(_take)/gather | solution.py:204
  226.6 7.5 %fusion.4 = f32[16384]{0:T(1024)S(1)} fusion(f32[5,16384]{0,1:T(8,128)} %copy.228, f32[16384,5]{1,0:T(8,128)} %gather_fusion, pred[16384]{0:T(1024)(128)(4,1)S(1)} %compare_and_fusion.4), kind=kLoop, calls=%fused_computation.15 | loop fusion | flops 229376 | bytes 737280 | tf_op jit(solution)/shard_map/reduce_sum | solution.py:204
  235.2 18.7 %all-to-all-start = ((f32[6,128,128]{2,0,1:T(8,128)}), f32[6,128,128]{2,0,1:T(8,128)S(1)}, u32[]{:S(2)}, u32[]{:S(2)}) async-start(f32[6,128,128]{2,0,1:T(8,128)} %pad_maximum_fusion), calls=%async_computation | async-start | bytes 1048576 | tf_op jit(solution)/shard_map/all_to_all | solution.py:210
  254.9 32.2 %all-to-all-done = f32[6,128,128]{2,0,1:T(8,128)S(1)} async-done(((f32[6,128,128]{2,0,1:T(8,128)}), f32[6,128,128]{2,0,1:T(8,128)S(1)}, u32[]{:S(2)}, u32[]{:S(2)}) %all-to-all-start) | async-done | bytes 393248 | tf_op jit(solution)/shard_map/all_to_all | solution.py:210
  308.1 4.8 collective-permute-start.1
  312.9 4.9 copy.238
  321.2 4.9 collective-permute-start.2
  328.3 4.0 collective-permute-done.3
  334.9 4.9 collective-permute-start.5
  341.1 3.6 collective-permute-start.8
  344.7 3.7 collective-permute-start.7
  352.6 6.0 collective-permute-start.10
  363.6 4.6 collective-permute-start.12
  373.2 4.6 collective-permute-start.13
  382.4 54.5 %gather_fusion.4 = f32[16384,3]{1,0:T(8,128)} fusion(f32[3,70]{0,1:T(8,128)S(1)} %copy.239, s32[16384]{0:T(1024)S(1)} %get-tuple-element.189), kind=kCustom, calls=%fused_computation.3.clone | custom fusion | bytes 458752 | tf_op jit(solution)/shard_map/jit(_take)/gather | solution.py:240
  436.8 54.5 %gather_fusion.3 = f32[16384,3]{1,0:T(8,128)} fusion(f32[3,70]{0,1:T(8,128)S(1)} %copy.239, s32[16384]{0:T(1024)S(1)} %get-tuple-element.193), kind=kCustom, calls=%fused_computation.2.clone | custom fusion | bytes 458752 | tf_op jit(solution)/shard_map/jit(_take)/gather | solution.py:240
  491.3 54.5 %gather_fusion.2 = f32[16384,3]{1,0:T(8,128)} fusion(f32[3,70]{0,1:T(8,128)S(1)} %copy.239, s32[16384]{0:T(1024)S(1)} %get-tuple-element.195), kind=kCustom, calls=%fused_computation.1.clone | custom fusion | bytes 458752 | tf_op jit(solution)/shard_map/jit(_take)/gather | solution.py:240
  545.8 54.5 %gather_fusion.1 = f32[16384,3]{1,0:T(8,128)} fusion(f32[3,70]{0,1:T(8,128)S(1)} %copy.239, s32[16384]{0:T(1024)S(1)} %get-tuple-element.194), kind=kCustom, calls=%fused_computation.clone | custom fusion | bytes 458752 | tf_op jit(solution)/shard_map/jit(_take)/gather | solution.py:240
  600.3 26.1 %fusion.3 = (f32[16384]{0:T(1024)S(1)}, f32[16384]{0:T(1024)S(1)}, f32[16384]{0:T(1024)S(1)}, f32[16384]{0:T(1024)S(1)}) fusion(f32[3,128,128]{0,2,1:T(8,128)} %copy.238, f32[16384,3]{1,0:T(8,128)} %gather_fusion.1, pred[16384]{0:T(1024)(128)(4,1)S(1)} %get-tuple-element.187, f32[16384,3]{1,0:T(8,128)} %gather_fusion.2, ...), kind=kLoop, calls=%fused_computation.13 | loop fusion | flops 524288 | bytes 1310720 | tf_op jit(solution)/shard_map/reduce_sum | solution.py:241
  626.5 39.1 %all_to_all.11 = f32[128,1,128]{2,1,0:T(1,128)S(1)} all-to-all(f32[128,1,128]{2,1,0:T(1,128)S(1)} %bitcast.398), channel_id=1, replica_groups=mesh['src'=128,'seg'=4] {'src'}, dimensions={0} | all-to-all | bytes 131072 | tf_op jit(solution)/shard_map/all_to_all | solution.py:242
  (197 shorter events, 63.3 us)
Async XLA Ops:
  7.2 160.7 %all-reduce.2.cloned.1.call-start = ((), (), s32[]{:S(2)}) async-start(), calls=%async_computation.2 | async-start | bytes 393216 | tf_op jit(solution)/shard_map/psum | solution.py:202
  18.5 89.0 %copy-start.5 = (f32[16384]{0:T(1024)S(1)}, f32[16384]{0:T(1024)}, u32[]{:S(2)}) copy-start(f32[16384]{0:T(1024)} %param.18) | copy-start | bytes 196612
  18.5 89.0 %copy-start.6 = (s32[16384]{0:T(1024)S(1)}, s32[16384]{0:T(1024)}, u32[]{:S(2)}) copy-start(s32[16384]{0:T(1024)} %param.24) | copy-start | bytes 196612
  18.5 89.1 %copy-start = (f32[5,16384]{1,0:T(8,128)S(1)}, f32[5,16384]{1,0:T(8,128)}, u32[]{:S(2)}) copy-start(f32[5,16384]{1,0:T(8,128)} %param.19) | copy-start | bytes 983044
  107.6 60.2 %copy-start.8 = (f32[5,2048]{1,0:T(8,128)S(1)}, f32[5,2048]{1,0:T(8,128)}, u32[]{:S(2)}) copy-start(f32[5,2048]{1,0:T(8,128)} %param.21) | copy-start | bytes 122884
  171.7 54.9 %copy-start.3 = (f32[5,2048]{1,0:T(8,128)}, f32[5,2048]{1,0:T(8,128)S(1)}, u32[]{:S(2)}) copy-start(f32[5,2048]{1,0:T(8,128)S(1)} %stack.171) | copy-start | bytes 122884
  235.2 52.0 %all-to-all-start = ((f32[6,128,128]{2,0,1:T(8,128)}), f32[6,128,128]{2,0,1:T(8,128)S(1)}, u32[]{:S(2)}, u32[]{:S(2)}) async-start(f32[6,128,128]{2,0,1:T(8,128)} %pad_maximum_fusion), calls=%async_computation | async-start | bytes 1048576 | tf_op jit(solution)/shard_map/all_to_all | solution.py:210
  306.1 11.8 %collective-permute-start = (f32[27,2]{1,0:T(8,128)S(1)}, f32[27,2]{1,0:T(8,128)S(1)}, u32[]{:S(2)}, u32[]{:S(2)}) collective-permute-start(f32[27,2]{1,0:T(8,128)S(1)} %get-tuple-element.309), channel_id=1, source_target_pairs={{0,1},{1,2},{2,3},{3,4},{4,5},{5,6},{6,7},{7,8},{8,9},{9,10},{10,1... | collective-permute-start | bytes 656 | tf_op jit(solution)/shard_map/ppermute | solution.py:38
  308.1 10.7 %collective-permute-start.1 = (f32[27,2]{1,0:T(8,128)S(1)}, f32[27,2]{1,0:T(8,128)S(1)}, u32[]{:S(2)}, u32[]{:S(2)}) collective-permute-start(f32[27,2]{1,0:T(8,128)S(1)} %get-tuple-element.308), channel_id=1, source_target_pairs={{1,0},{2,1},{3,2},{4,3},{5,4},{6,5},{7,6},{8,7},{9,8},{10,9},{11,1... | collective-permute-start | bytes 656 | tf_op jit(solution)/shard_map/ppermute | solution.py:40
  319.3 8.7 %collective-permute-start.4 = (f32[3,3]{1,0:T(4,128)S(1)}, f32[3,3]{1,0:T(4,128)S(1)}, u32[]{:S(2)}, u32[]{:S(2)}) collective-permute-start(f32[3,3]{1,0:T(4,128)S(1)} %get-tuple-element.381), channel_id=1, source_target_pairs={{0,1},{1,2},{2,3},{3,4},{4,5},{5,6},{6,7},{7,8},{8,9},{9,10},{10,1... | collective-permute-start | bytes 116 | tf_op jit(solution)/shard_map/ppermute | solution.py:38
  321.2 6.8 %collective-permute-start.2 = (f32[3,3]{1,0:T(4,128)S(1)}, f32[3,3]{1,0:T(4,128)S(1)}, u32[]{:S(2)}, u32[]{:S(2)}) collective-permute-start(f32[3,3]{1,0:T(4,128)S(1)} %get-tuple-element.382), channel_id=1, source_target_pairs={{1,0},{2,1},{3,2},{4,3},{5,4},{6,5},{7,6},{8,7},{9,8},{10,9},{11,1... | collective-permute-start | bytes 116 | tf_op jit(solution)/shard_map/ppermute | solution.py:40
  326.1 6.2 collective-permute-start.3
  332.9 6.8 %collective-permute-start.6 = (f32[3,3]{1,0:T(4,128)S(1)}, f32[3,3]{1,0:T(4,128)S(1)}, u32[]{:S(2)}, u32[]{:S(2)}) collective-permute-start(f32[3,3]{1,0:T(4,128)S(1)} %get-tuple-element.377), channel_id=1, source_target_pairs={{0,1},{1,2},{2,3},{3,4},{4,5},{5,6},{6,7},{7,8},{8,9},{9,10},{10,1... | collective-permute-start | bytes 116 | tf_op jit(solution)/shard_map/ppermute | solution.py:38
  334.9 5.6 collective-permute-start.5
  341.1 7.3 %collective-permute-start.8 = (f32[3,3]{1,0:T(4,128)S(1)}, f32[3,3]{1,0:T(4,128)S(1)}, u32[]{:S(2)}, u32[]{:S(2)}) collective-permute-start(f32[3,3]{1,0:T(4,128)S(1)} %get-tuple-element.373), channel_id=1, source_target_pairs={{0,1},{1,2},{2,3},{3,4},{4,5},{5,6},{6,7},{7,8},{8,9},{9,10},{10,1... | collective-permute-start | bytes 116 | tf_op jit(solution)/shard_map/ppermute | solution.py:38
  344.7 7.3 %collective-permute-start.7 = (f32[3,3]{1,0:T(4,128)S(1)}, f32[3,3]{1,0:T(4,128)S(1)}, u32[]{:S(2)}, u32[]{:S(2)}) collective-permute-start(f32[3,3]{1,0:T(4,128)S(1)} %get-tuple-element.374), channel_id=1, source_target_pairs={{1,0},{2,1},{3,2},{4,3},{5,4},{6,5},{7,6},{8,7},{9,8},{10,9},{11,1... | collective-permute-start | bytes 116 | tf_op jit(solution)/shard_map/ppermute | solution.py:40
  352.6 8.0 %collective-permute-start.10 = (f32[3,3]{1,0:T(4,128)S(1)}, f32[3,3]{1,0:T(4,128)S(1)}, u32[]{:S(2)}, u32[]{:S(2)}) collective-permute-start(f32[3,3]{1,0:T(4,128)S(1)} %get-tuple-element.369), channel_id=1, source_target_pairs={{0,1},{1,2},{2,3},{3,4},{4,5},{5,6},{6,7},{7,8},{8,9},{9,10},{10,1... | collective-permute-start | bytes 116 | tf_op jit(solution)/shard_map/ppermute | solution.py:38
  358.6 4.3 collective-permute-start.9
  363.6 6.8 %collective-permute-start.12 = (f32[3,3]{1,0:T(4,128)S(1)}, f32[3,3]{1,0:T(4,128)S(1)}, u32[]{:S(2)}, u32[]{:S(2)}) collective-permute-start(f32[3,3]{1,0:T(4,128)S(1)} %get-tuple-element.365), channel_id=1, source_target_pairs={{0,1},{1,2},{2,3},{3,4},{4,5},{5,6},{6,7},{7,8},{8,9},{9,10},{10,1... | collective-permute-start | bytes 116 | tf_op jit(solution)/shard_map/ppermute | solution.py:38
  368.2 4.3 collective-permute-start.11
  373.1 118.2 %copy-start.7 = (f32[3,64]{1,0:T(4,128)}, f32[3,64]{1,0:T(4,128)S(1)}, u32[]{:S(2)}) copy-start(f32[3,64]{1,0:T(4,128)S(1)} %fusion.154) | copy-start | bytes 2308
  373.2 6.8 %collective-permute-start.13 = (f32[3,3]{1,0:T(4,128)S(1)}, f32[3,3]{1,0:T(4,128)S(1)}, u32[]{:S(2)}, u32[]{:S(2)}) collective-permute-start(f32[3,3]{1,0:T(4,128)S(1)} %get-tuple-element.361), channel_id=1, source_target_pairs={{0,1},{1,2},{2,3},{3,4},{4,5},{5,6},{6,7},{7,8},{8,9},{9,10},{10,1... | collective-permute-start | bytes 116 | tf_op jit(solution)/shard_map/ppermute | solution.py:38
  377.8 4.3 collective-permute-start.14
  600.3 65.3 %copy-start.9 = (s32[1,128]{1,0:T(1,128)S(1)}, s32[1,128]{1,0:T(1,128)}, u32[]{:S(2)}) copy-start(s32[1,128]{1,0:T(1,128)} %param.25) | copy-start | bytes 1540
  (5 other events, 32.3 us)
Sparse Core Ops, SparseCore 0:
  107.6 60.2 all-reduce.1
where the time goes:
time: 676 us; the launch traced here: 673 us
  local copies, waits for them, and re-layouts  295 us (44%)
  other arithmetic  141 us (21%)
  waiting for transfers between devices  102 us (15%)
  starting transfers between devices  69.8 us (10%)
  blocking collectives  39.1 us (6%)
  between operations  14.9 us (2%)
  matrix products  11.2 us (2%)
    gather x4, local copies, waits for them, and re-layouts, body(): looked = jnp.take(final_padded, arrived_floor[0] + spline_at + 2, axis=1)  218 us
    scatter-add x1, other arithmetic, body(): jax.ops.segment_sum(jnp.stack(features, 1), obs_source, num_segments=sour...  87.9 us
    psum x1, waiting for transfers between devices, body(): full_sums = lax.psum(src_sums, 'seg')  54.9 us
    gather x1, local copies, waits for them, and re-layouts, body(): jnp.take(src_update, obs_source, axis=1)  54.5 us
    all_to_all x1, blocking collectives, body(): lax.all_to_all(correction.reshape(src_count, capacity), 'src', split_axis...  39.1 us
    all_to_all x1, waiting for transfers between devices, body(): lax.all_to_all(packed, 'src', split_axis=1, concat_axis=1, tiled=True)  32.2 us
    reduce_sum x1, other arithmetic, body(): jnp.sum(arrived_dir * looked, 0)  26.1 us
    ppermute x7, starting transfers between devices, with_halo(): lax.ppermute(tail, axis, [(i, (i + 1) % count) for i in range(ends)])  24.7 us
  transfers between devices with their start and end apart: 17, of which 8 were waited for; matrix products, arithmetic and copies ran while one was open for 2% of the time, Pallas kernels for 0%

commit v1 on v0

v1 whole, which is shorter than its diff:
```python
import functools

import jax
import jax.numpy as jnp
from jax import lax
from jax.experimental import pallas as pl
from jax.experimental.pallas import tpu as pltpu
from jax.sharding import PartitionSpec as P

ITERS_ATT = 6
DAMPING = 0.5
LEFT = 20

param_pairs = [(i, j) for i in range(5) for j in range(i, 5)]
sym_pairs = [(0, 0), (0, 1), (0, 2), (1, 1), (1, 2), (2, 2)]
spline_pairs = [(m, m + d) for d in range(4) for m in range(4 - d)]

VMEM_SPEC = pl.BlockSpec(memory_space=pltpu.VMEM)
SMEM_SPEC = pl.BlockSpec(memory_space=pltpu.SMEM)
NT = (((1,), (1,)), ((), ()))


def split_parts(values):
    high = values.astype(jnp.bfloat16)
    low = (values - high.astype(jnp.float32)).astype(jnp.bfloat16)
    return high, low


def spline_weights(local_time):
    floor_part = jnp.floor(local_time)
    frac = local_time - floor_part
    square = frac * frac
    cube = square * frac
    rest = 1.0 - frac
    sixth = 1.0 / 6.0
    splines = [
        rest * rest * rest * sixth,
        (3.0 * cube - 6.0 * square + 4.0) * sixth,
        (-3.0 * cube + 3.0 * square + 3.0 * frac + 1.0) * sixth,
        cube * sixth,
    ]
    return floor_part.astype(jnp.int32), splines


def source_sums_kernel(count_ref, res_ref, weight_ref, part_ref, src_ref, out_ref, live_ref, a_ref, l_ref, acc_ref):
    acc_ref[...] = jnp.zeros_like(acc_ref)
    lane = lax.broadcasted_iota(jnp.int32, (1, 128), 1)
    high_id = lax.broadcasted_iota(jnp.int32, (8, 128), 0)
    low_id = lax.broadcasted_iota(jnp.int32, (256, 128), 0)

    def group(g, carry):
        first = pl.multiple_of(g * 8, 8)
        res8 = res_ref[pl.ds(first, 8), :]
        weight8 = weight_ref[pl.ds(first, 8), :]
        src8 = src_ref[pl.ds(first, 8), :]
        live_rows = []
        for k in range(8):
            at = pl.multiple_of((g * 8 + k) * 128, 128)
            live = lane < count_ref[0, g * 8 + k]
            weight = jnp.where(live, weight8[k : k + 1], 0.0)
            live_rows.append(weight)
            part = part_ref[:, pl.ds(at, 128)]
            both = jnp.concatenate([part, res8[k : k + 1]], 0)
            weighted = weight * part
            src = src8[k : k + 1]
            high_mask = jnp.broadcast_to(src >> 8, (8, 128)) == high_id
            tiles = []
            products = [jnp.broadcast_to(weighted[i : i + 1], (6, 128)) * both for i in range(5)]
            for i, j in param_pairs:
                tiles.append(products[i][j : j + 1])
            for i in range(5):
                tiles.append(products[i][5:6])
            rows = [jnp.where(high_mask, jnp.broadcast_to(t, (8, 128)), 0.0) for t in tiles]
            high, low = split_parts(jnp.concatenate(rows, 0))
            a_ref[0:160, k * 128 : (k + 1) * 128] = high
            a_ref[160:320, k * 128 : (k + 1) * 128] = low
            hot = jnp.broadcast_to(src & 255, (256, 128)) == low_id
            l_ref[:, k * 128 : (k + 1) * 128] = jnp.where(hot, 1.0, 0.0).astype(jnp.bfloat16)
        live_ref[pl.ds(first, 8), :] = jnp.concatenate(live_rows, 0)
        acc_ref[...] += lax.dot_general(a_ref[...], l_ref[...], NT, preferred_element_type=jnp.float32)
        return carry

    lax.fori_loop(0, 16, group, 0)
    for f in range(20):
        for h in range(2):
            total = acc_ref[f * 8 : f * 8 + 8, h * 128 : (h + 1) * 128] + acc_ref[160 + f * 8 : 168 + f * 8, h * 128 : (h + 1) * 128]
            for q in range(4):
                out_ref[q, (h * 20 + f) * 8 : (h * 20 + f) * 8 + 8, :] = total


def cholesky_solve5(normal, rhs_terms):
    matrix = {}
    for number, (i, j) in enumerate(param_pairs):
        matrix[i, j] = normal[number]
        matrix[j, i] = normal[number]
    factor = {}
    inverse_diag = []
    for row_at in range(5):
        for col_at in range(row_at + 1):
            running = matrix[row_at, col_at]
            for inner_k in range(col_at):
                running = running - factor[row_at, inner_k] * factor[col_at, inner_k]
            if row_at == col_at:
                factor[row_at, row_at] = jnp.sqrt(running)
                inverse_diag.append(1.0 / factor[row_at, row_at])
            else:
                factor[row_at, col_at] = running * inverse_diag[col_at]
    forward = []
    for row_at in range(5):
        running = rhs_terms[row_at]
        for inner_k in range(row_at):
            running = running - factor[row_at, inner_k] * forward[inner_k]
        forward.append(running * inverse_diag[row_at])
    backward = [None] * 5
    for row_at in reversed(range(5)):
        running = forward[row_at]
        for inner_k in range(row_at + 1, 5):
            running = running - factor[inner_k, row_at] * backward[inner_k]
        backward[row_at] = running * inverse_diag[row_at]
    return backward


def source_solve_kernel(
    sums_ref, prior_ref, res_ref, live_ref, part_ref, src_ref, frac_ref, interval_ref, dir_ref,
    update_ref, pack_ref, base_ref, scale_ref, table_ref, root_ref, corr_ref,
):
    table_ref[...] = jnp.zeros_like(table_ref)
    for h in range(2):
        terms = []
        for f in range(20):
            at = (h * 20 + f) * 8
            terms.append(
                (sums_ref[0, at : at + 8, :] + sums_ref[1, at : at + 8, :])
                + (sums_ref[2, at : at + 8, :] + sums_ref[3, at : at + 8, :])
            )
        for number, (i, j) in enumerate(param_pairs):
            if i == j:
                prior = [prior_ref[i : i + 1, (2 * r + h) * 128 : (2 * r + h + 1) * 128] for r in range(8)]
                terms[number] = terms[number] + jnp.concatenate(prior, 0)
        solved = cholesky_solve5(terms[:15], terms[15:])
        for p in range(5):
            for r in range(8):
                table_ref[p : p + 1, (2 * r + h) * 128 : (2 * r + h + 1) * 128] = solved[p][r : r + 1]
    update_ref[...] = table_ref[0:5, :]
    root_ref[...] = jnp.sqrt(live_ref[...])

    def group(g, carry):
        first = pl.multiple_of(g * 8, 8)
        res8 = res_ref[pl.ds(first, 8), :]
        src8 = src_ref[pl.ds(first, 8), :]
        root8 = root_ref[pl.ds(first, 8), :]
        time8 = (interval_ref[pl.ds(first, 8), :] & 63).astype(jnp.float32) + frac_ref[pl.ds(first, 8), :]
        low8 = src8 & 127
        high8 = src8 >> 7
        pack = pack_ref.at[pl.ds(pl.multiple_of(g * 40, 8), 40), :]
        corr_rows = []
        for k in range(8):
            at = pl.multiple_of((g * 8 + k) * 128, 128)
            low = jnp.broadcast_to(low8[k : k + 1], (8, 128))
            high = jnp.broadcast_to(high8[k : k + 1], (8, 128))
            found = jnp.zeros((8, 128), jnp.float32)
            for c in range(16):
                taken = jnp.take_along_axis(table_ref[:, c * 128 : (c + 1) * 128], low, axis=1, mode="promise_in_bounds")
                found = jnp.where(high == c, taken, found)
            corr = jnp.sum(part_ref[:, pl.ds(at, 128)] * found[0:5], 0, keepdims=True)
            corr_rows.append(corr)
            root = root8[k : k + 1]
            first_pass = root * (res8[k : k + 1] - corr)
            pack[k * 5 : k * 5 + 5, :] = jnp.concatenate([time8[k : k + 1], root * dir_ref[:, pl.ds(at, 128)], first_pass], 0)
        corr_ref[pl.ds(first, 8), :] = jnp.concatenate(corr_rows, 0)
        return carry

    lax.fori_loop(0, 16, group, 0)
    live = root_ref[...] > 0.0
    base_ref[...] = res_ref[...] - jnp.where(live, corr_ref[...], 0.0)
    scale_ref[...] = jnp.where(live, 1.0 / jnp.where(live, root_ref[...], 1.0), 0.0)


def band_sums_kernel(slots_ref, prior_ref, frame_ref, feat_ref, a_ref, o_ref, acc_ref, prior_pad):
    acc_ref[...] = jnp.zeros_like(acc_ref)
    feat_ref[...] = jnp.zeros_like(feat_ref)
    knot_id = lax.broadcasted_iota(jnp.int32, (64, 128), 0)

    def group(g, carry):
        first = pl.multiple_of(g * 40, 8)
        slots = slots_ref.at[pl.ds(first, 40), :]
        time8, d0, d1, d2, fp = [slots[pl.ds(k, 8, stride=5), :] for k in range(5)]
        direction = [d0, d1, d2]
        floor8, splines = spline_weights(time8)
        for number, (m, n) in enumerate(spline_pairs):
            feat_ref[number * 8 : number * 8 + 8, :] = splines[m] * splines[n]
        for m in range(4):
            feat_ref[80 + m * 8 : 88 + m * 8, :] = splines[m]
        for number, (i, j) in enumerate(sym_pairs):
            feat_ref[112 + number * 8 : 120 + number * 8, :] = direction[i] * direction[j]
        for i in range(3):
            feat_ref[176 + i * 8 : 184 + i * 8, :] = direction[i] * fp
        for k in range(8):
            outer = feat_ref[pl.ds(112 + k, 8, stride=8), :]
            right = feat_ref[pl.ds(176 + k, 8, stride=8), :]
            rows = []
            for c in range(14):
                coeff = jnp.broadcast_to(feat_ref[c * 8 + k : c * 8 + k + 1, :], (8, 128))
                rows.append(coeff * (outer if c < 10 else right))
            high, low = split_parts(jnp.concatenate(rows, 0))
            a_ref[0:112, k * 128 : (k + 1) * 128] = high
            a_ref[112:224, k * 128 : (k + 1) * 128] = low
            hot = jnp.broadcast_to(floor8[k : k + 1], (64, 128)) == knot_id
            o_ref[:, k * 128 : (k + 1) * 128] = jnp.where(hot, 1.0, 0.0).astype(jnp.bfloat16)
        acc_ref[:, 0:64] += lax.dot_general(a_ref[...], o_ref[...], NT, preferred_element_type=jnp.float32)
        return carry

    lax.fori_loop(0, 16, group, 0)
    prior_pad[...] = jnp.zeros_like(prior_pad)
    prior_pad[3:6, 0:64] = prior_ref[...]

    def tile(c, shift):
        return pltpu.roll(acc_ref[c * 8 : c * 8 + 8, :] + acc_ref[112 + c * 8 : 120 + c * 8, :], shift, 1)

    for d in range(4):
        total = None
        for number, (m, n) in enumerate(spline_pairs):
            if n - m == d:
                term = tile(number, LEFT - 1 + m)
                total = term if total is None else total + term
        frame_ref[d * 8 : d * 8 + 8, :] = total
    total = pltpu.roll(prior_pad[...], LEFT, 1)
    for m in range(4):
        total = total + tile(10 + m, LEFT - 1 + m)
    frame_ref[32:40, :] = total


def sym_columns(e):
    pad = [jnp.zeros((5, 128), jnp.float32)]
    return [
        jnp.concatenate([e[0], e[1], e[2]] + pad, 0),
        jnp.concatenate([e[1], e[3], e[4]] + pad, 0),
        jnp.concatenate([e[2], e[4], e[5]] + pad, 0),
    ]


def columns_apply(columns, vector):
    total = None
    for j in range(3):
        term = columns[j] * jnp.broadcast_to(vector[j : j + 1], (8, 128))
        total = term if total is None else total + term
    return total


def attitude_kernel(place_ref, own_ref, even_ref, odd_ref, slots_ref, att_ref, corr_ref, *, knots_total):
    place = place_ref[0]
    lane = lax.broadcasted_iota(jnp.int32, (1, 128), 1)
    lane8 = lax.broadcasted_iota(jnp.int32, (8, 128), 1)
    is_even = place % 2 == 0
    knot = place * 64 + lane - LEFT
    valid = (knot >= 0) & (knot < knots_total)

    def frame(row):
        swap_first = even_ref[row : row + 8, :]
        swap_next = odd_ref[row : row + 8, :]
        left = jnp.where(is_even, swap_next, swap_first)
        right = jnp.where(is_even, swap_first, swap_next)
        return own_ref[row : row + 8, :] + pltpu.roll(jnp.where(lane8 < 64, right, left), 64, 1)

    uppers = [frame(8 * d) for d in range(4)]
    last = frame(32)
    e = [uppers[0][n : n + 1] for n in range(6)]
    e[0] = e[0] + last[3:4]
    e[3] = e[3] + last[4:5]
    e[5] = e[5] + last[5:6]
    c00 = e[3] * e[5] - e[4] * e[4]
    c01 = e[2] * e[4] - e[1] * e[5]
    c02 = e[1] * e[4] - e[2] * e[3]
    c11 = e[0] * e[5] - e[2] * e[2]
    c12 = e[1] * e[2] - e[0] * e[4]
    c22 = e[0] * e[3] - e[1] * e[1]
    determinant = e[0] * c00 + e[1] * c01 + e[2] * c02
    scale = jnp.where(valid, DAMPING / jnp.where(valid, determinant, 1.0), 0.0)
    inverse = sym_columns([c * scale for c in (c00, c01, c02, c11, c12, c22)])
    diag = sym_columns(e)
    upper_cols = [sym_columns([u[n : n + 1] for n in range(6)]) for u in uppers[1:]]
    rhs = last
    att = columns_apply(inverse, rhs)
    for _ in range(1, ITERS_ATT):
        applied = columns_apply(diag, att)
        for d in range(1, 4):
            applied = applied + columns_apply(upper_cols[d - 1], pltpu.roll(att, 128 - d, 1))
            applied = applied + pltpu.roll(columns_apply(upper_cols[d - 1], att), d, 1)
        att = att + columns_apply(inverse, rhs - applied)
    att_ref[...] = pltpu.roll(att, 128 - LEFT, 1)[0:3, 0:64]
    tables = [jnp.broadcast_to(att[j : j + 1], (8, 128)) for j in range(3)]

    def group(g, carry):
        slots = slots_ref.at[pl.ds(pl.multiple_of(g * 40, 8), 40), :]
        time8, d0, d1, d2 = [slots[pl.ds(k, 8, stride=5), :] for k in range(4)]
        direction = [d0, d1, d2]
        floor8, splines = spline_weights(time8)
        total = jnp.zeros((8, 128), jnp.float32)
        for m in range(4):
            at = floor8 + (LEFT - 1 + m)
            part = None
            for j in range(3):
                term = direction[j] * jnp.take_along_axis(tables[j], at, axis=1, mode="promise_in_bounds")
                part = term if part is None else part + term
            total = total + splines[m] * part
        corr_ref[pl.ds(pl.multiple_of(g * 8, 8), 8), :] = total
        return carry

    lax.fori_loop(0, 16, group, 0, unroll=4)


def call(kernel, outs, n_in, smem_at=(), scratch=(), name=None):
    shapes = [jax.ShapeDtypeStruct(s, jnp.float32) for s in outs]
    return pl.pallas_call(
        kernel,
        out_shape=shapes,
        in_specs=[SMEM_SPEC if i in smem_at else VMEM_SPEC for i in range(n_in)],
        out_specs=[VMEM_SPEC] * len(shapes),
        scratch_shapes=list(scratch),
        name=name,
    )


def body(residual, obs_weight, time_frac, src_partials, att_dir, src_prior, att_prior, obs_source, obs_interval, obs_count):
    devices = lax.axis_size("src") * lax.axis_size("seg")
    square = lambda a: a.reshape(128, 128)
    res, weight, frac, src, interval = map(square, (residual, obs_weight, time_frac, obs_source, obs_interval))
    sums, live = call(
        source_sums_kernel,
        [(4, 320, 128), (128, 128)],
        5,
        (0,),
        [pltpu.VMEM((320, 1024), jnp.bfloat16), pltpu.VMEM((256, 1024), jnp.bfloat16), pltpu.VMEM((320, 256), jnp.float32)],
        "source_sums",
    )(obs_count, res, weight, src_partials, src)
    gathered = lax.all_to_all(sums, "seg", split_axis=0, concat_axis=0, tiled=True)
    src_update, packed, base, scale = call(
        source_solve_kernel,
        [(5, 2048), (640, 128), (128, 128), (128, 128)],
        9,
        (),
        [pltpu.VMEM((8, 2048), jnp.float32), pltpu.VMEM((128, 128), jnp.float32), pltpu.VMEM((128, 128), jnp.float32)],
        "source_solve",
    )(gathered, src_prior, res, live, src_partials, src, frac, interval, att_dir)
    arrived = lax.all_to_all(packed.reshape(128, 1, 640), "src", split_axis=0, concat_axis=0, tiled=True).reshape(640, 128)
    (frame,) = call(
        band_sums_kernel,
        [(40, 128)],
        2,
        (),
        [
            pltpu.VMEM((240, 128), jnp.float32),
            pltpu.VMEM((224, 1024), jnp.bfloat16),
            pltpu.VMEM((64, 1024), jnp.bfloat16),
            pltpu.VMEM((224, 128), jnp.float32),
            pltpu.VMEM((8, 128), jnp.float32),
        ],
        "band_sums",
    )(arrived, att_prior)
    both = ("src", "seg")
    swaps = []
    for start in (0, 1):
        pairs = [(i, i + 1) for i in range(start, devices - 1, 2)]
        swaps.append(lax.ppermute(frame, both, pairs + [(b, a) for a, b in pairs]))
    place = lax.axis_index(both).astype(jnp.int32).reshape(1)
    att_update, correction = call(
        functools.partial(attitude_kernel, knots_total=devices * 64),
        [(3, 64), (128, 128)],
        5,
        (0,),
        (),
        "attitude",
    )(place, frame, swaps[0], swaps[1], arrived)
    returned = lax.all_to_all(correction.reshape(128, 1, 128), "src", split_axis=0, concat_axis=0, tiled=True)
    residual_out = base - scale * returned.reshape(128, 128)
    return src_update, att_update, residual_out.reshape(-1)


def solution(mesh):
    pair = ("src", "seg")
    in_specs = (
        P(pair), P(pair), P(pair), P(None, pair), P(None, pair), P(None, "src"), P(None, pair), P(pair), P(pair), P(pair, None),
    )
    out_specs = (P(None, "src"), P(None, pair), P(pair))
    return jax.shard_map(body, mesh=mesh, in_specs=in_specs, out_specs=out_specs, check_vma=False)
```

time: 676 us -> 125 us (0.18)
  local copies, waits for them, and re-layouts: 295 us -> 0.61 us
  other arithmetic: 141 us -> 0.64 us
  waiting for transfers between devices: 102 us -> 2.05 us
  starting transfers between devices: 69.8 us -> 6.62 us
  blocking collectives: 39.1 us -> 86.1 us
  Pallas kernels: 0 us -> 27.8 us
  between operations: 14.9 us -> 0.68 us
  matrix products: 11.2 us -> 0 us
    gather x5 -> x0, local copies, waits for them, and re-layouts: 272 us -> none  [the longest x4 218 us: body(): looked = jnp.take(final_padded, arrived_floor[0] + spline_at + 2, axis=1)]
    scatter-add x1 -> x0, other arithmetic: 87.9 us -> none  [body(): jax.ops.segment_sum(jnp.stack(features, 1), obs_source, num_segments=sour...]
    psum x1 -> x0, waiting for transfers between devices: 54.9 us -> none  [body(): full_sums = lax.psum(src_sums, 'seg')]
    all_to_all x1 -> x3, blocking collectives: 39.1 us -> 86.1 us  [the longest x1 48.8 us: body(): lax.all_to_all(packed.reshape(128, 1, 640), 'src', split_axis=0, concat_a...]
    ppermute x15 -> x2, starting transfers between devices: 51 us -> 6.62 us  [body(): swaps.append(lax.ppermute(frame, both, pairs + [(b, a) for a, b in pairs]))]
    reduce_sum x2 -> x0, other arithmetic: 33.6 us -> none  [the longest x1 26.1 us: body(): jnp.sum(arrived_dir * looked, 0)]
    all_to_all x1 -> x0, waiting for transfers between devices: 32.2 us -> none  [body(): lax.all_to_all(packed, 'src', split_axis=1, concat_axis=1, tiled=True)]
    pallas_call x0 -> x4, Pallas kernels: none -> 27.8 us  [the longest x1 11.4 us: body(): call(source_sums_kernel, [(4, 320, 128), (128, 128)], 5, (0,), [pltpu.VME...]
  transfers between devices with their start and end apart: 17 -> 2, of which waited for: 8 -> 1; matrix products, arithmetic and copies ran while one was open for 2% -> 0% of each run, Pallas kernels for 0% -> 0%
where the time goes in v1:
time: 125 us; the launch traced here: 124 us
  blocking collectives  86.1 us (69%)
  Pallas kernels  27.8 us (22%)
  starting transfers between devices  6.62 us (5%)
  waiting for transfers between devices  2.05 us (2%)
    all_to_all x1, blocking collectives, body(): lax.all_to_all(packed.reshape(128, 1, 640), 'src', split_axis=0, concat_a...  48.8 us
    all_to_all x1, blocking collectives, body(): lax.all_to_all(correction.reshape(128, 1, 128), 'src', split_axis=0, conc...  24.7 us
    all_to_all x1, blocking collectives, body(): lax.all_to_all(sums, 'seg', split_axis=0, concat_axis=0, tiled=True)  12.6 us
    pallas_call x1, Pallas kernels, body(): call(source_sums_kernel, [(4, 320, 128), (128, 128)], 5, (0,), [pltpu.VME...  11.4 us
    pallas_call x1, Pallas kernels, body(): call(band_sums_kernel, [(40, 128)], 2, (), [pltpu.VMEM((240, 128), jnp.fl...  7.11 us
    ppermute x2, starting transfers between devices, body(): swaps.append(lax.ppermute(frame, both, pairs + [(b, a) for a, b in pairs]))  6.62 us
    pallas_call x1, Pallas kernels, body(): call(source_solve_kernel, [(5, 2048), (640, 128), (128, 128), (128, 128)]...  6.31 us
    pallas_call x1, Pallas kernels, body(): call(functools.partial(attitude_kernel, knots_total=devices * 64), [(3, 6...  2.97 us
  transfers between devices with their start and end apart: 2, of which 1 were waited for; matrix products, arithmetic and copies ran while one was open for 0% of the time, Pallas kernels for 0%

profile of v1, /device:TPU:1, one launch (start us, length us, event | category | flops | bytes accessed | tf_op | source)
XLA Modules:
  0.0 124.5 jit_solution(12251314339808666337)
XLA Ops:
  0.6 11.4 %source_sums.1 = (f32[4,320,128]{2,1,0:T(8,128)}, f32[128,128]{1,0:T(8,128)}) custom-call(s32[1,128]{1,0:T(1,128)} %count_ref.1, f32[128,128]{1,0:T(8,128)} %bitcast.17, f32[128,128]{1,0:T(8,128)} %bitcast.22, f32[5,16384]{1,0:T(8,128)} %part_ref.3, s32[128,128]{1,0:T(8,128)} %bitcast.19), custom_call_target="tpu_custom_call" | custom-call | tf_op jit(solution)/shard_map/source_sums/pallas_call | solution.py:328
  12.0 12.6 %all_to_all.15.sums_ref = f32[4,320,128]{2,1,0:T(8,128)} all-to-all(f32[4,320,128]{2,1,0:T(8,128)} %get-tuple-element.11), channel_id=1, replica_groups=mesh['src'=128,'seg'=4] {'seg'}, dimensions={0} | all-to-all | bytes 1310720 | tf_op jit(solution)/shard_map/all_to_all | solution.py:336
  24.6 6.3 %source_solve.1 = (f32[5,2048]{1,0:T(8,128)}, f32[640,128]{1,0:T(8,128)}, f32[128,128]{1,0:T(8,128)}, f32[128,128]{1,0:T(8,128)}) custom-call(f32[4,320,128]{2,1,0:T(8,128)} %all_to_all.15.sums_ref, f32[5,2048]{1,0:T(8,128)} %prior_ref.2, f32[128,128]{1,0:T(8,128)} %bitcast.18, f32[128,128]{1,0:T(8,128)} %get-tuple-element.12.live_ref, f32[5,16384]{1,0:T(8,128)} %part_ref.3, ...), custom_call_target="tpu_custom_call" | custom-call | tf_op jit(solution)/shard_map/source_solve/pallas_call | solution.py:337
  30.9 48.8 %all_to_all.16 = f32[128,1,640]{2,1,0:T(1,128)} all-to-all(f32[128,1,640]{2,1,0:T(1,128)} %bitcast.16), channel_id=1, replica_groups=mesh['src'=128,'seg'=4] {'src'}, dimensions={0} | all-to-all | bytes 655360 | tf_op jit(solution)/shard_map/all_to_all | solution.py:345
  79.7 7.1 %band_sums.1.own_ref = f32[40,128]{1,0:T(8,128)} custom-call(f32[640,128]{1,0:T(8,128)} %bitcast.14, f32[3,64]{1,0:T(4,128)} %prior_ref.3), custom_call_target="tpu_custom_call" | custom-call | tf_op jit(solution)/shard_map/band_sums/pallas_call | solution.py:346
  86.8 2.2 %collective-permute-start = (f32[40,128]{1,0:T(8,128)}, f32[40,128]{1,0:T(8,128)S(1)}, u32[]{:S(2)}, u32[]{:S(2)}) collective-permute-start(f32[40,128]{1,0:T(8,128)} %band_sums.1.own_ref), channel_id=1, source_target_pairs={{0,1},{2,3},{4,5},{6,7},{8,9},{10,11},{12,13},{14,15},{16,17},{18,... | collective-permute-start | bytes 61448 | tf_op jit(solution)/shard_map/ppermute | solution.py:364
  89.0 4.4 %collective-permute-start.1 = (f32[40,128]{1,0:T(8,128)}, f32[40,128]{1,0:T(8,128)S(1)}, u32[]{:S(2)}, u32[]{:S(2)}) collective-permute-start(f32[40,128]{1,0:T(8,128)} %band_sums.1.own_ref), channel_id=1, source_target_pairs={{1,2},{3,4},{5,6},{7,8},{9,10},{11,12},{13,14},{15,16},{17,18},{19... | collective-permute-start | bytes 61448 | tf_op jit(solution)/shard_map/ppermute | solution.py:364
  93.5 0.0 collective-permute-done.even_ref
  93.5 0.0 copy-start.2
  93.5 2.0 %collective-permute-done.1.odd_ref = f32[40,128]{1,0:T(8,128)S(1)} collective-permute-done((f32[40,128]{1,0:T(8,128)}, f32[40,128]{1,0:T(8,128)S(1)}, u32[]{:S(2)}, u32[]{:S(2)}) %collective-permute-start.1) | collective-permute-done | bytes 20512 | tf_op jit(solution)/shard_map/ppermute | solution.py:364
  95.5 0.0 copy-start.3
  95.5 0.0 copy-done.2
  95.5 0.6 copy-done.3
  96.1 3.0 %attitude.1 = (f32[3,64]{1,0:T(4,128)}, f32[128,128]{1,0:T(8,128)}) custom-call(s32[1]{0:T(128)} %bitcast.5.place_ref, f32[40,128]{1,0:T(8,128)} %band_sums.1.own_ref, f32[40,128]{1,0:T(8,128)} %copy-done.2, f32[40,128]{1,0:T(8,128)} %copy-done.3, f32[640,128]{1,0:T(8,128)} %bitcast.15), custom_call_target="tpu_custom_call" | custom-call | tf_op jit(solution)/shard_map/attitude/pallas_call | solution.py:366
  99.1 0.0 copy-start
  99.1 0.0 copy-start.1
  99.1 24.7 %all_to_all.17 = f32[128,1,128]{2,1,0:T(1,128)S(1)} all-to-all(f32[128,1,128]{2,1,0:T(1,128)} %bitcast.25), channel_id=1, replica_groups=mesh['src'=128,'seg'=4] {'src'}, dimensions={0} | all-to-all | bytes 131072 | tf_op jit(solution)/shard_map/all_to_all | solution.py:374
  123.8 0.0 copy-done
  123.8 0.0 copy-done.1
  123.9 0.6 subtract_bitcast_fusion
Async XLA Ops:
  86.8 6.6 %collective-permute-start = (f32[40,128]{1,0:T(8,128)}, f32[40,128]{1,0:T(8,128)S(1)}, u32[]{:S(2)}, u32[]{:S(2)}) collective-permute-start(f32[40,128]{1,0:T(8,128)} %band_sums.1.own_ref), channel_id=1, source_target_pairs={{0,1},{2,3},{4,5},{6,7},{8,9},{10,11},{12,13},{14,15},{16,17},{18,... | collective-permute-start | bytes 61448 | tf_op jit(solution)/shard_map/ppermute | solution.py:364
  89.0 6.5 %collective-permute-start.1 = (f32[40,128]{1,0:T(8,128)}, f32[40,128]{1,0:T(8,128)S(1)}, u32[]{:S(2)}, u32[]{:S(2)}) collective-permute-start(f32[40,128]{1,0:T(8,128)} %band_sums.1.own_ref), channel_id=1, source_target_pairs={{1,2},{3,4},{5,6},{7,8},{9,10},{11,12},{13,14},{15,16},{17,18},{19... | collective-permute-start | bytes 61448 | tf_op jit(solution)/shard_map/ppermute | solution.py:364
  93.5 2.1 %copy-start.2 = (f32[40,128]{1,0:T(8,128)}, f32[40,128]{1,0:T(8,128)S(1)}, u32[]{:S(2)}) copy-start(f32[40,128]{1,0:T(8,128)S(1)} %collective-permute-done.even_ref) | copy-start | bytes 61444
  95.5 0.6 copy-start.3
  99.1 24.7 %copy-start = (f32[128,128]{1,0:T(8,128)S(1)}, f32[128,128]{1,0:T(8,128)}, u32[]{:S(2)}) copy-start(f32[128,128]{1,0:T(8,128)} %get-tuple-element.16) | copy-start | bytes 196612
  99.1 24.7 %copy-start.1 = (f32[128,128]{1,0:T(8,128)S(1)}, f32[128,128]{1,0:T(8,128)}, u32[]{:S(2)}) copy-start(f32[128,128]{1,0:T(8,128)} %get-tuple-element.17) | copy-start | bytes 196612

commit v2 on v1

--- a/solution.py
+++ b/solution.py
@@ -18,6 +18,8 @@
 VMEM_SPEC = pl.BlockSpec(memory_space=pltpu.VMEM)
 SMEM_SPEC = pl.BlockSpec(memory_space=pltpu.SMEM)
 NT = (((1,), (1,)), ((), ()))
+SUMS_UNROLL = 4
+BAND_UNROLL = 4
 
 
 def split_parts(values):
@@ -42,50 +44,86 @@
     return floor_part.astype(jnp.int32), splines
 
 
-def source_sums_kernel(count_ref, res_ref, weight_ref, part_ref, src_ref, out_ref, live_ref, a_ref, l_ref, acc_ref):
+def side_by_side(ref):
+    return jnp.concatenate([ref[k] for k in range(8)], 1)
+
+
+def hot_rows(ids, row):
+    wide = jnp.broadcast_to(row, (16, 128)).astype(jnp.bfloat16)
+    one, zero = jnp.ones((16, 128), jnp.bfloat16), jnp.zeros((16, 128), jnp.bfloat16)
+    count = ids.shape[0] // 16
+    return jnp.concatenate([jnp.where(ids[16 * n : 16 * n + 16] == wide, one, zero) for n in range(count)], 0)
+
+
+def source_sums_kernel(
+    count_ref, res_ref, weight_ref, part_ref, src_ref, out_ref, live_ref, acc_ref, rows_refs, feat_refs
+):
     acc_ref[...] = jnp.zeros_like(acc_ref)
-    lane = lax.broadcasted_iota(jnp.int32, (1, 128), 1)
-    high_id = lax.broadcasted_iota(jnp.int32, (8, 128), 0)
-    low_id = lax.broadcasted_iota(jnp.int32, (256, 128), 0)
-
-    def group(g, carry):
+    ids = lax.broadcasted_iota(jnp.int32, (256, 128), 0).astype(jnp.float32).astype(jnp.bfloat16)
+    lane8 = lax.broadcasted_iota(jnp.int32, (8, 128), 1)
+    sub8 = lax.broadcasted_iota(jnp.int32, (8, 128), 0)
+    sub16 = lax.broadcasted_iota(jnp.int32, (16, 128), 0)
+    zero = jnp.zeros((16, 128), jnp.bfloat16)
+
+    def group(g, feat_ref, rows_ref):
         first = pl.multiple_of(g * 8, 8)
         res8 = res_ref[pl.ds(first, 8), :]
-        weight8 = weight_ref[pl.ds(first, 8), :]
         src8 = src_ref[pl.ds(first, 8), :]
-        live_rows = []
+        low8 = (src8 & 255).astype(jnp.float32)
+        high8 = (src8 >> 8).astype(jnp.float32)
+        count8 = jnp.zeros((8, 128), jnp.int32)
         for k in range(8):
-            at = pl.multiple_of((g * 8 + k) * 128, 128)
-            live = lane < count_ref[0, g * 8 + k]
-            weight = jnp.where(live, weight8[k : k + 1], 0.0)
-            live_rows.append(weight)
-            part = part_ref[:, pl.ds(at, 128)]
-            both = jnp.concatenate([part, res8[k : k + 1]], 0)
-            weighted = weight * part
-            src = src8[k : k + 1]
-            high_mask = jnp.broadcast_to(src >> 8, (8, 128)) == high_id
+            count8 = jnp.where(sub8 == k, count_ref[0, g * 8 + k], count8)
+            rows_ref[pl.ds(k, 5, stride=8), :] = part_ref[:, pl.ds(pl.multiple_of((g * 8 + k) * 128, 128), 128)]
+        weight8 = jnp.where(lane8 < count8, weight_ref[pl.ds(first, 8), :], 0.0)
+        live_ref[pl.ds(first, 8), :] = weight8
+        part8 = [rows_ref[p * 8 : p * 8 + 8, :] for p in range(5)]
+        weighted = [weight8 * p for p in part8]
+        features = [weighted[i] * part8[j] for i, j in param_pairs] + [weighted[i] * res8 for i in range(5)]
+        for f, feature in enumerate(features):
+            high = feature.astype(jnp.bfloat16).astype(jnp.float32)
+            feat_ref[f * 8 : f * 8 + 8, :] = high
+            feat_ref[160 + f * 8 : 168 + f * 8, :] = feature - high
+        hots = []
+        blocks = []
+        for k in range(8):
+            body = [feat_ref[pl.ds(128 * n + k, 16, stride=8), :].astype(jnp.bfloat16) for n in range(2)]
+            tail = feat_ref[pl.ds(256 + k, 8, stride=8), :]
+            tail = jnp.concatenate([tail, tail], 0).astype(jnp.bfloat16)
+            high = jnp.broadcast_to(high8[k : k + 1], (16, 128)).astype(jnp.bfloat16)
             tiles = []
-            products = [jnp.broadcast_to(weighted[i : i + 1], (6, 128)) * both for i in range(5)]
-            for i, j in param_pairs:
-                tiles.append(products[i][j : j + 1])
-            for i in range(5):
-                tiles.append(products[i][5:6])
-            rows = [jnp.where(high_mask, jnp.broadcast_to(t, (8, 128)), 0.0) for t in tiles]
-            high, low = split_parts(jnp.concatenate(rows, 0))
-            a_ref[0:160, k * 128 : (k + 1) * 128] = high
-            a_ref[160:320, k * 128 : (k + 1) * 128] = low
-            hot = jnp.broadcast_to(src & 255, (256, 128)) == low_id
-            l_ref[:, k * 128 : (k + 1) * 128] = jnp.where(hot, 1.0, 0.0).astype(jnp.bfloat16)
-        live_ref[pl.ds(first, 8), :] = jnp.concatenate(live_rows, 0)
-        acc_ref[...] += lax.dot_general(a_ref[...], l_ref[...], NT, preferred_element_type=jnp.float32)
+            for pair in range(4):
+                for e in range(2):
+                    mask = high == jnp.bfloat16(2 * pair + e)
+                    tiles.append(jnp.where(mask, body[0], zero))
+                    tiles.append(jnp.where(mask, body[1], zero))
+                mixed = jnp.where(sub16 < 8, 2.0 * pair, 2.0 * pair + 1.0).astype(jnp.bfloat16)
+                tiles.append(jnp.where(high == mixed, tail, zero))
+            blocks.append(jnp.concatenate(tiles, 0))
+            hots.append(hot_rows(ids, low8[k : k + 1]))
+        sums = lax.dot_general(jnp.concatenate(blocks, 1), jnp.concatenate(hots, 1), NT, preferred_element_type=jnp.float32)
+        for h in range(2):
+            acc_ref[h] += sums[:, h * 128 : (h + 1) * 128]
+
+    def groups(step, carry):
+        for n in range(SUMS_UNROLL):
+            group(step * SUMS_UNROLL + n, feat_refs.at[n], rows_refs.at[n])
         return carry
 
-    lax.fori_loop(0, 16, group, 0)
+    lax.fori_loop(0, 16 // SUMS_UNROLL, groups, 0)
+
+    def rows_of(q, e, h):
+        at = 32 * e + q if q < 32 else 64 + 8 * e + q - 32
+        return acc_ref[h, pl.ds(at, 4, stride=80), :]
+
     for f in range(20):
         for h in range(2):
-            total = acc_ref[f * 8 : f * 8 + 8, h * 128 : (h + 1) * 128] + acc_ref[160 + f * 8 : 168 + f * 8, h * 128 : (h + 1) * 128]
+            total = jnp.concatenate([rows_of(f, e, h) + rows_of(20 + f, e, h) for e in range(2)], 0)
             for q in range(4):
                 out_ref[q, (h * 20 + f) * 8 : (h * 20 + f) * 8 + 8, :] = total
+
+
+HIGH_ORDER = (0, 2, 4, 6, 1, 3, 5, 7)
 
 
 def cholesky_solve5(normal, rhs_terms):
@@ -135,12 +173,12 @@
             )
         for number, (i, j) in enumerate(param_pairs):
             if i == j:
-                prior = [prior_ref[i : i + 1, (2 * r + h) * 128 : (2 * r + h + 1) * 128] for r in range(8)]
+                prior = [prior_ref[i : i + 1, (2 * r + h) * 128 : (2 * r + h + 1) * 128] for r in HIGH_ORDER]
                 terms[number] = terms[number] + jnp.concatenate(prior, 0)
         solved = cholesky_solve5(terms[:15], terms[15:])
         for p in range(5):
-            for r in range(8):
-                table_ref[p : p + 1, (2 * r + h) * 128 : (2 * r + h + 1) * 128] = solved[p][r : r + 1]
+            for n, r in enumerate(HIGH_ORDER):
+                table_ref[p : p + 1, (2 * r + h) * 128 : (2 * r + h + 1) * 128] = solved[p][n : n + 1]
     update_ref[...] = table_ref[0:5, :]
     root_ref[...] = jnp.sqrt(live_ref[...])
 
@@ -176,57 +214,67 @@
     scale_ref[...] = jnp.where(live, 1.0 / jnp.where(live, root_ref[...], 1.0), 0.0)
 
 
-def band_sums_kernel(slots_ref, prior_ref, frame_ref, feat_ref, a_ref, o_ref, acc_ref, prior_pad):
+def band_sums_kernel(slots_ref, prior_ref, frame_ref, feat_refs, a_refs, acc_ref, prior_pad):
     acc_ref[...] = jnp.zeros_like(acc_ref)
-    feat_ref[...] = jnp.zeros_like(feat_ref)
-    knot_id = lax.broadcasted_iota(jnp.int32, (64, 128), 0)
-
-    def group(g, carry):
-        first = pl.multiple_of(g * 40, 8)
-        slots = slots_ref.at[pl.ds(first, 40), :]
+    ids = lax.broadcasted_iota(jnp.int32, (64, 128), 0).astype(jnp.float32).astype(jnp.bfloat16)
+
+    def group(g, a_ref, feat_ref):
+        slots = slots_ref.at[pl.ds(pl.multiple_of(g * 40, 8), 40), :]
         time8, d0, d1, d2, fp = [slots[pl.ds(k, 8, stride=5), :] for k in range(5)]
         direction = [d0, d1, d2]
-        floor8, splines = spline_weights(time8)
-        for number, (m, n) in enumerate(spline_pairs):
-            feat_ref[number * 8 : number * 8 + 8, :] = splines[m] * splines[n]
+        floor8 = jnp.floor(time8)
+        _, splines = spline_weights(time8)
+        outer = [direction[i] * direction[j] for i, j in sym_pairs]
+        right = [direction[i] * fp for i in range(3)]
+        at = 0
+        for m, n in spline_pairs:
+            coeff = splines[m] * splines[n]
+            for entry in outer:
+                feat_ref[at : at + 8, :] = coeff * entry
+                at += 8
         for m in range(4):
-            feat_ref[80 + m * 8 : 88 + m * 8, :] = splines[m]
-        for number, (i, j) in enumerate(sym_pairs):
-            feat_ref[112 + number * 8 : 120 + number * 8, :] = direction[i] * direction[j]
-        for i in range(3):
-            feat_ref[176 + i * 8 : 184 + i * 8, :] = direction[i] * fp
+            for entry in right:
+                feat_ref[at : at + 8, :] = splines[m] * entry
+                at += 8
+        hots = []
         for k in range(8):
-            outer = feat_ref[pl.ds(112 + k, 8, stride=8), :]
-            right = feat_ref[pl.ds(176 + k, 8, stride=8), :]
-            rows = []
-            for c in range(14):
-                coeff = jnp.broadcast_to(feat_ref[c * 8 + k : c * 8 + k + 1, :], (8, 128))
-                rows.append(coeff * (outer if c < 10 else right))
-            high, low = split_parts(jnp.concatenate(rows, 0))
-            a_ref[0:112, k * 128 : (k + 1) * 128] = high
-            a_ref[112:224, k * 128 : (k + 1) * 128] = low
-            hot = jnp.broadcast_to(floor8[k : k + 1], (64, 128)) == knot_id
-            o_ref[:, k * 128 : (k + 1) * 128] = jnp.where(hot, 1.0, 0.0).astype(jnp.bfloat16)
-        acc_ref[:, 0:64] += lax.dot_general(a_ref[...], o_ref[...], NT, preferred_element_type=jnp.float32)
+            for n in range(5):
+                size = 16 if n < 4 else 8
+                rows = feat_ref[pl.ds(128 * n + k, size, stride=8), :]
+                high = rows.astype(jnp.bfloat16)
+                rest = rows - high.astype(jnp.float32)
+                if n < 4:
+                    a_ref[k, 16 * n : 16 * n + 16, :] = high
+                    a_ref[k, 64 + 16 * n : 80 + 16 * n, :] = rest.astype(jnp.bfloat16)
+                else:
+                    a_ref[k, 128:144, :] = jnp.concatenate([high.astype(jnp.float32), rest], 0).astype(jnp.bfloat16)
+            hots.append(hot_rows(ids, floor8[k : k + 1]))
+        acc_ref[:, 0:64] += lax.dot_general(side_by_side(a_ref), jnp.concatenate(hots, 1), NT, preferred_element_type=jnp.float32)
+
+    def groups(step, carry):
+        for n in range(BAND_UNROLL):
+            group(step * BAND_UNROLL + n, a_refs.at[n], feat_refs.at[n])
         return carry
 
-    lax.fori_loop(0, 16, group, 0)
+    lax.fori_loop(0, 16 // BAND_UNROLL, groups, 0)
     prior_pad[...] = jnp.zeros_like(prior_pad)
     prior_pad[3:6, 0:64] = prior_ref[...]
-
-    def tile(c, shift):
-        return pltpu.roll(acc_ref[c * 8 : c * 8 + 8, :] + acc_ref[112 + c * 8 : 120 + c * 8, :], shift, 1)
+    sums = jnp.concatenate([acc_ref[0:64, :] + acc_ref[64:128, :], acc_ref[128:136, :] + acc_ref[136:144, :]], 0)
+
+    def tile(first, count, shift):
+        rows = sums[first : first + count]
+        return pltpu.roll(jnp.concatenate([rows, jnp.zeros((8 - count, 128), jnp.float32)], 0), shift, 1)
 
     for d in range(4):
         total = None
         for number, (m, n) in enumerate(spline_pairs):
             if n - m == d:
-                term = tile(number, LEFT - 1 + m)
+                term = tile(6 * number, 6, LEFT - 1 + m)
                 total = term if total is None else total + term
         frame_ref[d * 8 : d * 8 + 8, :] = total
     total = pltpu.roll(prior_pad[...], LEFT, 1)
     for m in range(4):
-        total = total + tile(10 + m, LEFT - 1 + m)
+        total = total + tile(60 + 3 * m, 3, LEFT - 1 + m)
     frame_ref[32:40, :] = total
 
 
@@ -309,9 +357,9 @@
     lax.fori_loop(0, 16, group, 0, unroll=4)
 
 
-def call(kernel, outs, n_in, smem_at=(), scratch=(), name=None):
-    shapes = [jax.ShapeDtypeStruct(s, jnp.float32) for s in outs]
-    return pl.pallas_call(
+def call(kernel, outs, n_in, smem_at=(), scratch=(), name=None, far_out=(), far_in=()):
+    shapes = [jax.ShapeDtypeStruct(s, jnp.float32) if i in far_out else pltpu.VMEM(s, jnp.float32) for i, s in enumerate(outs)]
+    run = pl.pallas_call(
         kernel,
         out_shape=shapes,
         in_specs=[SMEM_SPEC if i in smem_at else VMEM_SPEC for i in range(n_in)],
@@ -319,6 +367,12 @@
         scratch_shapes=list(scratch),
         name=name,
     )
+
+    def on_chip(*args):
+        near = [a if i in smem_at or i in far_in else pltpu.with_memory_space_constraint(a, pltpu.VMEM) for i, a in enumerate(args)]
+        return run(*near)
+
+    return on_chip
 
 
 def body(residual, obs_weight, time_frac, src_partials, att_dir, src_prior, att_prior, obs_source, obs_interval, obs_count):
@@ -330,8 +384,14 @@
         [(4, 320, 128), (128, 128)],
         5,
         (0,),
-        [pltpu.VMEM((320, 1024), jnp.bfloat16), pltpu.VMEM((256, 1024), jnp.bfloat16), pltpu.VMEM((320, 256), jnp.float32)],
+        [
+            pltpu.VMEM((2, 320, 128), jnp.float32),
+            pltpu.VMEM((SUMS_UNROLL, 40, 128), jnp.float32),
+            pltpu.VMEM((SUMS_UNROLL, 320, 128), jnp.float32),
+        ],
         "source_sums",
+        (),
+        range(5),
     )(obs_count, res, weight, src_partials, src)
     gathered = lax.all_to_all(sums, "seg", split_axis=0, concat_axis=0, tiled=True)
     src_update, packed, base, scale = call(
@@ -341,6 +401,7 @@
         (),
         [pltpu.VMEM((8, 2048), jnp.float32), pltpu.VMEM((128, 128), jnp.float32), pltpu.VMEM((128, 128), jnp.float32)],
         "source_solve",
+        (0,),
     )(gathered, src_prior, res, live, src_partials, src, frac, interval, att_dir)
     arrived = lax.all_to_all(packed.reshape(128, 1, 640), "src", split_axis=0, concat_axis=0, tiled=True).reshape(640, 128)
     (frame,) = call(
@@ -349,10 +410,9 @@
         2,
         (),
         [
-            pltpu.VMEM((240, 128), jnp.float32),
-            pltpu.VMEM((224, 1024), jnp.bfloat16),
-            pltpu.VMEM((64, 1024), jnp.bfloat16),
-            pltpu.VMEM((224, 128), jnp.float32),
+            pltpu.VMEM((BAND_UNROLL, 576, 128), jnp.float32),
+            pltpu.VMEM((BAND_UNROLL, 8, 144, 128), jnp.bfloat16),
+            pltpu.VMEM((144, 128), jnp.float32),
             pltpu.VMEM((8, 128), jnp.float32),
         ],
         "band_sums",
@@ -370,6 +430,7 @@
         (0,),
         (),
         "attitude",
+        (0,),
     )(place, frame, swaps[0], swaps[1], arrived)
     returned = lax.all_to_all(correction.reshape(128, 1, 128), "src", split_axis=0, concat_axis=0, tiled=True)
     residual_out = base - scale * returned.reshape(128, 128)

time: 125 us -> 110 us (0.88)
  Pallas kernels: 27.8 us -> 13.9 us
    pallas_call x4, Pallas kernels: 27.8 us -> 13.9 us  [on_chip(): return run(*near)]
where the time goes in v2:
time: 110 us; the launch traced here: 109 us
  blocking collectives  85.4 us (78%)
  Pallas kernels  13.9 us (13%)
  starting transfers between devices  6.63 us (6%)
  waiting for transfers between devices  1.85 us (2%)
    all_to_all x1, blocking collectives, body(): lax.all_to_all(packed.reshape(128, 1, 640), 'src', split_axis=0, concat_a...  48.5 us
    all_to_all x1, blocking collectives, body(): lax.all_to_all(correction.reshape(128, 1, 128), 'src', split_axis=0, conc...  24.5 us
    pallas_call x4, Pallas kernels, on_chip(): return run(*near)  13.9 us
    all_to_all x1, blocking collectives, body(): lax.all_to_all(sums, 'seg', split_axis=0, concat_axis=0, tiled=True)  12.4 us
    ppermute x2, starting transfers between devices, body(): swaps.append(lax.ppermute(frame, both, pairs + [(b, a) for a, b in pairs]))  6.63 us
  transfers between devices with their start and end apart: 2, of which 1 were waited for; matrix products, arithmetic and copies ran while one was open for 0% of the time, Pallas kernels for 0%

profile of v2, /device:TPU:1, one launch (start us, length us, event | category | flops | bytes accessed | tf_op | source)
XLA Modules:
  0.0 109.2 jit_solution(16824578053794973560)
XLA Ops:
  0.6 4.9 %source_sums.1 = (f32[4,320,128]{2,1,0:T(8,128)S(1)}, f32[128,128]{1,0:T(8,128)S(1)}) custom-call(s32[1,128]{1,0:T(1,128)} %count_ref.1, f32[128,128]{1,0:T(8,128)} %bitcast.17, f32[128,128]{1,0:T(8,128)} %bitcast.25, f32[5,16384]{1,0:T(8,128)} %part_ref.3, s32[128,128]{1,0:T(8,128)} %bitcast.19), custom_call_target="tpu_custom_call" | custom-call | tf_op jit(solution)/shard_map/source_sums/pallas_call | solution.py:373
  5.5 0.0 copy-start
  5.5 0.0 copy-start.1
  5.5 0.0 copy-start.2
  5.5 0.0 copy-start.3
  5.6 0.0 copy-start.4
  5.6 0.0 copy-start.5
  5.6 0.0 copy-start.6
  5.6 12.4 %all_to_all.15.sums_ref = f32[4,320,128]{2,1,0:T(8,128)S(1)} all-to-all(f32[4,320,128]{2,1,0:T(8,128)S(1)} %get-tuple-element.11), channel_id=1, replica_groups=mesh['src'=128,'seg'=4] {'seg'}, dimensions={0} | all-to-all | bytes 1310720 | tf_op jit(solution)/shard_map/all_to_all | solution.py:396
  18.0 0.0 copy-done
  18.0 0.0 copy-done.1
  18.0 0.0 copy-done.2
  18.0 0.0 copy-done.3
  18.0 0.0 copy-done.4
  18.0 4.7 %source_solve.1 = (f32[5,2048]{1,0:T(8,128)}, f32[640,128]{1,0:T(8,128)S(1)}, f32[128,128]{1,0:T(8,128)S(1)}, f32[128,128]{1,0:T(8,128)S(1)}) custom-call(f32[4,320,128]{2,1,0:T(8,128)S(1)} %all_to_all.15.sums_ref, f32[5,2048]{1,0:T(8,128)S(1)} %copy-done.4, f32[128,128]{1,0:T(8,128)S(1)} %bitcast.18, f32[128,128]{1,0:T(8,128)S(1)} %get-tuple-element.12.live_ref, ...), custom_call_target="tpu_custom_call" | custom-call | tf_op jit(solution)/shard_map/source_solve/pallas_call | solution.py:373
  22.7 48.5 %all_to_all.16 = f32[128,1,640]{2,1,0:T(1,128)S(1)} all-to-all(f32[128,1,640]{2,1,0:T(1,128)S(1)} %bitcast.16), channel_id=1, replica_groups=mesh['src'=128,'seg'=4] {'src'}, dimensions={0} | all-to-all | bytes 655360 | tf_op jit(solution)/shard_map/all_to_all | solution.py:406
  71.3 2.6 %band_sums.1.own_ref = f32[40,128]{1,0:T(8,128)S(1)} custom-call(f32[640,128]{1,0:T(8,128)S(1)} %bitcast.14, f32[3,64]{1,0:T(4,128)S(1)} %copy-done.7), custom_call_target="tpu_custom_call" | custom-call | tf_op jit(solution)/shard_map/band_sums/pallas_call | solution.py:373
  73.9 2.2 %collective-permute-start = (f32[40,128]{1,0:T(8,128)S(1)}, f32[40,128]{1,0:T(8,128)S(1)}, u32[]{:S(2)}, u32[]{:S(2)}) collective-permute-start(f32[40,128]{1,0:T(8,128)S(1)} %band_sums.1.own_ref), channel_id=1, source_target_pairs={{0,1},{2,3},{4,5},{6,7},{8,9},{10,11},{12,13},{14,15},{16,17},{18,... | collective-permute-start | bytes 61448 | tf_op jit(solution)/shard_map/ppermute | solution.py:424
  76.1 4.4 %collective-permute-start.1 = (f32[40,128]{1,0:T(8,128)S(1)}, f32[40,128]{1,0:T(8,128)S(1)}, u32[]{:S(2)}, u32[]{:S(2)}) collective-permute-start(f32[40,128]{1,0:T(8,128)S(1)} %band_sums.1.own_ref), channel_id=1, source_target_pairs={{1,2},{3,4},{5,6},{7,8},{9,10},{11,12},{13,14},{15,16},{17,18},{19... | collective-permute-start | bytes 61448 | tf_op jit(solution)/shard_map/ppermute | solution.py:424
  80.6 0.0 collective-permute-done.even_ref
  80.6 1.8 %collective-permute-done.1.odd_ref = f32[40,128]{1,0:T(8,128)S(1)} collective-permute-done((f32[40,128]{1,0:T(8,128)S(1)}, f32[40,128]{1,0:T(8,128)S(1)}, u32[]{:S(2)}, u32[]{:S(2)}) %collective-permute-start.1) | collective-permute-done | bytes 20512 | tf_op jit(solution)/shard_map/ppermute | solution.py:424
  82.4 1.7 %attitude.1 = (f32[3,64]{1,0:T(4,128)}, f32[128,128]{1,0:T(8,128)S(1)}) custom-call(s32[1]{0:T(128)} %bitcast.5.place_ref, f32[40,128]{1,0:T(8,128)S(1)} %band_sums.1.own_ref, f32[40,128]{1,0:T(8,128)S(1)} %collective-permute-done.even_ref, f32[40,128]{1,0:T(8,128)S(1)} %collective-permute-done.1.odd_ref, f32[640,128]{1,0:T(8,128)S(1)} %bitcast.15), custom_call_target="tpu_custom_call" | custom-call | tf_op jit(solution)/shard_map/attitude/pallas_call | solution.py:373
  84.1 24.5 %all_to_all.17 = f32[128,1,128]{2,1,0:T(1,128)S(1)} all-to-all(f32[128,1,128]{2,1,0:T(1,128)S(1)} %bitcast.23), channel_id=1, replica_groups=mesh['src'=128,'seg'=4] {'src'}, dimensions={0} | all-to-all | bytes 131072 | tf_op jit(solution)/shard_map/all_to_all | solution.py:435
  108.6 0.6 subtract_bitcast_fusion
  (4 shorter events, 0.0 us)
Async XLA Ops:
  5.5 12.5 %copy-start = (f32[5,16384]{1,0:T(8,128)S(1)}, f32[5,16384]{1,0:T(8,128)}, u32[]{:S(2)}) copy-start(f32[5,16384]{1,0:T(8,128)} %part_ref.3) | copy-start | bytes 983044
  5.5 12.5 %copy-start.1 = (f32[3,16384]{1,0:T(4,128)S(1)}, f32[3,16384]{1,0:T(4,128)}, u32[]{:S(2)}) copy-start(f32[3,16384]{1,0:T(4,128)} %dir_ref.1) | copy-start | bytes 589828
  5.5 12.5 %copy-start.2 = (f32[16384]{0:T(1024)S(1)}, f32[16384]{0:T(1024)}, u32[]{:S(2)}) copy-start(f32[16384]{0:T(1024)} %param.10) | copy-start | bytes 196612
  5.5 12.5 %copy-start.3 = (s32[16384]{0:T(1024)S(1)}, s32[16384]{0:T(1024)}, u32[]{:S(2)}) copy-start(s32[16384]{0:T(1024)} %param.17) | copy-start | bytes 196612
  5.6 12.5 %copy-start.4 = (f32[5,2048]{1,0:T(8,128)S(1)}, f32[5,2048]{1,0:T(8,128)}, u32[]{:S(2)}) copy-start(f32[5,2048]{1,0:T(8,128)} %prior_ref.2) | copy-start | bytes 122884
  5.6 12.5 %copy-start.5 = (f32[16384]{0:T(1024)S(1)}, f32[16384]{0:T(1024)}, u32[]{:S(2)}) copy-start(f32[16384]{0:T(1024)} %param.12) | copy-start | bytes 196612
  5.6 12.4 %copy-start.6 = (s32[16384]{0:T(1024)S(1)}, s32[16384]{0:T(1024)}, u32[]{:S(2)}) copy-start(s32[16384]{0:T(1024)} %param.18) | copy-start | bytes 196612
  22.7 48.6 %copy-start.7 = (f32[3,64]{1,0:T(4,128)S(1)}, f32[3,64]{1,0:T(4,128)}, u32[]{:S(2)}) copy-start(f32[3,64]{1,0:T(4,128)} %prior_ref.3) | copy-start | bytes 2308
  73.9 6.7 %collective-permute-start = (f32[40,128]{1,0:T(8,128)S(1)}, f32[40,128]{1,0:T(8,128)S(1)}, u32[]{:S(2)}, u32[]{:S(2)}) collective-permute-start(f32[40,128]{1,0:T(8,128)S(1)} %band_sums.1.own_ref), channel_id=1, source_target_pairs={{0,1},{2,3},{4,5},{6,7},{8,9},{10,11},{12,13},{14,15},{16,17},{18,... | collective-permute-start | bytes 61448 | tf_op jit(solution)/shard_map/ppermute | solution.py:424
  76.1 6.3 %collective-permute-start.1 = (f32[40,128]{1,0:T(8,128)S(1)}, f32[40,128]{1,0:T(8,128)S(1)}, u32[]{:S(2)}, u32[]{:S(2)}) collective-permute-start(f32[40,128]{1,0:T(8,128)S(1)} %band_sums.1.own_ref), channel_id=1, source_target_pairs={{1,2},{3,4},{5,6},{7,8},{9,10},{11,12},{13,14},{15,16},{17,18},{19... | collective-permute-start | bytes 61448 | tf_op jit(solution)/shard_map/ppermute | solution.py:424

commit v3 on v2

--- a/solution.py
+++ b/solution.py
@@ -7,6 +7,7 @@
 from jax.experimental.pallas import tpu as pltpu
 from jax.sharding import PartitionSpec as P
 
+
 ITERS_ATT = 6
 DAMPING = 0.5
 LEFT = 20
@@ -17,15 +18,10 @@
 
 VMEM_SPEC = pl.BlockSpec(memory_space=pltpu.VMEM)
 SMEM_SPEC = pl.BlockSpec(memory_space=pltpu.SMEM)
+ANY_SPEC = pl.BlockSpec(memory_space=pl.ANY)
 NT = (((1,), (1,)), ((), ()))
 SUMS_UNROLL = 4
 BAND_UNROLL = 4
-
-
-def split_parts(values):
-    high = values.astype(jnp.bfloat16)
-    low = (values - high.astype(jnp.float32)).astype(jnp.bfloat16)
-    return high, low
 
 
 def spline_weights(local_time):
@@ -56,8 +52,24 @@
 
 
 def source_sums_kernel(
-    count_ref, res_ref, weight_ref, part_ref, src_ref, out_ref, live_ref, acc_ref, rows_refs, feat_refs
+    count_ref, res_far, weight_far, part_far, src_far, out_ref, live_ref,
+    acc_ref, rows_refs, feat_refs, res_ref, weight_ref, part_ref, src_ref, sems,
 ):
+    chunks = 16 // SUMS_UNROLL
+
+    def copies(n):
+        rows = pl.ds(pl.multiple_of(n * (8 * SUMS_UNROLL), 8 * SUMS_UNROLL), 8 * SUMS_UNROLL)
+        cols = pl.ds(pl.multiple_of(n * (1024 * SUMS_UNROLL), 1024 * SUMS_UNROLL), 1024 * SUMS_UNROLL)
+        return [
+            pltpu.make_async_copy(part_far.at[:, cols], part_ref.at[:, cols], sems.at[n, 0]),
+            pltpu.make_async_copy(src_far.at[rows, :], src_ref.at[rows, :], sems.at[n, 1]),
+            pltpu.make_async_copy(weight_far.at[rows, :], weight_ref.at[rows, :], sems.at[n, 2]),
+            pltpu.make_async_copy(res_far.at[rows, :], res_ref.at[rows, :], sems.at[n, 3]),
+        ]
+
+    for n in range(chunks):
+        for copy in copies(n):
+            copy.start()
     acc_ref[...] = jnp.zeros_like(acc_ref)
     ids = lax.broadcasted_iota(jnp.int32, (256, 128), 0).astype(jnp.float32).astype(jnp.bfloat16)
     lane8 = lax.broadcasted_iota(jnp.int32, (8, 128), 1)
@@ -106,6 +118,8 @@
             acc_ref[h] += sums[:, h * 128 : (h + 1) * 128]
 
     def groups(step, carry):
+        for copy in copies(step):
+            copy.wait()
         for n in range(SUMS_UNROLL):
             group(step * SUMS_UNROLL + n, feat_refs.at[n], rows_refs.at[n])
         return carry
@@ -160,9 +174,9 @@
 
 def source_solve_kernel(
     sums_ref, prior_ref, res_ref, live_ref, part_ref, src_ref, frac_ref, interval_ref, dir_ref,
-    update_ref, pack_ref, base_ref, scale_ref, table_ref, root_ref, corr_ref,
+    update_far, pack_ref, base_ref, scale_ref, update_ref, root_ref, corr_ref, sem,
 ):
-    table_ref[...] = jnp.zeros_like(table_ref)
+    tables = []
     for h in range(2):
         terms = []
         for f in range(20):
@@ -176,11 +190,14 @@
                 prior = [prior_ref[i : i + 1, (2 * r + h) * 128 : (2 * r + h + 1) * 128] for r in HIGH_ORDER]
                 terms[number] = terms[number] + jnp.concatenate(prior, 0)
         solved = cholesky_solve5(terms[:15], terms[15:])
+        tables.append(solved)
         for p in range(5):
             for n, r in enumerate(HIGH_ORDER):
-                table_ref[p : p + 1, (2 * r + h) * 128 : (2 * r + h + 1) * 128] = solved[p][n : n + 1]
-    update_ref[...] = table_ref[0:5, :]
+                update_ref[p : p + 1, (2 * r + h) * 128 : (2 * r + h + 1) * 128] = solved[p][n : n + 1]
+    update_copy = pltpu.make_async_copy(update_ref, update_far, sem)
+    update_copy.start()
     root_ref[...] = jnp.sqrt(live_ref[...])
+    sub8 = lax.broadcasted_iota(jnp.int32, (8, 128), 0)
 
     def group(g, carry):
         first = pl.multiple_of(g * 8, 8)
@@ -189,18 +206,24 @@
         root8 = root_ref[pl.ds(first, 8), :]
         time8 = (interval_ref[pl.ds(first, 8), :] & 63).astype(jnp.float32) + frac_ref[pl.ds(first, 8), :]
         low8 = src8 & 127
-        high8 = src8 >> 7
+        high8 = src8 >> 8
+        place8 = (high8 >> 1) + ((high8 & 1) << 2) + (((src8 >> 7) & 1) << 3)
         pack = pack_ref.at[pl.ds(pl.multiple_of(g * 40, 8), 40), :]
         corr_rows = []
         for k in range(8):
             at = pl.multiple_of((g * 8 + k) * 128, 128)
             low = jnp.broadcast_to(low8[k : k + 1], (8, 128))
-            high = jnp.broadcast_to(high8[k : k + 1], (8, 128))
-            found = jnp.zeros((8, 128), jnp.float32)
-            for c in range(16):
-                taken = jnp.take_along_axis(table_ref[:, c * 128 : (c + 1) * 128], low, axis=1, mode="promise_in_bounds")
-                found = jnp.where(high == c, taken, found)
-            corr = jnp.sum(part_ref[:, pl.ds(at, 128)] * found[0:5], 0, keepdims=True)
+            place = jnp.broadcast_to(place8[k : k + 1], (8, 128))
+            part = part_ref[:, pl.ds(at, 128)]
+            found = None
+            masks = [place == sub8, place == sub8 + 8]
+            for p in range(5):
+                wide = jnp.broadcast_to(part[p : p + 1], (8, 128))
+                for h in range(2):
+                    taken = jnp.take_along_axis(tables[h][p], low, axis=1, mode="promise_in_bounds")
+                    term = jnp.where(masks[h], taken * wide, 0.0)
+                    found = term if found is None else found + term
+            corr = jnp.sum(found, 0, keepdims=True)
             corr_rows.append(corr)
             root = root8[k : k + 1]
             first_pass = root * (res8[k : k + 1] - corr)
@@ -208,10 +231,11 @@
         corr_ref[pl.ds(first, 8), :] = jnp.concatenate(corr_rows, 0)
         return carry
 
-    lax.fori_loop(0, 16, group, 0)
+    lax.fori_loop(0, 16, group, 0, unroll=4)
     live = root_ref[...] > 0.0
     base_ref[...] = res_ref[...] - jnp.where(live, corr_ref[...], 0.0)
     scale_ref[...] = jnp.where(live, 1.0 / jnp.where(live, root_ref[...], 1.0), 0.0)
+    update_copy.wait()
 
 
 def band_sums_kernel(slots_ref, prior_ref, frame_ref, feat_refs, a_refs, acc_ref, prior_pad):
@@ -295,7 +319,7 @@
     return total
 
 
-def attitude_kernel(place_ref, own_ref, even_ref, odd_ref, slots_ref, att_ref, corr_ref, *, knots_total):
+def attitude_kernel(place_ref, own_ref, even_ref, odd_ref, slots_ref, att_far, corr_ref, att_ref, sem, *, knots_total):
     place = place_ref[0]
     lane = lax.broadcasted_iota(jnp.int32, (1, 128), 1)
     lane8 = lax.broadcasted_iota(jnp.int32, (8, 128), 1)
@@ -336,6 +360,8 @@
             applied = applied + pltpu.roll(columns_apply(upper_cols[d - 1], att), d, 1)
         att = att + columns_apply(inverse, rhs - applied)
     att_ref[...] = pltpu.roll(att, 128 - LEFT, 1)[0:3, 0:64]
+    att_copy = pltpu.make_async_copy(att_ref, att_far, sem)
+    att_copy.start()
     tables = [jnp.broadcast_to(att[j : j + 1], (8, 128)) for j in range(3)]
 
     def group(g, carry):
@@ -355,17 +381,17 @@
         return carry
 
     lax.fori_loop(0, 16, group, 0, unroll=4)
-
-
-def call(kernel, outs, n_in, smem_at=(), scratch=(), name=None, far_out=(), far_in=()):
+    att_copy.wait()
+
+
+def call(kernel, outs, n_in, smem_at=(), scratch=(), far_in=(), far_out=()):
     shapes = [jax.ShapeDtypeStruct(s, jnp.float32) if i in far_out else pltpu.VMEM(s, jnp.float32) for i, s in enumerate(outs)]
     run = pl.pallas_call(
         kernel,
         out_shape=shapes,
-        in_specs=[SMEM_SPEC if i in smem_at else VMEM_SPEC for i in range(n_in)],
-        out_specs=[VMEM_SPEC] * len(shapes),
+        in_specs=[SMEM_SPEC if i in smem_at else ANY_SPEC if i in far_in else VMEM_SPEC for i in range(n_in)],
+        out_specs=[ANY_SPEC if i in far_out else VMEM_SPEC for i in range(len(shapes))],
         scratch_shapes=list(scratch),
-        name=name,
     )
 
     def on_chip(*args):
@@ -388,10 +414,13 @@
             pltpu.VMEM((2, 320, 128), jnp.float32),
             pltpu.VMEM((SUMS_UNROLL, 40, 128), jnp.float32),
             pltpu.VMEM((SUMS_UNROLL, 320, 128), jnp.float32),
+            pltpu.VMEM((128, 128), jnp.float32),
+            pltpu.VMEM((128, 128), jnp.float32),
+            pltpu.VMEM((5, 16384), jnp.float32),
+            pltpu.VMEM((128, 128), jnp.int32),
+            pltpu.SemaphoreType.DMA((16 // SUMS_UNROLL, 4)),
         ],
-        "source_sums",
-        (),
-        range(5),
+        range(1, 5),
     )(obs_count, res, weight, src_partials, src)
     gathered = lax.all_to_all(sums, "seg", split_axis=0, concat_axis=0, tiled=True)
     src_update, packed, base, scale = call(
@@ -399,8 +428,13 @@
         [(5, 2048), (640, 128), (128, 128), (128, 128)],
         9,
         (),
-        [pltpu.VMEM((8, 2048), jnp.float32), pltpu.VMEM((128, 128), jnp.float32), pltpu.VMEM((128, 128), jnp.float32)],
-        "source_solve",
+        [
+            pltpu.VMEM((5, 2048), jnp.float32),
+            pltpu.VMEM((128, 128), jnp.float32),
+            pltpu.VMEM((128, 128), jnp.float32),
+            pltpu.SemaphoreType.DMA,
+        ],
+        (),
         (0,),
     )(gathered, src_prior, res, live, src_partials, src, frac, interval, att_dir)
     arrived = lax.all_to_all(packed.reshape(128, 1, 640), "src", split_axis=0, concat_axis=0, tiled=True).reshape(640, 128)
@@ -415,21 +449,20 @@
             pltpu.VMEM((144, 128), jnp.float32),
             pltpu.VMEM((8, 128), jnp.float32),
         ],
-        "band_sums",
     )(arrived, att_prior)
     both = ("src", "seg")
-    swaps = []
-    for start in (0, 1):
+    swaps = {}
+    for start in (1, 0):
         pairs = [(i, i + 1) for i in range(start, devices - 1, 2)]
-        swaps.append(lax.ppermute(frame, both, pairs + [(b, a) for a, b in pairs]))
+        swaps[start] = lax.ppermute(frame, both, pairs + [(b, a) for a, b in pairs])
     place = lax.axis_index(both).astype(jnp.int32).reshape(1)
     att_update, correction = call(
         functools.partial(attitude_kernel, knots_total=devices * 64),
         [(3, 64), (128, 128)],
         5,
         (0,),
+        [pltpu.VMEM((3, 64), jnp.float32), pltpu.SemaphoreType.DMA],
         (),
-        "attitude",
         (0,),
     )(place, frame, swaps[0], swaps[1], arrived)
     returned = lax.all_to_all(correction.reshape(128, 1, 128), "src", split_axis=0, concat_axis=0, tiled=True)

time: 110 us -> 107 us (0.973)
  Pallas kernels: 13.9 us -> 11.7 us
    pallas_call x4, Pallas kernels: 13.9 us -> 11.7 us  [on_chip(): return run(*near)]
where the time goes in v3:
time: 107 us
  blocking collectives  85.3 us (80%)
  Pallas kernels  11.7 us (11%)
  starting transfers between devices  6.63 us (6%)
  waiting for transfers between devices  1.85 us (2%)
    all_to_all x1, blocking collectives, body(): lax.all_to_all(packed.reshape(128, 1, 640), 'src', split_axis=0, concat_a...  48.4 us
    all_to_all x1, blocking collectives, body(): lax.all_to_all(correction.reshape(128, 1, 128), 'src', split_axis=0, conc...  24.5 us
    all_to_all x1, blocking collectives, body(): lax.all_to_all(sums, 'seg', split_axis=0, concat_axis=0, tiled=True)  12.4 us
    pallas_call x4, Pallas kernels, on_chip(): return run(*near)  11.7 us
    ppermute x2, starting transfers between devices, body(): swaps[start] = lax.ppermute(frame, both, pairs + [(b, a) for a, b in pairs])  6.63 us
  transfers between devices with their start and end apart: 2, of which 1 were waited for; matrix products, arithmetic and copies ran while one was open for 0% of the time, Pallas kernels for 0%

profile of v3, /device:TPU:1, one launch (start us, length us, event | category | flops | bytes accessed | tf_op | source)
XLA Modules:
  0.0 107.0 jit_solution(6645655901685962760)
XLA Ops:
  0.6 5.4 %shard_map.121 = (f32[4,320,128]{2,1,0:T(8,128)S(1)}, f32[128,128]{1,0:T(8,128)S(1)}) custom-call(s32[1,128]{1,0:T(1,128)} %count_ref.1, f32[128,128]{1,0:T(8,128)} %bitcast.17, f32[128,128]{1,0:T(8,128)} %bitcast.25, f32[5,16384]{1,0:T(8,128)} %part_ref.1, s32[128,128]{1,0:T(8,128)} %bitcast.19), custom_call_target="tpu_custom_call" | custom-call | tf_op jit(solution)/shard_map/pallas_call | solution.py:399
  6.1 0.0 copy-start
  6.1 0.0 copy-start.1
  6.1 0.0 copy-start.2
  6.1 0.0 copy-start.3
  6.1 0.0 copy-start.4
  6.1 0.0 copy-start.5
  6.1 0.0 copy-start.6
  6.2 12.4 %all_to_all.15.sums_ref = f32[4,320,128]{2,1,0:T(8,128)S(1)} all-to-all(f32[4,320,128]{2,1,0:T(8,128)S(1)} %get-tuple-element.11), channel_id=1, replica_groups=mesh['src'=128,'seg'=4] {'seg'}, dimensions={0} | all-to-all | bytes 1310720 | tf_op jit(solution)/shard_map/all_to_all | solution.py:425
  18.6 0.0 copy-done
  18.6 0.0 copy-done.1
  18.6 0.0 copy-done.2
  18.6 0.0 copy-done.3
  18.6 2.4 %shard_map.122 = (f32[5,2048]{1,0:T(8,128)}, f32[640,128]{1,0:T(8,128)S(1)}, f32[128,128]{1,0:T(8,128)S(1)}, f32[128,128]{1,0:T(8,128)S(1)}) custom-call(f32[4,320,128]{2,1,0:T(8,128)S(1)} %all_to_all.15.sums_ref, f32[5,2048]{1,0:T(8,128)S(1)} %copy-done.4, f32[128,128]{1,0:T(8,128)S(1)} %bitcast.18, f32[128,128]{1,0:T(8,128)S(1)} %get-tuple-element.12.live_ref, ...), custom_call_target="tpu_custom_call" | custom-call | tf_op jit(solution)/shard_map/pallas_call | solution.py:399
  21.0 0.0 copy-start.7
  21.0 48.4 %all_to_all.16 = f32[128,1,640]{2,1,0:T(1,128)S(1)} all-to-all(f32[128,1,640]{2,1,0:T(1,128)S(1)} %bitcast.16), channel_id=1, replica_groups=mesh['src'=128,'seg'=4] {'src'}, dimensions={0} | all-to-all | bytes 655360 | tf_op jit(solution)/shard_map/all_to_all | solution.py:440
  69.4 2.6 %shard_map.123.own_ref = f32[40,128]{1,0:T(8,128)S(1)} custom-call(f32[640,128]{1,0:T(8,128)S(1)} %bitcast.14, f32[3,64]{1,0:T(4,128)S(1)} %copy-done.7), custom_call_target="tpu_custom_call" | custom-call | tf_op jit(solution)/shard_map/pallas_call | solution.py:399
  72.0 2.2 %collective-permute-start = (f32[40,128]{1,0:T(8,128)S(1)}, f32[40,128]{1,0:T(8,128)S(1)}, u32[]{:S(2)}, u32[]{:S(2)}) collective-permute-start(f32[40,128]{1,0:T(8,128)S(1)} %shard_map.123.own_ref), channel_id=1, source_target_pairs={{0,1},{2,3},{4,5},{6,7},{8,9},{10,11},{12,13},{14,15},{16,17},{18,... | collective-permute-start | bytes 61448 | tf_op jit(solution)/shard_map/ppermute | solution.py:457
  74.2 4.4 %collective-permute-start.1 = (f32[40,128]{1,0:T(8,128)S(1)}, f32[40,128]{1,0:T(8,128)S(1)}, u32[]{:S(2)}, u32[]{:S(2)}) collective-permute-start(f32[40,128]{1,0:T(8,128)S(1)} %shard_map.123.own_ref), channel_id=1, source_target_pairs={{1,2},{3,4},{5,6},{7,8},{9,10},{11,12},{13,14},{15,16},{17,18},{19... | collective-permute-start | bytes 61448 | tf_op jit(solution)/shard_map/ppermute | solution.py:457
  78.7 0.0 collective-permute-done.even_ref
  78.7 1.9 %collective-permute-done.1.odd_ref = f32[40,128]{1,0:T(8,128)S(1)} collective-permute-done((f32[40,128]{1,0:T(8,128)S(1)}, f32[40,128]{1,0:T(8,128)S(1)}, u32[]{:S(2)}, u32[]{:S(2)}) %collective-permute-start.1) | collective-permute-done | bytes 20512 | tf_op jit(solution)/shard_map/ppermute | solution.py:457
  80.6 1.3 %shard_map.124 = (f32[3,64]{1,0:T(4,128)}, f32[128,128]{1,0:T(8,128)S(1)}) custom-call(s32[1]{0:T(128)} %bitcast.5.place_ref, f32[40,128]{1,0:T(8,128)S(1)} %shard_map.123.own_ref, f32[40,128]{1,0:T(8,128)S(1)} %collective-permute-done.even_ref, f32[40,128]{1,0:T(8,128)S(1)} %collective-permute-done.1.odd_ref, f32[640,128]{1,0:T(8,128)S(1)} %bitcast.15), custom_call_target="tpu_custom_call" | custom-call | tf_op jit(solution)/shard_map/pallas_call | solution.py:399
  81.9 24.5 %all_to_all.17 = f32[128,1,128]{2,1,0:T(1,128)S(1)} all-to-all(f32[128,1,128]{2,1,0:T(1,128)S(1)} %bitcast.23), channel_id=1, replica_groups=mesh['src'=128,'seg'=4] {'src'}, dimensions={0} | all-to-all | bytes 131072 | tf_op jit(solution)/shard_map/all_to_all | solution.py:468
  106.4 0.6 subtract_bitcast_fusion
  (4 shorter events, 0.0 us)
Async XLA Ops:
  6.1 12.5 %copy-start = (f32[5,16384]{1,0:T(8,128)S(1)}, f32[5,16384]{1,0:T(8,128)}, u32[]{:S(2)}) copy-start(f32[5,16384]{1,0:T(8,128)} %part_ref.1) | copy-start | bytes 983044
  6.1 12.5 %copy-start.1 = (f32[3,16384]{1,0:T(4,128)S(1)}, f32[3,16384]{1,0:T(4,128)}, u32[]{:S(2)}) copy-start(f32[3,16384]{1,0:T(4,128)} %dir_ref.1) | copy-start | bytes 589828
  6.1 12.5 %copy-start.2 = (f32[16384]{0:T(1024)S(1)}, f32[16384]{0:T(1024)}, u32[]{:S(2)}) copy-start(f32[16384]{0:T(1024)} %param.10) | copy-start | bytes 196612
  6.1 12.5 %copy-start.3 = (s32[16384]{0:T(1024)S(1)}, s32[16384]{0:T(1024)}, u32[]{:S(2)}) copy-start(s32[16384]{0:T(1024)} %param.17) | copy-start | bytes 196612
  6.1 12.5 %copy-start.4 = (f32[5,2048]{1,0:T(8,128)S(1)}, f32[5,2048]{1,0:T(8,128)}, u32[]{:S(2)}) copy-start(f32[5,2048]{1,0:T(8,128)} %prior_ref.2) | copy-start | bytes 122884
  6.1 12.5 %copy-start.5 = (f32[16384]{0:T(1024)S(1)}, f32[16384]{0:T(1024)}, u32[]{:S(2)}) copy-start(f32[16384]{0:T(1024)} %param.12) | copy-start | bytes 196612
  6.1 12.5 %copy-start.6 = (s32[16384]{0:T(1024)S(1)}, s32[16384]{0:T(1024)}, u32[]{:S(2)}) copy-start(s32[16384]{0:T(1024)} %param.18) | copy-start | bytes 196612
  21.0 48.4 %copy-start.7 = (f32[3,64]{1,0:T(4,128)S(1)}, f32[3,64]{1,0:T(4,128)}, u32[]{:S(2)}) copy-start(f32[3,64]{1,0:T(4,128)} %prior_ref.3) | copy-start | bytes 2308
  72.0 6.7 %collective-permute-start = (f32[40,128]{1,0:T(8,128)S(1)}, f32[40,128]{1,0:T(8,128)S(1)}, u32[]{:S(2)}, u32[]{:S(2)}) collective-permute-start(f32[40,128]{1,0:T(8,128)S(1)} %shard_map.123.own_ref), channel_id=1, source_target_pairs={{0,1},{2,3},{4,5},{6,7},{8,9},{10,11},{12,13},{14,15},{16,17},{18,... | collective-permute-start | bytes 61448 | tf_op jit(solution)/shard_map/ppermute | solution.py:457
  74.2 6.3 %collective-permute-start.1 = (f32[40,128]{1,0:T(8,128)S(1)}, f32[40,128]{1,0:T(8,128)S(1)}, u32[]{:S(2)}, u32[]{:S(2)}) collective-permute-start(f32[40,128]{1,0:T(8,128)S(1)} %shard_map.123.own_ref), channel_id=1, source_target_pairs={{1,2},{3,4},{5,6},{7,8},{9,10},{11,12},{13,14},{15,16},{17,18},{19... | collective-permute-start | bytes 61448 | tf_op jit(solution)/shard_map/ppermute | solution.py:457

commit v4 on v3

--- a/solution.py
+++ b/solution.py
@@ -20,8 +20,8 @@
 SMEM_SPEC = pl.BlockSpec(memory_space=pltpu.SMEM)
 ANY_SPEC = pl.BlockSpec(memory_space=pl.ANY)
 NT = (((1,), (1,)), ((), ()))
-SUMS_UNROLL = 4
-BAND_UNROLL = 4
+SUMS_UNROLL = 8
+BAND_UNROLL = 8
 
 
 def spline_weights(local_time):
@@ -52,24 +52,8 @@
 
 
 def source_sums_kernel(
-    count_ref, res_far, weight_far, part_far, src_far, out_ref, live_ref,
-    acc_ref, rows_refs, feat_refs, res_ref, weight_ref, part_ref, src_ref, sems,
+    count_ref, res_ref, weight_ref, part_ref, src_ref, out_ref, live_ref, acc_ref, rows_refs, feat_refs
 ):
-    chunks = 16 // SUMS_UNROLL
-
-    def copies(n):
-        rows = pl.ds(pl.multiple_of(n * (8 * SUMS_UNROLL), 8 * SUMS_UNROLL), 8 * SUMS_UNROLL)
-        cols = pl.ds(pl.multiple_of(n * (1024 * SUMS_UNROLL), 1024 * SUMS_UNROLL), 1024 * SUMS_UNROLL)
-        return [
-            pltpu.make_async_copy(part_far.at[:, cols], part_ref.at[:, cols], sems.at[n, 0]),
-            pltpu.make_async_copy(src_far.at[rows, :], src_ref.at[rows, :], sems.at[n, 1]),
-            pltpu.make_async_copy(weight_far.at[rows, :], weight_ref.at[rows, :], sems.at[n, 2]),
-            pltpu.make_async_copy(res_far.at[rows, :], res_ref.at[rows, :], sems.at[n, 3]),
-        ]
-
-    for n in range(chunks):
-        for copy in copies(n):
-            copy.start()
     acc_ref[...] = jnp.zeros_like(acc_ref)
     ids = lax.broadcasted_iota(jnp.int32, (256, 128), 0).astype(jnp.float32).astype(jnp.bfloat16)
     lane8 = lax.broadcasted_iota(jnp.int32, (8, 128), 1)
@@ -118,8 +102,6 @@
             acc_ref[h] += sums[:, h * 128 : (h + 1) * 128]
 
     def groups(step, carry):
-        for copy in copies(step):
-            copy.wait()
         for n in range(SUMS_UNROLL):
             group(step * SUMS_UNROLL + n, feat_refs.at[n], rows_refs.at[n])
         return carry
@@ -240,7 +222,7 @@
 
 def band_sums_kernel(slots_ref, prior_ref, frame_ref, feat_refs, a_refs, acc_ref, prior_pad):
     acc_ref[...] = jnp.zeros_like(acc_ref)
-    ids = lax.broadcasted_iota(jnp.int32, (64, 128), 0).astype(jnp.float32).astype(jnp.bfloat16)
+    ids = lax.broadcasted_iota(jnp.int32, (128, 128), 0).astype(jnp.float32).astype(jnp.bfloat16)
 
     def group(g, a_ref, feat_ref):
         slots = slots_ref.at[pl.ds(pl.multiple_of(g * 40, 8), 40), :]
@@ -273,7 +255,7 @@
                 else:
                     a_ref[k, 128:144, :] = jnp.concatenate([high.astype(jnp.float32), rest], 0).astype(jnp.bfloat16)
             hots.append(hot_rows(ids, floor8[k : k + 1]))
-        acc_ref[:, 0:64] += lax.dot_general(side_by_side(a_ref), jnp.concatenate(hots, 1), NT, preferred_element_type=jnp.float32)
+        acc_ref[...] += lax.dot_general(side_by_side(a_ref), jnp.concatenate(hots, 1), NT, preferred_element_type=jnp.float32)
 
     def groups(step, carry):
         for n in range(BAND_UNROLL):
@@ -389,7 +371,7 @@
     run = pl.pallas_call(
         kernel,
         out_shape=shapes,
-        in_specs=[SMEM_SPEC if i in smem_at else ANY_SPEC if i in far_in else VMEM_SPEC for i in range(n_in)],
+        in_specs=[SMEM_SPEC if i in smem_at else VMEM_SPEC for i in range(n_in)],
         out_specs=[ANY_SPEC if i in far_out else VMEM_SPEC for i in range(len(shapes))],
         scratch_shapes=list(scratch),
     )
@@ -414,11 +396,6 @@
             pltpu.VMEM((2, 320, 128), jnp.float32),
             pltpu.VMEM((SUMS_UNROLL, 40, 128), jnp.float32),
             pltpu.VMEM((SUMS_UNROLL, 320, 128), jnp.float32),
-            pltpu.VMEM((128, 128), jnp.float32),
-            pltpu.VMEM((128, 128), jnp.float32),
-            pltpu.VMEM((5, 16384), jnp.float32),
-            pltpu.VMEM((128, 128), jnp.int32),
-            pltpu.SemaphoreType.DMA((16 // SUMS_UNROLL, 4)),
         ],
         range(1, 5),
     )(obs_count, res, weight, src_partials, src)

time: 107 us -> 106 us (level)
  Pallas kernels: 11.7 us -> 10.6 us
    pallas_call x4, Pallas kernels: 11.7 us -> 10.6 us  [on_chip(): return run(*near)]
where the time goes in v4:
time: 106 us
  blocking collectives  85.3 us (80%)
  Pallas kernels  10.6 us (10%)
  starting transfers between devices  6.63 us (6%)
  waiting for transfers between devices  1.85 us (2%)
    all_to_all x1, blocking collectives, body(): lax.all_to_all(packed.reshape(128, 1, 640), 'src', split_axis=0, concat_a...  48.4 us
    all_to_all x1, blocking collectives, body(): lax.all_to_all(correction.reshape(128, 1, 128), 'src', split_axis=0, conc...  24.5 us
    all_to_all x1, blocking collectives, body(): lax.all_to_all(sums, 'seg', split_axis=0, concat_axis=0, tiled=True)  12.4 us
    pallas_call x4, Pallas kernels, on_chip(): return run(*near)  10.6 us
    ppermute x2, starting transfers between devices, body(): swaps[start] = lax.ppermute(frame, both, pairs + [(b, a) for a, b in pairs])  6.63 us
  transfers between devices with their start and end apart: 2, of which 1 were waited for; matrix products, arithmetic and copies ran while one was open for 0% of the time, Pallas kernels for 0%

profile of v4, /device:TPU:1, one launch (start us, length us, event | category | flops | bytes accessed | tf_op | source)
XLA Modules:
  0.0 105.8 jit_solution(17784116427964115151)
XLA Ops:
  0.6 4.4 %shard_map.121 = (f32[4,320,128]{2,1,0:T(8,128)S(1)}, f32[128,128]{1,0:T(8,128)S(1)}) custom-call(s32[1,128]{1,0:T(1,128)} %count_ref.1, f32[128,128]{1,0:T(8,128)} %bitcast.17, f32[128,128]{1,0:T(8,128)} %bitcast.25, f32[5,16384]{1,0:T(8,128)} %part_ref.3, s32[128,128]{1,0:T(8,128)} %bitcast.19), custom_call_target="tpu_custom_call" | custom-call | tf_op jit(solution)/shard_map/pallas_call | solution.py:381
  5.1 0.0 copy-start
  5.1 0.0 copy-start.1
  5.1 0.0 copy-start.2
  5.1 0.0 copy-start.3
  5.1 0.0 copy-start.4
  5.1 0.0 copy-start.5
  5.2 0.0 copy-start.6
  5.2 12.4 %all_to_all.15.sums_ref = f32[4,320,128]{2,1,0:T(8,128)S(1)} all-to-all(f32[4,320,128]{2,1,0:T(8,128)S(1)} %get-tuple-element.11), channel_id=1, replica_groups=mesh['src'=128,'seg'=4] {'seg'}, dimensions={0} | all-to-all | bytes 1310720 | tf_op jit(solution)/shard_map/all_to_all | solution.py:402
  17.6 0.0 copy-done
  17.6 0.0 copy-done.1
  17.6 0.0 copy-done.2
  17.6 2.4 %shard_map.122 = (f32[5,2048]{1,0:T(8,128)}, f32[640,128]{1,0:T(8,128)S(1)}, f32[128,128]{1,0:T(8,128)S(1)}, f32[128,128]{1,0:T(8,128)S(1)}) custom-call(f32[4,320,128]{2,1,0:T(8,128)S(1)} %all_to_all.15.sums_ref, f32[5,2048]{1,0:T(8,128)S(1)} %copy-done.4, f32[128,128]{1,0:T(8,128)S(1)} %bitcast.18, f32[128,128]{1,0:T(8,128)S(1)} %get-tuple-element.12.live_ref, ...), custom_call_target="tpu_custom_call" | custom-call | tf_op jit(solution)/shard_map/pallas_call | solution.py:381
  20.0 0.0 copy-start.7
  20.0 48.4 %all_to_all.16 = f32[128,1,640]{2,1,0:T(1,128)S(1)} all-to-all(f32[128,1,640]{2,1,0:T(1,128)S(1)} %bitcast.16), channel_id=1, replica_groups=mesh['src'=128,'seg'=4] {'src'}, dimensions={0} | all-to-all | bytes 655360 | tf_op jit(solution)/shard_map/all_to_all | solution.py:417
  68.4 0.0 copy-done.7
  68.4 2.4 %shard_map.123.own_ref = f32[40,128]{1,0:T(8,128)S(1)} custom-call(f32[640,128]{1,0:T(8,128)S(1)} %bitcast.14, f32[3,64]{1,0:T(4,128)S(1)} %copy-done.7), custom_call_target="tpu_custom_call" | custom-call | tf_op jit(solution)/shard_map/pallas_call | solution.py:381
  70.9 2.2 %collective-permute-start = (f32[40,128]{1,0:T(8,128)S(1)}, f32[40,128]{1,0:T(8,128)S(1)}, u32[]{:S(2)}, u32[]{:S(2)}) collective-permute-start(f32[40,128]{1,0:T(8,128)S(1)} %shard_map.123.own_ref), channel_id=1, source_target_pairs={{0,1},{2,3},{4,5},{6,7},{8,9},{10,11},{12,13},{14,15},{16,17},{18,... | collective-permute-start | bytes 61448 | tf_op jit(solution)/shard_map/ppermute | solution.py:434
  73.1 4.4 %collective-permute-start.1 = (f32[40,128]{1,0:T(8,128)S(1)}, f32[40,128]{1,0:T(8,128)S(1)}, u32[]{:S(2)}, u32[]{:S(2)}) collective-permute-start(f32[40,128]{1,0:T(8,128)S(1)} %shard_map.123.own_ref), channel_id=1, source_target_pairs={{1,2},{3,4},{5,6},{7,8},{9,10},{11,12},{13,14},{15,16},{17,18},{19... | collective-permute-start | bytes 61448 | tf_op jit(solution)/shard_map/ppermute | solution.py:434
  77.5 0.0 collective-permute-done.even_ref
  77.5 1.8 %collective-permute-done.1.odd_ref = f32[40,128]{1,0:T(8,128)S(1)} collective-permute-done((f32[40,128]{1,0:T(8,128)S(1)}, f32[40,128]{1,0:T(8,128)S(1)}, u32[]{:S(2)}, u32[]{:S(2)}) %collective-permute-start.1) | collective-permute-done | bytes 20512 | tf_op jit(solution)/shard_map/ppermute | solution.py:434
  79.4 1.3 %shard_map.124 = (f32[3,64]{1,0:T(4,128)}, f32[128,128]{1,0:T(8,128)S(1)}) custom-call(s32[1]{0:T(128)} %bitcast.5.place_ref, f32[40,128]{1,0:T(8,128)S(1)} %shard_map.123.own_ref, f32[40,128]{1,0:T(8,128)S(1)} %collective-permute-done.even_ref, f32[40,128]{1,0:T(8,128)S(1)} %collective-permute-done.1.odd_ref, f32[640,128]{1,0:T(8,128)S(1)} %bitcast.15), custom_call_target="tpu_custom_call" | custom-call | tf_op jit(solution)/shard_map/pallas_call | solution.py:381
  80.7 24.5 %all_to_all.17 = f32[128,1,128]{2,1,0:T(1,128)S(1)} all-to-all(f32[128,1,128]{2,1,0:T(1,128)S(1)} %bitcast.23), channel_id=1, replica_groups=mesh['src'=128,'seg'=4] {'src'}, dimensions={0} | all-to-all | bytes 131072 | tf_op jit(solution)/shard_map/all_to_all | solution.py:445
  105.2 0.6 subtract_bitcast_fusion
  (4 shorter events, 0.0 us)
Async XLA Ops:
  5.1 12.5 %copy-start = (f32[5,16384]{1,0:T(8,128)S(1)}, f32[5,16384]{1,0:T(8,128)}, u32[]{:S(2)}) copy-start(f32[5,16384]{1,0:T(8,128)} %part_ref.3) | copy-start | bytes 983044
  5.1 12.5 %copy-start.1 = (f32[3,16384]{1,0:T(4,128)S(1)}, f32[3,16384]{1,0:T(4,128)}, u32[]{:S(2)}) copy-start(f32[3,16384]{1,0:T(4,128)} %dir_ref.1) | copy-start | bytes 589828
  5.1 12.5 %copy-start.2 = (f32[16384]{0:T(1024)S(1)}, f32[16384]{0:T(1024)}, u32[]{:S(2)}) copy-start(f32[16384]{0:T(1024)} %param.10) | copy-start | bytes 196612
  5.1 12.5 %copy-start.3 = (s32[16384]{0:T(1024)S(1)}, s32[16384]{0:T(1024)}, u32[]{:S(2)}) copy-start(s32[16384]{0:T(1024)} %param.17) | copy-start | bytes 196612
  5.1 12.5 %copy-start.4 = (f32[5,2048]{1,0:T(8,128)S(1)}, f32[5,2048]{1,0:T(8,128)}, u32[]{:S(2)}) copy-start(f32[5,2048]{1,0:T(8,128)} %prior_ref.2) | copy-start | bytes 122884
  5.1 12.5 %copy-start.5 = (f32[16384]{0:T(1024)S(1)}, f32[16384]{0:T(1024)}, u32[]{:S(2)}) copy-start(f32[16384]{0:T(1024)} %param.12) | copy-start | bytes 196612
  5.2 12.4 %copy-start.6 = (s32[16384]{0:T(1024)S(1)}, s32[16384]{0:T(1024)}, u32[]{:S(2)}) copy-start(s32[16384]{0:T(1024)} %param.18) | copy-start | bytes 196612
  20.0 48.4 %copy-start.7 = (f32[3,64]{1,0:T(4,128)S(1)}, f32[3,64]{1,0:T(4,128)}, u32[]{:S(2)}) copy-start(f32[3,64]{1,0:T(4,128)} %prior_ref.3) | copy-start | bytes 2308
  70.9 6.7 %collective-permute-start = (f32[40,128]{1,0:T(8,128)S(1)}, f32[40,128]{1,0:T(8,128)S(1)}, u32[]{:S(2)}, u32[]{:S(2)}) collective-permute-start(f32[40,128]{1,0:T(8,128)S(1)} %shard_map.123.own_ref), channel_id=1, source_target_pairs={{0,1},{2,3},{4,5},{6,7},{8,9},{10,11},{12,13},{14,15},{16,17},{18,... | collective-permute-start | bytes 61448 | tf_op jit(solution)/shard_map/ppermute | solution.py:434
  73.1 6.3 %collective-permute-start.1 = (f32[40,128]{1,0:T(8,128)S(1)}, f32[40,128]{1,0:T(8,128)S(1)}, u32[]{:S(2)}, u32[]{:S(2)}) collective-permute-start(f32[40,128]{1,0:T(8,128)S(1)} %shard_map.123.own_ref), channel_id=1, source_target_pairs={{1,2},{3,4},{5,6},{7,8},{9,10},{11,12},{13,14},{15,16},{17,18},{19... | collective-permute-start | bytes 61448 | tf_op jit(solution)/shard_map/ppermute | solution.py:434

commit v5 on v4

--- a/solution.py
+++ b/solution.py
@@ -51,13 +51,32 @@
     return jnp.concatenate([jnp.where(ids[16 * n : 16 * n + 16] == wide, one, zero) for n in range(count)], 0)
 
 
-def source_sums_kernel(
-    count_ref, res_ref, weight_ref, part_ref, src_ref, out_ref, live_ref, acc_ref, rows_refs, feat_refs
-):
+def slot_pack_kernel(count_ref, weight_ref, frac_ref, interval_ref, dir_ref, pack_ref, live_ref, root_ref):
+    lane8 = lax.broadcasted_iota(jnp.int32, (8, 128), 1)
+    sub8 = lax.broadcasted_iota(jnp.int32, (8, 128), 0)
+
+    def group(g, carry):
+        first = pl.multiple_of(g * 8, 8)
+        count8 = jnp.zeros((8, 128), jnp.int32)
+        for k in range(8):
+            count8 = jnp.where(sub8 == k, count_ref[0, g * 8 + k], count8)
+        live8 = jnp.where(lane8 < count8, weight_ref[pl.ds(first, 8), :], 0.0)
+        root8 = jnp.sqrt(live8)
+        live_ref[pl.ds(first, 8), :] = live8
+        root_ref[pl.ds(first, 8), :] = root8
+        time8 = (interval_ref[pl.ds(first, 8), :] & 63).astype(jnp.float32) + frac_ref[pl.ds(first, 8), :]
+        pack = pack_ref.at[pl.ds(pl.multiple_of(g * 32, 8), 32), :]
+        for k in range(8):
+            at = pl.multiple_of((g * 8 + k) * 128, 128)
+            pack[k * 4 : k * 4 + 4, :] = jnp.concatenate([time8[k : k + 1], root8[k : k + 1] * dir_ref[:, pl.ds(at, 128)]], 0)
+        return carry
+
+    lax.fori_loop(0, 16, group, 0, unroll=4)
+
+
+def source_sums_kernel(live_ref, res_ref, part_ref, src_ref, out_ref, acc_ref, rows_refs, feat_refs):
     acc_ref[...] = jnp.zeros_like(acc_ref)
     ids = lax.broadcasted_iota(jnp.int32, (256, 128), 0).astype(jnp.float32).astype(jnp.bfloat16)
-    lane8 = lax.broadcasted_iota(jnp.int32, (8, 128), 1)
-    sub8 = lax.broadcasted_iota(jnp.int32, (8, 128), 0)
     sub16 = lax.broadcasted_iota(jnp.int32, (16, 128), 0)
     zero = jnp.zeros((16, 128), jnp.bfloat16)
 
@@ -67,12 +86,9 @@
         src8 = src_ref[pl.ds(first, 8), :]
         low8 = (src8 & 255).astype(jnp.float32)
         high8 = (src8 >> 8).astype(jnp.float32)
-        count8 = jnp.zeros((8, 128), jnp.int32)
-        for k in range(8):
-            count8 = jnp.where(sub8 == k, count_ref[0, g * 8 + k], count8)
+        for k in range(8):
             rows_ref[pl.ds(k, 5, stride=8), :] = part_ref[:, pl.ds(pl.multiple_of((g * 8 + k) * 128, 128), 128)]
-        weight8 = jnp.where(lane8 < count8, weight_ref[pl.ds(first, 8), :], 0.0)
-        live_ref[pl.ds(first, 8), :] = weight8
+        weight8 = live_ref[pl.ds(first, 8), :]
         part8 = [rows_ref[p * 8 : p * 8 + 8, :] for p in range(5)]
         weighted = [weight8 * p for p in part8]
         features = [weighted[i] * part8[j] for i, j in param_pairs] + [weighted[i] * res8 for i in range(5)]
@@ -115,8 +131,7 @@
     for f in range(20):
         for h in range(2):
             total = jnp.concatenate([rows_of(f, e, h) + rows_of(20 + f, e, h) for e in range(2)], 0)
-            for q in range(4):
-                out_ref[q, (h * 20 + f) * 8 : (h * 20 + f) * 8 + 8, :] = total
+            out_ref[(h * 20 + f) * 8 : (h * 20 + f) * 8 + 8, :] = total
 
 
 HIGH_ORDER = (0, 2, 4, 6, 1, 3, 5, 7)
@@ -155,8 +170,8 @@
 
 
 def source_solve_kernel(
-    sums_ref, prior_ref, res_ref, live_ref, part_ref, src_ref, frac_ref, interval_ref, dir_ref,
-    update_far, pack_ref, base_ref, scale_ref, update_ref, root_ref, corr_ref, sem,
+    after_ref, sums_0, sums_1, sums_2, sums_3, prior_ref, res_ref, root_ref, part_ref, src_ref,
+    update_far, first_ref, base_ref, scale_ref, update_ref, corr_ref, sem,
 ):
     tables = []
     for h in range(2):
@@ -164,8 +179,8 @@
         for f in range(20):
             at = (h * 20 + f) * 8
             terms.append(
-                (sums_ref[0, at : at + 8, :] + sums_ref[1, at : at + 8, :])
-                + (sums_ref[2, at : at + 8, :] + sums_ref[3, at : at + 8, :])
+                (sums_0[at : at + 8, :] + sums_1[at : at + 8, :])
+                + (sums_2[at : at + 8, :] + sums_3[at : at + 8, :])
             )
         for number, (i, j) in enumerate(param_pairs):
             if i == j:
@@ -178,19 +193,14 @@
                 update_ref[p : p + 1, (2 * r + h) * 128 : (2 * r + h + 1) * 128] = solved[p][n : n + 1]
     update_copy = pltpu.make_async_copy(update_ref, update_far, sem)
     update_copy.start()
-    root_ref[...] = jnp.sqrt(live_ref[...])
     sub8 = lax.broadcasted_iota(jnp.int32, (8, 128), 0)
 
     def group(g, carry):
         first = pl.multiple_of(g * 8, 8)
-        res8 = res_ref[pl.ds(first, 8), :]
         src8 = src_ref[pl.ds(first, 8), :]
-        root8 = root_ref[pl.ds(first, 8), :]
-        time8 = (interval_ref[pl.ds(first, 8), :] & 63).astype(jnp.float32) + frac_ref[pl.ds(first, 8), :]
         low8 = src8 & 127
         high8 = src8 >> 8
         place8 = (high8 >> 1) + ((high8 & 1) << 2) + (((src8 >> 7) & 1) << 3)
-        pack = pack_ref.at[pl.ds(pl.multiple_of(g * 40, 8), 40), :]
         corr_rows = []
         for k in range(8):
             at = pl.multiple_of((g * 8 + k) * 128, 128)
@@ -207,26 +217,25 @@
                     found = term if found is None else found + term
             corr = jnp.sum(found, 0, keepdims=True)
             corr_rows.append(corr)
-            root = root8[k : k + 1]
-            first_pass = root * (res8[k : k + 1] - corr)
-            pack[k * 5 : k * 5 + 5, :] = jnp.concatenate([time8[k : k + 1], root * dir_ref[:, pl.ds(at, 128)], first_pass], 0)
         corr_ref[pl.ds(first, 8), :] = jnp.concatenate(corr_rows, 0)
         return carry
 
     lax.fori_loop(0, 16, group, 0, unroll=4)
     live = root_ref[...] > 0.0
     base_ref[...] = res_ref[...] - jnp.where(live, corr_ref[...], 0.0)
+    first_ref[...] = root_ref[...] * (res_ref[...] - corr_ref[...])
     scale_ref[...] = jnp.where(live, 1.0 / jnp.where(live, root_ref[...], 1.0), 0.0)
     update_copy.wait()
 
 
-def band_sums_kernel(slots_ref, prior_ref, frame_ref, feat_refs, a_refs, acc_ref, prior_pad):
+def band_sums_kernel(slots_ref, first_ref, prior_ref, frame_ref, feat_refs, a_refs, acc_ref, prior_pad):
     acc_ref[...] = jnp.zeros_like(acc_ref)
     ids = lax.broadcasted_iota(jnp.int32, (128, 128), 0).astype(jnp.float32).astype(jnp.bfloat16)
 
     def group(g, a_ref, feat_ref):
-        slots = slots_ref.at[pl.ds(pl.multiple_of(g * 40, 8), 40), :]
-        time8, d0, d1, d2, fp = [slots[pl.ds(k, 8, stride=5), :] for k in range(5)]
+        slots = slots_ref.at[pl.ds(pl.multiple_of(g * 32, 8), 32), :]
+        time8, d0, d1, d2 = [slots[pl.ds(k, 8, stride=4), :] for k in range(4)]
+        fp = first_ref[pl.ds(pl.multiple_of(g * 8, 8), 8), :]
         direction = [d0, d1, d2]
         floor8 = jnp.floor(time8)
         _, splines = spline_weights(time8)
@@ -347,8 +356,8 @@
     tables = [jnp.broadcast_to(att[j : j + 1], (8, 128)) for j in range(3)]
 
     def group(g, carry):
-        slots = slots_ref.at[pl.ds(pl.multiple_of(g * 40, 8), 40), :]
-        time8, d0, d1, d2 = [slots[pl.ds(k, 8, stride=5), :] for k in range(4)]
+        slots = slots_ref.at[pl.ds(pl.multiple_of(g * 32, 8), 32), :]
+        time8, d0, d1, d2 = [slots[pl.ds(k, 8, stride=4), :] for k in range(4)]
         direction = [d0, d1, d2]
         floor8, splines = spline_weights(time8)
         total = jnp.zeros((8, 128), jnp.float32)
@@ -366,8 +375,8 @@
     att_copy.wait()
 
 
-def call(kernel, outs, n_in, smem_at=(), scratch=(), far_in=(), far_out=()):
-    shapes = [jax.ShapeDtypeStruct(s, jnp.float32) if i in far_out else pltpu.VMEM(s, jnp.float32) for i, s in enumerate(outs)]
+def call(kernel, outs, n_in, smem_at=(), scratch=(), far_in=(), far_out=(), plain_out=()):
+    shapes = [jax.ShapeDtypeStruct(s, jnp.float32) if i in far_out or i in plain_out else pltpu.VMEM(s, jnp.float32) for i, s in enumerate(outs)]
     run = pl.pallas_call(
         kernel,
         out_shape=shapes,
@@ -387,38 +396,39 @@
     devices = lax.axis_size("src") * lax.axis_size("seg")
     square = lambda a: a.reshape(128, 128)
     res, weight, frac, src, interval = map(square, (residual, obs_weight, time_frac, obs_source, obs_interval))
-    sums, live = call(
+    pack, live, root = call(
+        slot_pack_kernel, [(512, 128), (128, 128), (128, 128)], 5, (0,), (), range(1, 5), (), (0,)
+    )(obs_count, weight, frac, interval, att_dir)
+    packed = lax.all_to_all(pack.reshape(128, 1, 512), "src", split_axis=0, concat_axis=0, tiled=True)
+    (sums,) = call(
         source_sums_kernel,
-        [(4, 320, 128), (128, 128)],
-        5,
-        (0,),
+        [(320, 128)],
+        4,
+        (),
         [
             pltpu.VMEM((2, 320, 128), jnp.float32),
             pltpu.VMEM((SUMS_UNROLL, 40, 128), jnp.float32),
             pltpu.VMEM((SUMS_UNROLL, 320, 128), jnp.float32),
         ],
-        range(1, 5),
-    )(obs_count, res, weight, src_partials, src)
-    gathered = lax.all_to_all(sums, "seg", split_axis=0, concat_axis=0, tiled=True)
-    src_update, packed, base, scale = call(
+        range(1, 4),
+    )(live, res, src_partials, src)
+    arrived = packed.reshape(512, 128)
+    segs = lax.axis_size("seg")
+    others = [lax.ppermute(sums, "seg", [(i, (i + k) % segs) for i in range(segs)]) for k in (2, 1, 3)]
+    src_update, first_pass, base, scale = call(
         source_solve_kernel,
-        [(5, 2048), (640, 128), (128, 128), (128, 128)],
-        9,
+        [(5, 2048), (128, 128), (128, 128), (128, 128)],
+        10,
         (),
-        [
-            pltpu.VMEM((5, 2048), jnp.float32),
-            pltpu.VMEM((128, 128), jnp.float32),
-            pltpu.VMEM((128, 128), jnp.float32),
-            pltpu.SemaphoreType.DMA,
-        ],
+        [pltpu.VMEM((5, 2048), jnp.float32), pltpu.VMEM((128, 128), jnp.float32), pltpu.SemaphoreType.DMA],
         (),
         (0,),
-    )(gathered, src_prior, res, live, src_partials, src, frac, interval, att_dir)
-    arrived = lax.all_to_all(packed.reshape(128, 1, 640), "src", split_axis=0, concat_axis=0, tiled=True).reshape(640, 128)
+    )(arrived, sums, *others, src_prior, res, root, src_partials, src)
+    arrived_first = lax.all_to_all(first_pass.reshape(128, 1, 128), "src", split_axis=0, concat_axis=0, tiled=True).reshape(128, 128)
     (frame,) = call(
         band_sums_kernel,
         [(40, 128)],
-        2,
+        3,
         (),
         [
             pltpu.VMEM((BAND_UNROLL, 576, 128), jnp.float32),
@@ -426,7 +436,7 @@
             pltpu.VMEM((144, 128), jnp.float32),
             pltpu.VMEM((8, 128), jnp.float32),
         ],
-    )(arrived, att_prior)
+    )(arrived, arrived_first, att_prior)
     both = ("src", "seg")
     swaps = {}
     for start in (1, 0):

time: 106 us -> 113 us (1.066)
  blocking collectives: 85.3 us -> 50.1 us
  starting transfers between devices: 6.63 us -> 40.2 us
  waiting for transfers between devices: 1.85 us -> 8.2 us
  Pallas kernels: 10.6 us -> 12.6 us
    all_to_all x2 -> x1, blocking collectives: 60.8 us -> 28.3 us  [body(): lax.all_to_all(first_pass.reshape(128, 1, 128), 'src', split_axis=0, conc...]
    all_to_all x0 -> x1, starting transfers between devices: none -> 20.6 us  [body(): lax.all_to_all(pack.reshape(128, 1, 512), 'src', split_axis=0, concat_axi...]
    ppermute x0 -> x3, starting transfers between devices: none -> 11.1 us  [body(): lax.ppermute(sums, 'seg', [(i, (i + k) % segs) for i in range(segs)])]
    all_to_all x0 -> x1, waiting for transfers between devices: none -> 4.53 us  [body(): lax.all_to_all(pack.reshape(128, 1, 512), 'src', split_axis=0, concat_axi...]
    all_to_all x1, blocking collectives: 24.5 us -> 21.8 us  [body(): lax.all_to_all(correction.reshape(128, 1, 128), 'src', split_axis=0, conc...]
    ppermute x0 -> x3, waiting for transfers between devices: none -> 2.23 us  [body(): lax.ppermute(sums, 'seg', [(i, (i + k) % segs) for i in range(segs)])]
    pallas_call x4 -> x5, Pallas kernels: 10.6 us -> 12.6 us  [on_chip(): return run(*near)]
    ppermute x2, starting transfers between devices: 6.63 us -> 8.54 us  [body(): swaps[start] = lax.ppermute(frame, both, pairs + [(b, a) for a, b in pairs])]
  transfers between devices with their start and end apart: 2 -> 6, of which waited for: 1 -> 4; matrix products, arithmetic and copies ran while one was open for 0% -> 0% of each run, Pallas kernels for 0% -> 4%
where the time goes in v5:
time: 113 us
  blocking collectives  50.1 us (44%)
  starting transfers between devices  40.2 us (36%)
  Pallas kernels  12.6 us (11%)
  waiting for transfers between devices  8.2 us (7%)
    all_to_all x1, blocking collectives, body(): lax.all_to_all(first_pass.reshape(128, 1, 128), 'src', split_axis=0, conc...  28.3 us
    all_to_all x1, blocking collectives, body(): lax.all_to_all(correction.reshape(128, 1, 128), 'src', split_axis=0, conc...  21.8 us
    all_to_all x1, starting transfers between devices, body(): lax.all_to_all(pack.reshape(128, 1, 512), 'src', split_axis=0, concat_axi...  20.6 us
    pallas_call x5, Pallas kernels, on_chip(): return run(*near)  12.6 us
    ppermute x3, starting transfers between devices, body(): lax.ppermute(sums, 'seg', [(i, (i + k) % segs) for i in range(segs)])  11.1 us
    ppermute x2, starting transfers between devices, body(): swaps[start] = lax.ppermute(frame, both, pairs + [(b, a) for a, b in pairs])  8.54 us
    all_to_all x1, waiting for transfers between devices, body(): lax.all_to_all(pack.reshape(128, 1, 512), 'src', split_axis=0, concat_axi...  4.53 us
  transfers between devices with their start and end apart: 6, of which 4 were waited for; matrix products, arithmetic and copies ran while one was open for 0% of the time, Pallas kernels for 4%

profile of v5, /device:TPU:1, one launch (start us, length us, event | category | flops | bytes accessed | tf_op | source)
XLA Modules:
  0.0 112.6 jit_solution(6907648312983682367)
XLA Ops:
  0.6 2.0 %shard_map.121 = (f32[512,128]{1,0:T(8,128)}, f32[128,128]{1,0:T(8,128)S(1)}, f32[128,128]{1,0:T(8,128)S(1)}) custom-call(s32[1,128]{1,0:T(1,128)} %count_ref.1, f32[128,128]{1,0:T(8,128)} %bitcast.30, f32[128,128]{1,0:T(8,128)} %bitcast.31, s32[128,128]{1,0:T(8,128)} %bitcast.32, f32[3,16384]{1,0:T(4,128)} %dir_ref.1), custom_call_target="tpu_custom_call" | custom-call | tf_op jit(solution)/shard_map/pallas_call | solution.py:390
  2.7 20.6 %all-to-all-start = ((f32[128,1,512]{2,1,0:T(1,128)}), f32[128,1,512]{2,1,0:T(1,128)S(1)}, u32[]{:S(2)}, u32[]{:S(2)}) async-start(f32[128,1,512]{2,1,0:T(1,128)} %bitcast.28), calls=%async_computation | async-start | bytes 524288 | tf_op jit(solution)/shard_map/all_to_all | solution.py:402
  23.2 0.0 copy-start
  23.3 0.0 copy-start.1
  23.3 0.0 copy-start.2
  23.3 0.0 copy-start.3
  23.3 4.4 %shard_map.122.sums_0 = f32[320,128]{1,0:T(8,128)S(1)} custom-call(f32[128,128]{1,0:T(8,128)S(1)} %get-tuple-element.13.live_ref, f32[128,128]{1,0:T(8,128)} %bitcast.22, f32[5,16384]{1,0:T(8,128)} %part_ref.3, s32[128,128]{1,0:T(8,128)} %bitcast.24), custom_call_target="tpu_custom_call" | custom-call | tf_op jit(solution)/shard_map/pallas_call | solution.py:390
  27.7 4.6 %collective-permute-start = (f32[320,128]{1,0:T(8,128)S(1)}, f32[320,128]{1,0:T(8,128)S(1)}, u32[]{:S(2)}, u32[]{:S(2)}) collective-permute-start(f32[320,128]{1,0:T(8,128)S(1)} %shard_map.122.sums_0), channel_id=1, source_target_pairs={{0,2},{1,3},{2,0},{3,1},{4,6},{5,7},{6,4},{7,5},{8,10},{9,11},{10,... | collective-permute-start | bytes 491528 | tf_op jit(solution)/shard_map/ppermute | solution.py:417
  32.4 2.2 %collective-permute-start.1 = (f32[320,128]{1,0:T(8,128)S(1)}, f32[320,128]{1,0:T(8,128)S(1)}, u32[]{:S(2)}, u32[]{:S(2)}) collective-permute-start(f32[320,128]{1,0:T(8,128)S(1)} %shard_map.122.sums_0), channel_id=1, source_target_pairs={{0,1},{1,2},{2,3},{3,0},{4,5},{5,6},{6,7},{7,4},{8,9},{9,10},{10,1... | collective-permute-start | bytes 491528 | tf_op jit(solution)/shard_map/ppermute | solution.py:417
  34.6 4.3 %collective-permute-start.2 = (f32[320,128]{1,0:T(8,128)S(1)}, f32[320,128]{1,0:T(8,128)S(1)}, u32[]{:S(2)}, u32[]{:S(2)}) collective-permute-start(f32[320,128]{1,0:T(8,128)S(1)} %shard_map.122.sums_0), channel_id=1, source_target_pairs={{0,3},{1,0},{2,1},{3,2},{4,7},{5,4},{6,5},{7,6},{8,11},{9,8},{10,9... | collective-permute-start | bytes 491528 | tf_op jit(solution)/shard_map/ppermute | solution.py:417
  38.9 0.0 collective-permute-done.sums_1
  38.9 1.2 %collective-permute-done.1.sums_2 = f32[320,128]{1,0:T(8,128)S(1)} collective-permute-done((f32[320,128]{1,0:T(8,128)S(1)}, f32[320,128]{1,0:T(8,128)S(1)}, u32[]{:S(2)}, u32[]{:S(2)}) %collective-permute-start.1) | collective-permute-done | bytes 163872 | tf_op jit(solution)/shard_map/ppermute | solution.py:417
  40.0 1.1 collective-permute-done.2.sums_3
  41.1 4.5 %all-to-all-done = f32[128,1,512]{2,1,0:T(1,128)S(1)} async-done(((f32[128,1,512]{2,1,0:T(1,128)}), f32[128,1,512]{2,1,0:T(1,128)S(1)}, u32[]{:S(2)}, u32[]{:S(2)}) %all-to-all-start) | async-done | bytes 262176 | tf_op jit(solution)/shard_map/all_to_all | solution.py:402
  45.7 2.4 %shard_map.123 = (f32[5,2048]{1,0:T(8,128)}, f32[128,128]{1,0:T(8,128)S(1)}, f32[128,128]{1,0:T(8,128)S(1)}, f32[128,128]{1,0:T(8,128)S(1)}) custom-call(f32[512,128]{1,0:T(8,128)S(1)} %bitcast.18, f32[320,128]{1,0:T(8,128)S(1)} %shard_map.122.sums_0, f32[320,128]{1,0:T(8,128)S(1)} %collective-permute-done.sums_1, ...), custom_call_target="tpu_custom_call" | custom-call | tf_op jit(solution)/shard_map/pallas_call | solution.py:390
  48.0 0.0 copy-start.4
  48.0 28.3 %all_to_all.15 = f32[128,1,128]{2,1,0:T(1,128)S(1)} all-to-all(f32[128,1,128]{2,1,0:T(1,128)S(1)} %bitcast.26), channel_id=1, replica_groups=mesh['src'=128,'seg'=4] {'src'}, dimensions={0} | all-to-all | bytes 131072 | tf_op jit(solution)/shard_map/all_to_all | solution.py:427
  76.3 2.4 %shard_map.124.own_ref = f32[40,128]{1,0:T(8,128)S(1)} custom-call(f32[512,128]{1,0:T(8,128)S(1)} %bitcast.19, f32[128,128]{1,0:T(8,128)S(1)} %bitcast.21, f32[3,64]{1,0:T(4,128)S(1)} %copy-done.4), custom_call_target="tpu_custom_call" | custom-call | tf_op jit(solution)/shard_map/pallas_call | solution.py:390
  78.8 1.9 %collective-permute-start.3 = (f32[40,128]{1,0:T(8,128)S(1)}, f32[40,128]{1,0:T(8,128)S(1)}, u32[]{:S(2)}, u32[]{:S(2)}) collective-permute-start(f32[40,128]{1,0:T(8,128)S(1)} %shard_map.124.own_ref), channel_id=1, source_target_pairs={{0,1},{2,3},{4,5},{6,7},{8,9},{10,11},{12,13},{14,15},{16,17},{18,... | collective-permute-start | bytes 61448 | tf_op jit(solution)/shard_map/ppermute | solution.py:444
  80.7 6.6 %collective-permute-start.4 = (f32[40,128]{1,0:T(8,128)S(1)}, f32[40,128]{1,0:T(8,128)S(1)}, u32[]{:S(2)}, u32[]{:S(2)}) collective-permute-start(f32[40,128]{1,0:T(8,128)S(1)} %shard_map.124.own_ref), channel_id=1, source_target_pairs={{1,2},{3,4},{5,6},{7,8},{9,10},{11,12},{13,14},{15,16},{17,18},{19... | collective-permute-start | bytes 61448 | tf_op jit(solution)/shard_map/ppermute | solution.py:444
  87.3 1.4 %collective-permute-done.4.odd_ref = f32[40,128]{1,0:T(8,128)S(1)} collective-permute-done((f32[40,128]{1,0:T(8,128)S(1)}, f32[40,128]{1,0:T(8,128)S(1)}, u32[]{:S(2)}, u32[]{:S(2)}) %collective-permute-start.4) | collective-permute-done | bytes 20512 | tf_op jit(solution)/shard_map/ppermute | solution.py:444
  88.8 1.3 %shard_map.125 = (f32[3,64]{1,0:T(4,128)}, f32[128,128]{1,0:T(8,128)S(1)}) custom-call(s32[1]{0:T(128)} %bitcast.7.place_ref, f32[40,128]{1,0:T(8,128)S(1)} %shard_map.124.own_ref, f32[40,128]{1,0:T(8,128)S(1)} %collective-permute-done.3.even_ref, f32[40,128]{1,0:T(8,128)S(1)} %collective-permute-done.4.odd_ref, f32[512,128]{1,0:T(8,128)S(1)} %bitcast.20), custom_call_target="tpu_custom_call" | custom-call | tf_op jit(solution)/shard_map/pallas_call | solution.py:390
  90.1 21.8 %all_to_all.16 = f32[128,1,128]{2,1,0:T(1,128)S(1)} all-to-all(f32[128,1,128]{2,1,0:T(1,128)S(1)} %bitcast.27), channel_id=1, replica_groups=mesh['src'=128,'seg'=4] {'src'}, dimensions={0} | all-to-all | bytes 131072 | tf_op jit(solution)/shard_map/all_to_all | solution.py:455
  111.9 0.6 subtract_bitcast_fusion
  (6 shorter events, 0.0 us)
Async XLA Ops:
  2.7 43.0 %all-to-all-start = ((f32[128,1,512]{2,1,0:T(1,128)}), f32[128,1,512]{2,1,0:T(1,128)S(1)}, u32[]{:S(2)}, u32[]{:S(2)}) async-start(f32[128,1,512]{2,1,0:T(1,128)} %bitcast.28), calls=%async_computation | async-start | bytes 524288 | tf_op jit(solution)/shard_map/all_to_all | solution.py:402
  23.2 22.4 %copy-start = (f32[5,16384]{1,0:T(8,128)S(1)}, f32[5,16384]{1,0:T(8,128)}, u32[]{:S(2)}) copy-start(f32[5,16384]{1,0:T(8,128)} %part_ref.3) | copy-start | bytes 983044
  23.3 22.4 %copy-start.1 = (f32[16384]{0:T(1024)S(1)}, f32[16384]{0:T(1024)}, u32[]{:S(2)}) copy-start(f32[16384]{0:T(1024)} %param.10) | copy-start | bytes 196612
  23.3 22.4 %copy-start.2 = (s32[16384]{0:T(1024)S(1)}, s32[16384]{0:T(1024)}, u32[]{:S(2)}) copy-start(s32[16384]{0:T(1024)} %param.17) | copy-start | bytes 196612
  23.3 22.4 %copy-start.3 = (f32[5,2048]{1,0:T(8,128)S(1)}, f32[5,2048]{1,0:T(8,128)}, u32[]{:S(2)}) copy-start(f32[5,2048]{1,0:T(8,128)} %prior_ref.2) | copy-start | bytes 122884
  27.7 11.2 %collective-permute-start = (f32[320,128]{1,0:T(8,128)S(1)}, f32[320,128]{1,0:T(8,128)S(1)}, u32[]{:S(2)}, u32[]{:S(2)}) collective-permute-start(f32[320,128]{1,0:T(8,128)S(1)} %shard_map.122.sums_0), channel_id=1, source_target_pairs={{0,2},{1,3},{2,0},{3,1},{4,6},{5,7},{6,4},{7,5},{8,10},{9,11},{10,... | collective-permute-start | bytes 491528 | tf_op jit(solution)/shard_map/ppermute | solution.py:417
  32.4 7.7 %collective-permute-start.1 = (f32[320,128]{1,0:T(8,128)S(1)}, f32[320,128]{1,0:T(8,128)S(1)}, u32[]{:S(2)}, u32[]{:S(2)}) collective-permute-start(f32[320,128]{1,0:T(8,128)S(1)} %shard_map.122.sums_0), channel_id=1, source_target_pairs={{0,1},{1,2},{2,3},{3,0},{4,5},{5,6},{6,7},{7,4},{8,9},{9,10},{10,1... | collective-permute-start | bytes 491528 | tf_op jit(solution)/shard_map/ppermute | solution.py:417
  34.6 6.5 %collective-permute-start.2 = (f32[320,128]{1,0:T(8,128)S(1)}, f32[320,128]{1,0:T(8,128)S(1)}, u32[]{:S(2)}, u32[]{:S(2)}) collective-permute-start(f32[320,128]{1,0:T(8,128)S(1)} %shard_map.122.sums_0), channel_id=1, source_target_pairs={{0,3},{1,0},{2,1},{3,2},{4,7},{5,4},{6,5},{7,6},{8,11},{9,8},{10,9... | collective-permute-start | bytes 491528 | tf_op jit(solution)/shard_map/ppermute | solution.py:417
  48.0 28.3 %copy-start.4 = (f32[3,64]{1,0:T(4,128)S(1)}, f32[3,64]{1,0:T(4,128)}, u32[]{:S(2)}) copy-start(f32[3,64]{1,0:T(4,128)} %prior_ref.3) | copy-start | bytes 2308
  78.8 8.6 %collective-permute-start.3 = (f32[40,128]{1,0:T(8,128)S(1)}, f32[40,128]{1,0:T(8,128)S(1)}, u32[]{:S(2)}, u32[]{:S(2)}) collective-permute-start(f32[40,128]{1,0:T(8,128)S(1)} %shard_map.124.own_ref), channel_id=1, source_target_pairs={{0,1},{2,3},{4,5},{6,7},{8,9},{10,11},{12,13},{14,15},{16,17},{18,... | collective-permute-start | bytes 61448 | tf_op jit(solution)/shard_map/ppermute | solution.py:444
  80.7 8.1 %collective-permute-start.4 = (f32[40,128]{1,0:T(8,128)S(1)}, f32[40,128]{1,0:T(8,128)S(1)}, u32[]{:S(2)}, u32[]{:S(2)}) collective-permute-start(f32[40,128]{1,0:T(8,128)S(1)} %shard_map.124.own_ref), channel_id=1, source_target_pairs={{1,2},{3,4},{5,6},{7,8},{9,10},{11,12},{13,14},{15,16},{17,18},{19... | collective-permute-start | bytes 61448 | tf_op jit(solution)/shard_map/ppermute | solution.py:444

commit v6 on v4

--- a/solution.py
+++ b/solution.py
@@ -154,6 +154,23 @@
     return backward
 
 
+def row_sums(tiles):
+    sub = lax.broadcasted_iota(jnp.int32, (8, 128), 0)
+    for width in (4, 2, 1):
+        mask = (sub & width) == 0
+        half = len(tiles) // 2
+        folded = []
+        for x, y in zip(tiles[:half], tiles[half:]):
+            other = jnp.where(mask, y, x)
+            if width == 4:
+                moved = pltpu.roll(other, 4, 0)
+            else:
+                moved = jnp.where(mask, pltpu.roll(other, 8 - width, 0), pltpu.roll(other, width, 0))
+            folded.append(jnp.where(mask, x, y) + moved)
+        tiles = folded
+    return tiles[0]
+
+
 def source_solve_kernel(
     sums_ref, prior_ref, res_ref, live_ref, part_ref, src_ref, frac_ref, interval_ref, dir_ref,
     update_far, pack_ref, base_ref, scale_ref, update_ref, root_ref, corr_ref, sem,
@@ -191,7 +208,7 @@
         high8 = src8 >> 8
         place8 = (high8 >> 1) + ((high8 & 1) << 2) + (((src8 >> 7) & 1) << 3)
         pack = pack_ref.at[pl.ds(pl.multiple_of(g * 40, 8), 40), :]
-        corr_rows = []
+        tiles = []
         for k in range(8):
             at = pl.multiple_of((g * 8 + k) * 128, 128)
             low = jnp.broadcast_to(low8[k : k + 1], (8, 128))
@@ -200,20 +217,19 @@
             found = None
             masks = [place == sub8, place == sub8 + 8]
             for p in range(5):
-                wide = jnp.broadcast_to(part[p : p + 1], (8, 128))
-                for h in range(2):
-                    taken = jnp.take_along_axis(tables[h][p], low, axis=1, mode="promise_in_bounds")
-                    term = jnp.where(masks[h], taken * wide, 0.0)
-                    found = term if found is None else found + term
-            corr = jnp.sum(found, 0, keepdims=True)
-            corr_rows.append(corr)
-            root = root8[k : k + 1]
-            first_pass = root * (res8[k : k + 1] - corr)
-            pack[k * 5 : k * 5 + 5, :] = jnp.concatenate([time8[k : k + 1], root * dir_ref[:, pl.ds(at, 128)], first_pass], 0)
-        corr_ref[pl.ds(first, 8), :] = jnp.concatenate(corr_rows, 0)
+                taken = [jnp.take_along_axis(tables[h][p], low, axis=1, mode="promise_in_bounds") for h in range(2)]
+                picked = jnp.where(masks[0], taken[0], jnp.where(masks[1], taken[1], 0.0))
+                term = picked * jnp.broadcast_to(part[p : p + 1], (8, 128))
+                found = term if found is None else found + term
+            tiles.append(found)
+            pack[k * 5 + 1 : k * 5 + 4, :] = root8[k : k + 1] * dir_ref[:, pl.ds(at, 128)]
+        corr8 = row_sums(tiles)
+        corr_ref[pl.ds(first, 8), :] = corr8
+        pack[pl.ds(0, 8, stride=5), :] = time8
+        pack[pl.ds(4, 8, stride=5), :] = root8 * (res8 - corr8)
         return carry
 
-    lax.fori_loop(0, 16, group, 0, unroll=4)
+    lax.fori_loop(0, 16, group, 0, unroll=8)
     live = root_ref[...] > 0.0
     base_ref[...] = res_ref[...] - jnp.where(live, corr_ref[...], 0.0)
     scale_ref[...] = jnp.where(live, 1.0 / jnp.where(live, root_ref[...], 1.0), 0.0)
@@ -362,7 +378,7 @@
         corr_ref[pl.ds(pl.multiple_of(g * 8, 8), 8), :] = total
         return carry
 
-    lax.fori_loop(0, 16, group, 0, unroll=4)
+    lax.fori_loop(0, 16, group, 0, unroll=8)
     att_copy.wait()
 
 

time: 106 us -> 106 us (level)
  no operation moved by 1% of the time
where the time goes in v6:
time: 106 us; the launch traced here: 105 us
  blocking collectives  85.3 us (80%)
  Pallas kernels  10.2 us (10%)
  starting transfers between devices  6.63 us (6%)
  waiting for transfers between devices  1.85 us (2%)
    all_to_all x1, blocking collectives, body(): lax.all_to_all(packed.reshape(128, 1, 640), 'src', split_axis=0, concat_a...  48.4 us
    all_to_all x1, blocking collectives, body(): lax.all_to_all(correction.reshape(128, 1, 128), 'src', split_axis=0, conc...  24.5 us
    all_to_all x1, blocking collectives, body(): lax.all_to_all(sums, 'seg', split_axis=0, concat_axis=0, tiled=True)  12.4 us
    pallas_call x4, Pallas kernels, on_chip(): return run(*near)  10.2 us
    ppermute x2, starting transfers between devices, body(): swaps[start] = lax.ppermute(frame, both, pairs + [(b, a) for a, b in pairs])  6.63 us
  transfers between devices with their start and end apart: 2, of which 1 were waited for; matrix products, arithmetic and copies ran while one was open for 0% of the time, Pallas kernels for 0%

profile of v6, /device:TPU:1, one launch (start us, length us, event | category | flops | bytes accessed | tf_op | source)
XLA Modules:
  0.0 105.5 jit_solution(2827436222060082222)
XLA Ops:
  0.6 4.4 %shard_map.121 = (f32[4,320,128]{2,1,0:T(8,128)S(1)}, f32[128,128]{1,0:T(8,128)S(1)}) custom-call(s32[1,128]{1,0:T(1,128)} %count_ref.1, f32[128,128]{1,0:T(8,128)} %bitcast.17, f32[128,128]{1,0:T(8,128)} %bitcast.25, f32[5,16384]{1,0:T(8,128)} %part_ref.3, s32[128,128]{1,0:T(8,128)} %bitcast.19), custom_call_target="tpu_custom_call" | custom-call | tf_op jit(solution)/shard_map/pallas_call | solution.py:397
  5.1 0.0 copy-start
  5.1 0.0 copy-start.1
  5.1 0.0 copy-start.2
  5.1 0.0 copy-start.3
  5.1 0.0 copy-start.4
  5.1 0.0 copy-start.5
  5.2 0.0 copy-start.6
  5.2 12.4 %all_to_all.15.sums_ref = f32[4,320,128]{2,1,0:T(8,128)S(1)} all-to-all(f32[4,320,128]{2,1,0:T(8,128)S(1)} %get-tuple-element.11), channel_id=1, replica_groups=mesh['src'=128,'seg'=4] {'seg'}, dimensions={0} | all-to-all | bytes 1310720 | tf_op jit(solution)/shard_map/all_to_all | solution.py:418
  17.6 0.0 copy-done
  17.6 0.0 copy-done.1
  17.6 0.0 copy-done.2
  17.6 0.0 copy-done.3
  17.6 2.1 %shard_map.122 = (f32[5,2048]{1,0:T(8,128)}, f32[640,128]{1,0:T(8,128)S(1)}, f32[128,128]{1,0:T(8,128)S(1)}, f32[128,128]{1,0:T(8,128)S(1)}) custom-call(f32[4,320,128]{2,1,0:T(8,128)S(1)} %all_to_all.15.sums_ref, f32[5,2048]{1,0:T(8,128)S(1)} %copy-done.4, f32[128,128]{1,0:T(8,128)S(1)} %bitcast.18, f32[128,128]{1,0:T(8,128)S(1)} %get-tuple-element.12.live_ref, ...), custom_call_target="tpu_custom_call" | custom-call | tf_op jit(solution)/shard_map/pallas_call | solution.py:397
  19.8 0.0 copy-start.7
  19.8 48.4 %all_to_all.16 = f32[128,1,640]{2,1,0:T(1,128)S(1)} all-to-all(f32[128,1,640]{2,1,0:T(1,128)S(1)} %bitcast.16), channel_id=1, replica_groups=mesh['src'=128,'seg'=4] {'src'}, dimensions={0} | all-to-all | bytes 655360 | tf_op jit(solution)/shard_map/all_to_all | solution.py:433
  68.2 2.4 %shard_map.123.own_ref = f32[40,128]{1,0:T(8,128)S(1)} custom-call(f32[640,128]{1,0:T(8,128)S(1)} %bitcast.14, f32[3,64]{1,0:T(4,128)S(1)} %copy-done.7), custom_call_target="tpu_custom_call" | custom-call | tf_op jit(solution)/shard_map/pallas_call | solution.py:397
  70.7 2.2 %collective-permute-start = (f32[40,128]{1,0:T(8,128)S(1)}, f32[40,128]{1,0:T(8,128)S(1)}, u32[]{:S(2)}, u32[]{:S(2)}) collective-permute-start(f32[40,128]{1,0:T(8,128)S(1)} %shard_map.123.own_ref), channel_id=1, source_target_pairs={{0,1},{2,3},{4,5},{6,7},{8,9},{10,11},{12,13},{14,15},{16,17},{18,... | collective-permute-start | bytes 61448 | tf_op jit(solution)/shard_map/ppermute | solution.py:450
  72.9 4.4 %collective-permute-start.1 = (f32[40,128]{1,0:T(8,128)S(1)}, f32[40,128]{1,0:T(8,128)S(1)}, u32[]{:S(2)}, u32[]{:S(2)}) collective-permute-start(f32[40,128]{1,0:T(8,128)S(1)} %shard_map.123.own_ref), channel_id=1, source_target_pairs={{1,2},{3,4},{5,6},{7,8},{9,10},{11,12},{13,14},{15,16},{17,18},{19... | collective-permute-start | bytes 61448 | tf_op jit(solution)/shard_map/ppermute | solution.py:450
  77.3 0.0 collective-permute-done.even_ref
  77.3 1.8 %collective-permute-done.1.odd_ref = f32[40,128]{1,0:T(8,128)S(1)} collective-permute-done((f32[40,128]{1,0:T(8,128)S(1)}, f32[40,128]{1,0:T(8,128)S(1)}, u32[]{:S(2)}, u32[]{:S(2)}) %collective-permute-start.1) | collective-permute-done | bytes 20512 | tf_op jit(solution)/shard_map/ppermute | solution.py:450
  79.2 1.2 %shard_map.124 = (f32[3,64]{1,0:T(4,128)}, f32[128,128]{1,0:T(8,128)S(1)}) custom-call(s32[1]{0:T(128)} %bitcast.5.place_ref, f32[40,128]{1,0:T(8,128)S(1)} %shard_map.123.own_ref, f32[40,128]{1,0:T(8,128)S(1)} %collective-permute-done.even_ref, f32[40,128]{1,0:T(8,128)S(1)} %collective-permute-done.1.odd_ref, f32[640,128]{1,0:T(8,128)S(1)} %bitcast.15), custom_call_target="tpu_custom_call" | custom-call | tf_op jit(solution)/shard_map/pallas_call | solution.py:397
  80.3 24.5 %all_to_all.17 = f32[128,1,128]{2,1,0:T(1,128)S(1)} all-to-all(f32[128,1,128]{2,1,0:T(1,128)S(1)} %bitcast.23), channel_id=1, replica_groups=mesh['src'=128,'seg'=4] {'src'}, dimensions={0} | all-to-all | bytes 131072 | tf_op jit(solution)/shard_map/all_to_all | solution.py:461
  104.8 0.6 subtract_bitcast_fusion
  (4 shorter events, 0.0 us)
Async XLA Ops:
  5.1 12.5 %copy-start = (f32[5,16384]{1,0:T(8,128)S(1)}, f32[5,16384]{1,0:T(8,128)}, u32[]{:S(2)}) copy-start(f32[5,16384]{1,0:T(8,128)} %part_ref.3) | copy-start | bytes 983044
  5.1 12.5 %copy-start.1 = (f32[3,16384]{1,0:T(4,128)S(1)}, f32[3,16384]{1,0:T(4,128)}, u32[]{:S(2)}) copy-start(f32[3,16384]{1,0:T(4,128)} %dir_ref.1) | copy-start | bytes 589828
  5.1 12.5 %copy-start.2 = (f32[16384]{0:T(1024)S(1)}, f32[16384]{0:T(1024)}, u32[]{:S(2)}) copy-start(f32[16384]{0:T(1024)} %param.10) | copy-start | bytes 196612
  5.1 12.5 %copy-start.3 = (s32[16384]{0:T(1024)S(1)}, s32[16384]{0:T(1024)}, u32[]{:S(2)}) copy-start(s32[16384]{0:T(1024)} %param.17) | copy-start | bytes 196612
  5.1 12.5 %copy-start.4 = (f32[5,2048]{1,0:T(8,128)S(1)}, f32[5,2048]{1,0:T(8,128)}, u32[]{:S(2)}) copy-start(f32[5,2048]{1,0:T(8,128)} %prior_ref.2) | copy-start | bytes 122884
  5.1 12.5 %copy-start.5 = (f32[16384]{0:T(1024)S(1)}, f32[16384]{0:T(1024)}, u32[]{:S(2)}) copy-start(f32[16384]{0:T(1024)} %param.12) | copy-start | bytes 196612
  5.2 12.4 %copy-start.6 = (s32[16384]{0:T(1024)S(1)}, s32[16384]{0:T(1024)}, u32[]{:S(2)}) copy-start(s32[16384]{0:T(1024)} %param.18) | copy-start | bytes 196612
  19.8 48.4 %copy-start.7 = (f32[3,64]{1,0:T(4,128)S(1)}, f32[3,64]{1,0:T(4,128)}, u32[]{:S(2)}) copy-start(f32[3,64]{1,0:T(4,128)} %prior_ref.3) | copy-start | bytes 2308
  70.7 6.7 %collective-permute-start = (f32[40,128]{1,0:T(8,128)S(1)}, f32[40,128]{1,0:T(8,128)S(1)}, u32[]{:S(2)}, u32[]{:S(2)}) collective-permute-start(f32[40,128]{1,0:T(8,128)S(1)} %shard_map.123.own_ref), channel_id=1, source_target_pairs={{0,1},{2,3},{4,5},{6,7},{8,9},{10,11},{12,13},{14,15},{16,17},{18,... | collective-permute-start | bytes 61448 | tf_op jit(solution)/shard_map/ppermute | solution.py:450
  72.9 6.3 %collective-permute-start.1 = (f32[40,128]{1,0:T(8,128)S(1)}, f32[40,128]{1,0:T(8,128)S(1)}, u32[]{:S(2)}, u32[]{:S(2)}) collective-permute-start(f32[40,128]{1,0:T(8,128)S(1)} %shard_map.123.own_ref), channel_id=1, source_target_pairs={{1,2},{3,4},{5,6},{7,8},{9,10},{11,12},{13,14},{15,16},{17,18},{19... | collective-permute-start | bytes 61448 | tf_op jit(solution)/shard_map/ppermute | solution.py:450

commit v7 on v6

--- a/solution.py
+++ b/solution.py
@@ -317,7 +317,7 @@
     return total
 
 
-def attitude_kernel(place_ref, own_ref, even_ref, odd_ref, slots_ref, att_far, corr_ref, att_ref, sem, *, knots_total):
+def attitude_kernel(place_ref, own_ref, even_ref, odd_ref, slots_ref, att_ref, corr_ref, *, knots_total):
     place = place_ref[0]
     lane = lax.broadcasted_iota(jnp.int32, (1, 128), 1)
     lane8 = lax.broadcasted_iota(jnp.int32, (8, 128), 1)
@@ -358,8 +358,6 @@
             applied = applied + pltpu.roll(columns_apply(upper_cols[d - 1], att), d, 1)
         att = att + columns_apply(inverse, rhs - applied)
     att_ref[...] = pltpu.roll(att, 128 - LEFT, 1)[0:3, 0:64]
-    att_copy = pltpu.make_async_copy(att_ref, att_far, sem)
-    att_copy.start()
     tables = [jnp.broadcast_to(att[j : j + 1], (8, 128)) for j in range(3)]
 
     def group(g, carry):
@@ -379,7 +377,16 @@
         return carry
 
     lax.fori_loop(0, 16, group, 0, unroll=8)
+
+
+def finish_kernel(base_ref, scale_ref, returned_ref, att_ref, residual_far, att_far, residual_ref, sems):
+    att_copy = pltpu.make_async_copy(att_ref, att_far, sems.at[0])
+    att_copy.start()
+    residual_ref[...] = base_ref[...] - scale_ref[...] * returned_ref[...]
+    residual_copy = pltpu.make_async_copy(residual_ref, residual_far, sems.at[1])
+    residual_copy.start()
     att_copy.wait()
+    residual_copy.wait()
 
 
 def call(kernel, outs, n_in, smem_at=(), scratch=(), far_in=(), far_out=()):
@@ -450,17 +457,19 @@
         swaps[start] = lax.ppermute(frame, both, pairs + [(b, a) for a, b in pairs])
     place = lax.axis_index(both).astype(jnp.int32).reshape(1)
     att_update, correction = call(
-        functools.partial(attitude_kernel, knots_total=devices * 64),
-        [(3, 64), (128, 128)],
-        5,
-        (0,),
-        [pltpu.VMEM((3, 64), jnp.float32), pltpu.SemaphoreType.DMA],
-        (),
-        (0,),
+        functools.partial(attitude_kernel, knots_total=devices * 64), [(3, 64), (128, 128)], 5, (0,), ()
     )(place, frame, swaps[0], swaps[1], arrived)
     returned = lax.all_to_all(correction.reshape(128, 1, 128), "src", split_axis=0, concat_axis=0, tiled=True)
-    residual_out = base - scale * returned.reshape(128, 128)
-    return src_update, att_update, residual_out.reshape(-1)
+    residual_out, att_out = call(
+        finish_kernel,
+        [(128, 128), (3, 64)],
+        4,
+        (),
+        [pltpu.VMEM((128, 128), jnp.float32), pltpu.SemaphoreType.DMA((2,))],
+        (),
+        (0, 1),
+    )(base, scale, returned.reshape(128, 128), att_update)
+    return src_update, att_out, residual_out.reshape(-1)
 
 
 def solution(mesh):

time: 106 us -> 106 us (level)
    pallas_call x4 -> x5, Pallas kernels: 10.2 us -> 10.8 us  [on_chip(): return run(*near)]
where the time goes in v7:
time: 106 us; the launch traced here: 105 us
  blocking collectives  85.3 us (80%)
  Pallas kernels  10.8 us (10%)
  starting transfers between devices  6.63 us (6%)
  waiting for transfers between devices  1.85 us (2%)
    all_to_all x1, blocking collectives, body(): lax.all_to_all(packed.reshape(128, 1, 640), 'src', split_axis=0, concat_a...  48.4 us
    all_to_all x1, blocking collectives, body(): lax.all_to_all(correction.reshape(128, 1, 128), 'src', split_axis=0, conc...  24.5 us
    all_to_all x1, blocking collectives, body(): lax.all_to_all(sums, 'seg', split_axis=0, concat_axis=0, tiled=True)  12.4 us
    pallas_call x5, Pallas kernels, on_chip(): return run(*near)  10.8 us
    ppermute x2, starting transfers between devices, body(): swaps[start] = lax.ppermute(frame, both, pairs + [(b, a) for a, b in pairs])  6.63 us
  transfers between devices with their start and end apart: 2, of which 1 were waited for; matrix products, arithmetic and copies ran while one was open for 0% of the time, Pallas kernels for 0%

profile of v7, /device:TPU:1, one launch (start us, length us, event | category | flops | bytes accessed | tf_op | source)
XLA Modules:
  0.0 105.5 jit_solution(2279829848072338194)
XLA Ops:
  0.6 4.4 %shard_map.121 = (f32[4,320,128]{2,1,0:T(8,128)S(1)}, f32[128,128]{1,0:T(8,128)S(1)}) custom-call(s32[1,128]{1,0:T(1,128)} %count_ref.1, f32[128,128]{1,0:T(8,128)} %bitcast.16, f32[128,128]{1,0:T(8,128)} %bitcast.24, f32[5,16384]{1,0:T(8,128)} %part_ref.3, s32[128,128]{1,0:T(8,128)} %bitcast.18), custom_call_target="tpu_custom_call" | custom-call | tf_op jit(solution)/shard_map/pallas_call | solution.py:404
  5.1 0.0 copy-start
  5.1 0.0 copy-start.1
  5.1 0.0 copy-start.2
  5.1 0.0 copy-start.3
  5.1 0.0 copy-start.4
  5.1 0.0 copy-start.5
  5.2 0.0 copy-start.6
  5.2 12.4 %all_to_all.15.sums_ref = f32[4,320,128]{2,1,0:T(8,128)S(1)} all-to-all(f32[4,320,128]{2,1,0:T(8,128)S(1)} %get-tuple-element.13), channel_id=1, replica_groups=mesh['src'=128,'seg'=4] {'seg'}, dimensions={0} | all-to-all | bytes 1310720 | tf_op jit(solution)/shard_map/all_to_all | solution.py:425
  17.6 0.0 copy-done
  17.6 0.0 copy-done.1
  17.6 0.0 copy-done.2
  17.6 0.0 copy-done.3
  17.6 2.1 %shard_map.122 = (f32[5,2048]{1,0:T(8,128)}, f32[640,128]{1,0:T(8,128)S(1)}, f32[128,128]{1,0:T(8,128)S(1)}, f32[128,128]{1,0:T(8,128)S(1)}) custom-call(f32[4,320,128]{2,1,0:T(8,128)S(1)} %all_to_all.15.sums_ref, f32[5,2048]{1,0:T(8,128)S(1)} %copy-done.4, f32[128,128]{1,0:T(8,128)S(1)} %bitcast.17, f32[128,128]{1,0:T(8,128)S(1)} %get-tuple-element.14.live_ref, ...), custom_call_target="tpu_custom_call" | custom-call | tf_op jit(solution)/shard_map/pallas_call | solution.py:404
  19.8 0.0 copy-start.7
  19.8 48.4 %all_to_all.16 = f32[128,1,640]{2,1,0:T(1,128)S(1)} all-to-all(f32[128,1,640]{2,1,0:T(1,128)S(1)} %bitcast.15), channel_id=1, replica_groups=mesh['src'=128,'seg'=4] {'src'}, dimensions={0} | all-to-all | bytes 655360 | tf_op jit(solution)/shard_map/all_to_all | solution.py:440
  68.2 2.4 %shard_map.123.own_ref = f32[40,128]{1,0:T(8,128)S(1)} custom-call(f32[640,128]{1,0:T(8,128)S(1)} %bitcast.13, f32[3,64]{1,0:T(4,128)S(1)} %copy-done.7), custom_call_target="tpu_custom_call" | custom-call | tf_op jit(solution)/shard_map/pallas_call | solution.py:404
  70.7 2.2 %collective-permute-start = (f32[40,128]{1,0:T(8,128)S(1)}, f32[40,128]{1,0:T(8,128)S(1)}, u32[]{:S(2)}, u32[]{:S(2)}) collective-permute-start(f32[40,128]{1,0:T(8,128)S(1)} %shard_map.123.own_ref), channel_id=1, source_target_pairs={{0,1},{2,3},{4,5},{6,7},{8,9},{10,11},{12,13},{14,15},{16,17},{18,... | collective-permute-start | bytes 61448 | tf_op jit(solution)/shard_map/ppermute | solution.py:457
  72.9 4.4 %collective-permute-start.1 = (f32[40,128]{1,0:T(8,128)S(1)}, f32[40,128]{1,0:T(8,128)S(1)}, u32[]{:S(2)}, u32[]{:S(2)}) collective-permute-start(f32[40,128]{1,0:T(8,128)S(1)} %shard_map.123.own_ref), channel_id=1, source_target_pairs={{1,2},{3,4},{5,6},{7,8},{9,10},{11,12},{13,14},{15,16},{17,18},{19... | collective-permute-start | bytes 61448 | tf_op jit(solution)/shard_map/ppermute | solution.py:457
  77.3 0.0 collective-permute-done.even_ref
  77.3 1.8 %collective-permute-done.1.odd_ref = f32[40,128]{1,0:T(8,128)S(1)} collective-permute-done((f32[40,128]{1,0:T(8,128)S(1)}, f32[40,128]{1,0:T(8,128)S(1)}, u32[]{:S(2)}, u32[]{:S(2)}) %collective-permute-start.1) | collective-permute-done | bytes 20512 | tf_op jit(solution)/shard_map/ppermute | solution.py:457
  79.2 1.1 %shard_map.124 = (f32[3,64]{1,0:T(4,128)S(1)}, f32[128,128]{1,0:T(8,128)S(1)}) custom-call(s32[1]{0:T(128)} %bitcast.5.place_ref, f32[40,128]{1,0:T(8,128)S(1)} %shard_map.123.own_ref, f32[40,128]{1,0:T(8,128)S(1)} %collective-permute-done.even_ref, f32[40,128]{1,0:T(8,128)S(1)} %collective-permute-done.1.odd_ref, f32[640,128]{1,0:T(8,128)S(1)} %bitcast.14), custom_call_target="tpu_custom_call" | custom-call | tf_op jit(solution)/shard_map/pallas_call | solution.py:404
  80.3 24.5 %all_to_all.17 = f32[128,1,128]{2,1,0:T(1,128)S(1)} all-to-all(f32[128,1,128]{2,1,0:T(1,128)S(1)} %bitcast.23), channel_id=1, replica_groups=mesh['src'=128,'seg'=4] {'src'}, dimensions={0} | all-to-all | bytes 131072 | tf_op jit(solution)/shard_map/all_to_all | solution.py:462
  104.8 0.7 shard_map.125
  (4 shorter events, 0.0 us)
Async XLA Ops:
  5.1 12.5 %copy-start = (f32[5,16384]{1,0:T(8,128)S(1)}, f32[5,16384]{1,0:T(8,128)}, u32[]{:S(2)}) copy-start(f32[5,16384]{1,0:T(8,128)} %part_ref.3) | copy-start | bytes 983044
  5.1 12.5 %copy-start.1 = (f32[3,16384]{1,0:T(4,128)S(1)}, f32[3,16384]{1,0:T(4,128)}, u32[]{:S(2)}) copy-start(f32[3,16384]{1,0:T(4,128)} %dir_ref.1) | copy-start | bytes 589828
  5.1 12.5 %copy-start.2 = (f32[16384]{0:T(1024)S(1)}, f32[16384]{0:T(1024)}, u32[]{:S(2)}) copy-start(f32[16384]{0:T(1024)} %param.10) | copy-start | bytes 196612
  5.1 12.5 %copy-start.3 = (s32[16384]{0:T(1024)S(1)}, s32[16384]{0:T(1024)}, u32[]{:S(2)}) copy-start(s32[16384]{0:T(1024)} %param.17) | copy-start | bytes 196612
  5.1 12.5 %copy-start.4 = (f32[5,2048]{1,0:T(8,128)S(1)}, f32[5,2048]{1,0:T(8,128)}, u32[]{:S(2)}) copy-start(f32[5,2048]{1,0:T(8,128)} %prior_ref.2) | copy-start | bytes 122884
  5.1 12.5 %copy-start.5 = (f32[16384]{0:T(1024)S(1)}, f32[16384]{0:T(1024)}, u32[]{:S(2)}) copy-start(f32[16384]{0:T(1024)} %param.12) | copy-start | bytes 196612
  5.2 12.4 %copy-start.6 = (s32[16384]{0:T(1024)S(1)}, s32[16384]{0:T(1024)}, u32[]{:S(2)}) copy-start(s32[16384]{0:T(1024)} %param.18) | copy-start | bytes 196612
  19.8 48.4 %copy-start.7 = (f32[3,64]{1,0:T(4,128)S(1)}, f32[3,64]{1,0:T(4,128)}, u32[]{:S(2)}) copy-start(f32[3,64]{1,0:T(4,128)} %prior_ref.3) | copy-start | bytes 2308
  70.7 6.7 %collective-permute-start = (f32[40,128]{1,0:T(8,128)S(1)}, f32[40,128]{1,0:T(8,128)S(1)}, u32[]{:S(2)}, u32[]{:S(2)}) collective-permute-start(f32[40,128]{1,0:T(8,128)S(1)} %shard_map.123.own_ref), channel_id=1, source_target_pairs={{0,1},{2,3},{4,5},{6,7},{8,9},{10,11},{12,13},{14,15},{16,17},{18,... | collective-permute-start | bytes 61448 | tf_op jit(solution)/shard_map/ppermute | solution.py:457
  72.9 6.3 %collective-permute-start.1 = (f32[40,128]{1,0:T(8,128)S(1)}, f32[40,128]{1,0:T(8,128)S(1)}, u32[]{:S(2)}, u32[]{:S(2)}) collective-permute-start(f32[40,128]{1,0:T(8,128)S(1)} %shard_map.123.own_ref), channel_id=1, source_target_pairs={{1,2},{3,4},{5,6},{7,8},{9,10},{11,12},{13,14},{15,16},{17,18},{19... | collective-permute-start | bytes 61448 | tf_op jit(solution)/shard_map/ppermute | solution.py:457

commit v8 on v7

--- a/solution.py
+++ b/solution.py
@@ -317,8 +317,8 @@
     return total
 
 
-def attitude_kernel(place_ref, own_ref, even_ref, odd_ref, slots_ref, att_ref, corr_ref, *, knots_total):
-    place = place_ref[0]
+def attitude_kernel(own_ref, even_ref, odd_ref, slots_ref, att_ref, corr_ref, *, knots_total):
+    place = lax.axis_index(("src", "seg"))
     lane = lax.broadcasted_iota(jnp.int32, (1, 128), 1)
     lane8 = lax.broadcasted_iota(jnp.int32, (8, 128), 1)
     is_even = place % 2 == 0
@@ -455,10 +455,9 @@
     for start in (1, 0):
         pairs = [(i, i + 1) for i in range(start, devices - 1, 2)]
         swaps[start] = lax.ppermute(frame, both, pairs + [(b, a) for a, b in pairs])
-    place = lax.axis_index(both).astype(jnp.int32).reshape(1)
     att_update, correction = call(
-        functools.partial(attitude_kernel, knots_total=devices * 64), [(3, 64), (128, 128)], 5, (0,), ()
-    )(place, frame, swaps[0], swaps[1], arrived)
+        functools.partial(attitude_kernel, knots_total=devices * 64), [(3, 64), (128, 128)], 4, (), ()
+    )(frame, swaps[0], swaps[1], arrived)
     returned = lax.all_to_all(correction.reshape(128, 1, 128), "src", split_axis=0, concat_axis=0, tiled=True)
     residual_out, att_out = call(
         finish_kernel,

time: 106 us -> 104 us (0.981)
  blocking collectives: 85.3 us -> 82.8 us
    all_to_all x1, blocking collectives: 24.5 us -> 22 us  [body(): lax.all_to_all(correction.reshape(128, 1, 128), 'src', split_axis=0, conc...]
where the time goes in v8:
time: 104 us
  blocking collectives  82.8 us (80%)
  Pallas kernels  10.8 us (10%)
  starting transfers between devices  6.43 us (6%)
  waiting for transfers between devices  2.59 us (2%)
    all_to_all x1, blocking collectives, body(): lax.all_to_all(packed.reshape(128, 1, 640), 'src', split_axis=0, concat_a...  48.4 us
    all_to_all x1, blocking collectives, body(): lax.all_to_all(correction.reshape(128, 1, 128), 'src', split_axis=0, conc...  22 us
    all_to_all x1, blocking collectives, body(): lax.all_to_all(sums, 'seg', split_axis=0, concat_axis=0, tiled=True)  12.4 us
    pallas_call x5, Pallas kernels, on_chip(): return run(*near)  10.8 us
    ppermute x2, starting transfers between devices, body(): swaps[start] = lax.ppermute(frame, both, pairs + [(b, a) for a, b in pairs])  6.43 us
    ppermute x2, waiting for transfers between devices, body(): swaps[start] = lax.ppermute(frame, both, pairs + [(b, a) for a, b in pairs])  2.59 us
  transfers between devices with their start and end apart: 2, of which 1 were waited for; matrix products, arithmetic and copies ran while one was open for 0% of the time, Pallas kernels for 0%

profile of v8, /device:TPU:1, one launch (start us, length us, event | category | flops | bytes accessed | tf_op | source)
XLA Modules:
  0.0 103.5 jit_solution(4189894075732869139)
XLA Ops:
  0.6 4.4 %shard_map.121 = (f32[4,320,128]{2,1,0:T(8,128)S(1)}, f32[128,128]{1,0:T(8,128)S(1)}) custom-call(s32[1,128]{1,0:T(1,128)} %count_ref.1, f32[128,128]{1,0:T(8,128)} %bitcast.15, f32[128,128]{1,0:T(8,128)} %bitcast.23, f32[5,16384]{1,0:T(8,128)} %part_ref.3, s32[128,128]{1,0:T(8,128)} %bitcast.17), custom_call_target="tpu_custom_call" | custom-call | tf_op jit(solution)/shard_map/pallas_call | solution.py:404
  5.1 0.0 copy-start
  5.1 0.0 copy-start.1
  5.1 0.0 copy-start.2
  5.1 0.0 copy-start.3
  5.1 0.0 copy-start.4
  5.1 0.0 copy-start.5
  5.2 0.0 copy-start.6
  5.2 12.4 %all_to_all.15.sums_ref = f32[4,320,128]{2,1,0:T(8,128)S(1)} all-to-all(f32[4,320,128]{2,1,0:T(8,128)S(1)} %get-tuple-element.13), channel_id=1, replica_groups=mesh['src'=128,'seg'=4] {'seg'}, dimensions={0} | all-to-all | bytes 1310720 | tf_op jit(solution)/shard_map/all_to_all | solution.py:425
  17.6 0.0 copy-done
  17.6 0.0 copy-done.1
  17.6 0.0 copy-done.2
  17.6 0.0 copy-done.3
  17.6 2.1 %shard_map.122 = (f32[5,2048]{1,0:T(8,128)}, f32[640,128]{1,0:T(8,128)S(1)}, f32[128,128]{1,0:T(8,128)S(1)}, f32[128,128]{1,0:T(8,128)S(1)}) custom-call(f32[4,320,128]{2,1,0:T(8,128)S(1)} %all_to_all.15.sums_ref, f32[5,2048]{1,0:T(8,128)S(1)} %copy-done.4, f32[128,128]{1,0:T(8,128)S(1)} %bitcast.16, f32[128,128]{1,0:T(8,128)S(1)} %get-tuple-element.14.live_ref, ...), custom_call_target="tpu_custom_call" | custom-call | tf_op jit(solution)/shard_map/pallas_call | solution.py:404
  19.8 0.0 copy-start.7
  19.8 48.4 %all_to_all.16 = f32[128,1,640]{2,1,0:T(1,128)S(1)} all-to-all(f32[128,1,640]{2,1,0:T(1,128)S(1)} %bitcast.14), channel_id=1, replica_groups=mesh['src'=128,'seg'=4] {'src'}, dimensions={0} | all-to-all | bytes 655360 | tf_op jit(solution)/shard_map/all_to_all | solution.py:440
  68.2 2.4 %shard_map.123.own_ref = f32[40,128]{1,0:T(8,128)S(1)} custom-call(f32[640,128]{1,0:T(8,128)S(1)} %bitcast.12, f32[3,64]{1,0:T(4,128)S(1)} %copy-done.7), custom_call_target="tpu_custom_call" | custom-call | tf_op jit(solution)/shard_map/pallas_call | solution.py:404
  70.7 4.5 %collective-permute-start.1 = (f32[40,128]{1,0:T(8,128)S(1)}, f32[40,128]{1,0:T(8,128)S(1)}, u32[]{:S(2)}, u32[]{:S(2)}) collective-permute-start(f32[40,128]{1,0:T(8,128)S(1)} %shard_map.123.own_ref), channel_id=1, source_target_pairs={{1,2},{3,4},{5,6},{7,8},{9,10},{11,12},{13,14},{15,16},{17,18},{19... | collective-permute-start | bytes 61448 | tf_op jit(solution)/shard_map/ppermute | solution.py:457
  75.2 1.9 %collective-permute-start = (f32[40,128]{1,0:T(8,128)S(1)}, f32[40,128]{1,0:T(8,128)S(1)}, u32[]{:S(2)}, u32[]{:S(2)}) collective-permute-start(f32[40,128]{1,0:T(8,128)S(1)} %shard_map.123.own_ref), channel_id=1, source_target_pairs={{0,1},{2,3},{4,5},{6,7},{8,9},{10,11},{12,13},{14,15},{16,17},{18,... | collective-permute-start | bytes 61448 | tf_op jit(solution)/shard_map/ppermute | solution.py:457
  77.1 0.0 collective-permute-done.1.odd_ref
  77.1 2.6 %collective-permute-done.even_ref = f32[40,128]{1,0:T(8,128)S(1)} collective-permute-done((f32[40,128]{1,0:T(8,128)S(1)}, f32[40,128]{1,0:T(8,128)S(1)}, u32[]{:S(2)}, u32[]{:S(2)}) %collective-permute-start) | collective-permute-done | bytes 20512 | tf_op jit(solution)/shard_map/ppermute | solution.py:457
  79.7 1.2 %shard_map.124 = (f32[3,64]{1,0:T(4,128)S(1)}, f32[128,128]{1,0:T(8,128)S(1)}) custom-call(f32[40,128]{1,0:T(8,128)S(1)} %shard_map.123.own_ref, f32[40,128]{1,0:T(8,128)S(1)} %collective-permute-done.even_ref, f32[40,128]{1,0:T(8,128)S(1)} %collective-permute-done.1.odd_ref, f32[640,128]{1,0:T(8,128)S(1)} %bitcast.13), custom_call_target="tpu_custom_call" | custom-call | tf_op jit(solution)/shard_map/pallas_call | solution.py:404
  80.9 22.0 %all_to_all.17 = f32[128,1,128]{2,1,0:T(1,128)S(1)} all-to-all(f32[128,1,128]{2,1,0:T(1,128)S(1)} %bitcast.22), channel_id=1, replica_groups=mesh['src'=128,'seg'=4] {'src'}, dimensions={0} | all-to-all | bytes 131072 | tf_op jit(solution)/shard_map/all_to_all | solution.py:461
  102.8 0.7 shard_map.125
  (4 shorter events, 0.0 us)
Async XLA Ops:
  5.1 12.5 %copy-start = (f32[5,16384]{1,0:T(8,128)S(1)}, f32[5,16384]{1,0:T(8,128)}, u32[]{:S(2)}) copy-start(f32[5,16384]{1,0:T(8,128)} %part_ref.3) | copy-start | bytes 983044
  5.1 12.5 %copy-start.1 = (f32[3,16384]{1,0:T(4,128)S(1)}, f32[3,16384]{1,0:T(4,128)}, u32[]{:S(2)}) copy-start(f32[3,16384]{1,0:T(4,128)} %dir_ref.1) | copy-start | bytes 589828
  5.1 12.5 %copy-start.2 = (f32[16384]{0:T(1024)S(1)}, f32[16384]{0:T(1024)}, u32[]{:S(2)}) copy-start(f32[16384]{0:T(1024)} %param.10) | copy-start | bytes 196612
  5.1 12.5 %copy-start.3 = (s32[16384]{0:T(1024)S(1)}, s32[16384]{0:T(1024)}, u32[]{:S(2)}) copy-start(s32[16384]{0:T(1024)} %param.17) | copy-start | bytes 196612
  5.1 12.5 %copy-start.4 = (f32[5,2048]{1,0:T(8,128)S(1)}, f32[5,2048]{1,0:T(8,128)}, u32[]{:S(2)}) copy-start(f32[5,2048]{1,0:T(8,128)} %prior_ref.2) | copy-start | bytes 122884
  5.1 12.5 %copy-start.5 = (f32[16384]{0:T(1024)S(1)}, f32[16384]{0:T(1024)}, u32[]{:S(2)}) copy-start(f32[16384]{0:T(1024)} %param.12) | copy-start | bytes 196612
  5.2 12.4 %copy-start.6 = (s32[16384]{0:T(1024)S(1)}, s32[16384]{0:T(1024)}, u32[]{:S(2)}) copy-start(s32[16384]{0:T(1024)} %param.18) | copy-start | bytes 196612
  19.8 48.4 %copy-start.7 = (f32[3,64]{1,0:T(4,128)S(1)}, f32[3,64]{1,0:T(4,128)}, u32[]{:S(2)}) copy-start(f32[3,64]{1,0:T(4,128)} %prior_ref.3) | copy-start | bytes 2308
  70.7 6.4 %collective-permute-start.1 = (f32[40,128]{1,0:T(8,128)S(1)}, f32[40,128]{1,0:T(8,128)S(1)}, u32[]{:S(2)}, u32[]{:S(2)}) collective-permute-start(f32[40,128]{1,0:T(8,128)S(1)} %shard_map.123.own_ref), channel_id=1, source_target_pairs={{1,2},{3,4},{5,6},{7,8},{9,10},{11,12},{13,14},{15,16},{17,18},{19... | collective-permute-start | bytes 61448 | tf_op jit(solution)/shard_map/ppermute | solution.py:457
  75.2 4.5 %collective-permute-start = (f32[40,128]{1,0:T(8,128)S(1)}, f32[40,128]{1,0:T(8,128)S(1)}, u32[]{:S(2)}, u32[]{:S(2)}) collective-permute-start(f32[40,128]{1,0:T(8,128)S(1)} %shard_map.123.own_ref), channel_id=1, source_target_pairs={{0,1},{2,3},{4,5},{6,7},{8,9},{10,11},{12,13},{14,15},{16,17},{18,... | collective-permute-start | bytes 61448 | tf_op jit(solution)/shard_map/ppermute | solution.py:457

commit v9 on v6

--- a/solution.py
+++ b/solution.py
@@ -20,8 +20,8 @@
 SMEM_SPEC = pl.BlockSpec(memory_space=pltpu.SMEM)
 ANY_SPEC = pl.BlockSpec(memory_space=pl.ANY)
 NT = (((1,), (1,)), ((), ()))
-SUMS_UNROLL = 8
-BAND_UNROLL = 8
+SUMS_UNROLL = 16
+BAND_UNROLL = 16
 
 
 def spline_weights(local_time):
@@ -317,8 +317,8 @@
     return total
 
 
-def attitude_kernel(place_ref, own_ref, even_ref, odd_ref, slots_ref, att_far, corr_ref, att_ref, sem, *, knots_total):
-    place = place_ref[0]
+def attitude_kernel(own_ref, even_ref, odd_ref, slots_ref, att_far, corr_ref, att_ref, sem, *, knots_total):
+    place = lax.axis_index(("src", "seg"))
     lane = lax.broadcasted_iota(jnp.int32, (1, 128), 1)
     lane8 = lax.broadcasted_iota(jnp.int32, (8, 128), 1)
     is_even = place % 2 == 0
@@ -448,16 +448,15 @@
     for start in (1, 0):
         pairs = [(i, i + 1) for i in range(start, devices - 1, 2)]
         swaps[start] = lax.ppermute(frame, both, pairs + [(b, a) for a, b in pairs])
-    place = lax.axis_index(both).astype(jnp.int32).reshape(1)
     att_update, correction = call(
         functools.partial(attitude_kernel, knots_total=devices * 64),
         [(3, 64), (128, 128)],
-        5,
-        (0,),
+        4,
+        (),
         [pltpu.VMEM((3, 64), jnp.float32), pltpu.SemaphoreType.DMA],
         (),
         (0,),
-    )(place, frame, swaps[0], swaps[1], arrived)
+    )(frame, swaps[0], swaps[1], arrived)
     returned = lax.all_to_all(correction.reshape(128, 1, 128), "src", split_axis=0, concat_axis=0, tiled=True)
     residual_out = base - scale * returned.reshape(128, 128)
     return src_update, att_update, residual_out.reshape(-1)

time: 106 us -> 103 us (0.972)
  blocking collectives: 85.3 us -> 82.8 us
    all_to_all x1, blocking collectives: 24.5 us -> 22 us  [body(): lax.all_to_all(correction.reshape(128, 1, 128), 'src', split_axis=0, conc...]
where the time goes in v9:
time: 103 us
  blocking collectives  82.8 us (80%)
  Pallas kernels  9.75 us (9%)
  starting transfers between devices  6.43 us (6%)
  waiting for transfers between devices  2.59 us (3%)
    all_to_all x1, blocking collectives, body(): lax.all_to_all(packed.reshape(128, 1, 640), 'src', split_axis=0, concat_a...  48.4 us
    all_to_all x1, blocking collectives, body(): lax.all_to_all(correction.reshape(128, 1, 128), 'src', split_axis=0, conc...  22 us
    all_to_all x1, blocking collectives, body(): lax.all_to_all(sums, 'seg', split_axis=0, concat_axis=0, tiled=True)  12.4 us
    pallas_call x4, Pallas kernels, on_chip(): return run(*near)  9.75 us
    ppermute x2, starting transfers between devices, body(): swaps[start] = lax.ppermute(frame, both, pairs + [(b, a) for a, b in pairs])  6.43 us
    ppermute x2, waiting for transfers between devices, body(): swaps[start] = lax.ppermute(frame, both, pairs + [(b, a) for a, b in pairs])  2.59 us
  transfers between devices with their start and end apart: 2, of which 1 were waited for; matrix products, arithmetic and copies ran while one was open for 0% of the time, Pallas kernels for 0%

profile of v9, /device:TPU:1, one launch (start us, length us, event | category | flops | bytes accessed | tf_op | source)
XLA Modules:
  0.0 103.1 jit_solution(459896216446399973)
XLA Ops:
  0.6 4.2 %shard_map.121 = (f32[4,320,128]{2,1,0:T(8,128)S(1)}, f32[128,128]{1,0:T(8,128)S(1)}) custom-call(s32[1,128]{1,0:T(1,128)} %count_ref.1, f32[128,128]{1,0:T(8,128)} %bitcast.16, f32[128,128]{1,0:T(8,128)} %bitcast.24, f32[5,16384]{1,0:T(8,128)} %part_ref.3, s32[128,128]{1,0:T(8,128)} %bitcast.18), custom_call_target="tpu_custom_call" | custom-call | tf_op jit(solution)/shard_map/pallas_call | solution.py:397
  4.8 0.0 copy-start
  4.9 0.0 copy-start.1
  4.9 0.0 copy-start.2
  4.9 0.0 copy-start.3
  4.9 0.0 copy-start.4
  4.9 0.0 copy-start.5
  4.9 0.0 copy-start.6
  4.9 12.4 %all_to_all.15.sums_ref = f32[4,320,128]{2,1,0:T(8,128)S(1)} all-to-all(f32[4,320,128]{2,1,0:T(8,128)S(1)} %get-tuple-element.11), channel_id=1, replica_groups=mesh['src'=128,'seg'=4] {'seg'}, dimensions={0} | all-to-all | bytes 1310720 | tf_op jit(solution)/shard_map/all_to_all | solution.py:418
  17.3 0.0 copy-done
  17.3 0.0 copy-done.1
  17.3 0.0 copy-done.2
  17.3 0.0 copy-done.3
  17.4 2.1 %shard_map.122 = (f32[5,2048]{1,0:T(8,128)}, f32[640,128]{1,0:T(8,128)S(1)}, f32[128,128]{1,0:T(8,128)S(1)}, f32[128,128]{1,0:T(8,128)S(1)}) custom-call(f32[4,320,128]{2,1,0:T(8,128)S(1)} %all_to_all.15.sums_ref, f32[5,2048]{1,0:T(8,128)S(1)} %copy-done.4, f32[128,128]{1,0:T(8,128)S(1)} %bitcast.17, f32[128,128]{1,0:T(8,128)S(1)} %get-tuple-element.12.live_ref, ...), custom_call_target="tpu_custom_call" | custom-call | tf_op jit(solution)/shard_map/pallas_call | solution.py:397
  19.5 0.0 copy-start.7
  19.5 48.4 %all_to_all.16 = f32[128,1,640]{2,1,0:T(1,128)S(1)} all-to-all(f32[128,1,640]{2,1,0:T(1,128)S(1)} %bitcast.15), channel_id=1, replica_groups=mesh['src'=128,'seg'=4] {'src'}, dimensions={0} | all-to-all | bytes 655360 | tf_op jit(solution)/shard_map/all_to_all | solution.py:433
  68.0 2.2 %shard_map.123.own_ref = f32[40,128]{1,0:T(8,128)S(1)} custom-call(f32[640,128]{1,0:T(8,128)S(1)} %bitcast.13, f32[3,64]{1,0:T(4,128)S(1)} %copy-done.7), custom_call_target="tpu_custom_call" | custom-call | tf_op jit(solution)/shard_map/pallas_call | solution.py:397
  70.2 4.5 %collective-permute-start.1 = (f32[40,128]{1,0:T(8,128)S(1)}, f32[40,128]{1,0:T(8,128)S(1)}, u32[]{:S(2)}, u32[]{:S(2)}) collective-permute-start(f32[40,128]{1,0:T(8,128)S(1)} %shard_map.123.own_ref), channel_id=1, source_target_pairs={{1,2},{3,4},{5,6},{7,8},{9,10},{11,12},{13,14},{15,16},{17,18},{19... | collective-permute-start | bytes 61448 | tf_op jit(solution)/shard_map/ppermute | solution.py:450
  74.7 1.9 %collective-permute-start = (f32[40,128]{1,0:T(8,128)S(1)}, f32[40,128]{1,0:T(8,128)S(1)}, u32[]{:S(2)}, u32[]{:S(2)}) collective-permute-start(f32[40,128]{1,0:T(8,128)S(1)} %shard_map.123.own_ref), channel_id=1, source_target_pairs={{0,1},{2,3},{4,5},{6,7},{8,9},{10,11},{12,13},{14,15},{16,17},{18,... | collective-permute-start | bytes 61448 | tf_op jit(solution)/shard_map/ppermute | solution.py:450
  76.7 0.0 collective-permute-done.1.odd_ref
  76.7 2.6 %collective-permute-done.even_ref = f32[40,128]{1,0:T(8,128)S(1)} collective-permute-done((f32[40,128]{1,0:T(8,128)S(1)}, f32[40,128]{1,0:T(8,128)S(1)}, u32[]{:S(2)}, u32[]{:S(2)}) %collective-permute-start) | collective-permute-done | bytes 20512 | tf_op jit(solution)/shard_map/ppermute | solution.py:450
  79.3 1.2 %shard_map.124 = (f32[3,64]{1,0:T(4,128)}, f32[128,128]{1,0:T(8,128)S(1)}) custom-call(f32[40,128]{1,0:T(8,128)S(1)} %shard_map.123.own_ref, f32[40,128]{1,0:T(8,128)S(1)} %collective-permute-done.even_ref, f32[40,128]{1,0:T(8,128)S(1)} %collective-permute-done.1.odd_ref, f32[640,128]{1,0:T(8,128)S(1)} %bitcast.14), custom_call_target="tpu_custom_call" | custom-call | tf_op jit(solution)/shard_map/pallas_call | solution.py:397
  80.4 22.0 %all_to_all.17 = f32[128,1,128]{2,1,0:T(1,128)S(1)} all-to-all(f32[128,1,128]{2,1,0:T(1,128)S(1)} %bitcast.22), channel_id=1, replica_groups=mesh['src'=128,'seg'=4] {'src'}, dimensions={0} | all-to-all | bytes 131072 | tf_op jit(solution)/shard_map/all_to_all | solution.py:460
  102.4 0.6 subtract_bitcast_fusion
  (4 shorter events, 0.0 us)
Async XLA Ops:
  4.8 12.5 %copy-start = (f32[5,16384]{1,0:T(8,128)S(1)}, f32[5,16384]{1,0:T(8,128)}, u32[]{:S(2)}) copy-start(f32[5,16384]{1,0:T(8,128)} %part_ref.3) | copy-start | bytes 983044
  4.9 12.5 %copy-start.1 = (f32[3,16384]{1,0:T(4,128)S(1)}, f32[3,16384]{1,0:T(4,128)}, u32[]{:S(2)}) copy-start(f32[3,16384]{1,0:T(4,128)} %dir_ref.1) | copy-start | bytes 589828
  4.9 12.5 %copy-start.2 = (f32[16384]{0:T(1024)S(1)}, f32[16384]{0:T(1024)}, u32[]{:S(2)}) copy-start(f32[16384]{0:T(1024)} %param.10) | copy-start | bytes 196612
  4.9 12.5 %copy-start.3 = (s32[16384]{0:T(1024)S(1)}, s32[16384]{0:T(1024)}, u32[]{:S(2)}) copy-start(s32[16384]{0:T(1024)} %param.17) | copy-start | bytes 196612
  4.9 12.5 %copy-start.4 = (f32[5,2048]{1,0:T(8,128)S(1)}, f32[5,2048]{1,0:T(8,128)}, u32[]{:S(2)}) copy-start(f32[5,2048]{1,0:T(8,128)} %prior_ref.2) | copy-start | bytes 122884
  4.9 12.5 %copy-start.5 = (f32[16384]{0:T(1024)S(1)}, f32[16384]{0:T(1024)}, u32[]{:S(2)}) copy-start(f32[16384]{0:T(1024)} %param.12) | copy-start | bytes 196612
  4.9 12.5 %copy-start.6 = (s32[16384]{0:T(1024)S(1)}, s32[16384]{0:T(1024)}, u32[]{:S(2)}) copy-start(s32[16384]{0:T(1024)} %param.18) | copy-start | bytes 196612
  19.5 48.4 %copy-start.7 = (f32[3,64]{1,0:T(4,128)S(1)}, f32[3,64]{1,0:T(4,128)}, u32[]{:S(2)}) copy-start(f32[3,64]{1,0:T(4,128)} %prior_ref.3) | copy-start | bytes 2308
  70.2 6.5 %collective-permute-start.1 = (f32[40,128]{1,0:T(8,128)S(1)}, f32[40,128]{1,0:T(8,128)S(1)}, u32[]{:S(2)}, u32[]{:S(2)}) collective-permute-start(f32[40,128]{1,0:T(8,128)S(1)} %shard_map.123.own_ref), channel_id=1, source_target_pairs={{1,2},{3,4},{5,6},{7,8},{9,10},{11,12},{13,14},{15,16},{17,18},{19... | collective-permute-start | bytes 61448 | tf_op jit(solution)/shard_map/ppermute | solution.py:450
  74.7 4.5 %collective-permute-start = (f32[40,128]{1,0:T(8,128)S(1)}, f32[40,128]{1,0:T(8,128)S(1)}, u32[]{:S(2)}, u32[]{:S(2)}) collective-permute-start(f32[40,128]{1,0:T(8,128)S(1)} %shard_map.123.own_ref), channel_id=1, source_target_pairs={{0,1},{2,3},{4,5},{6,7},{8,9},{10,11},{12,13},{14,15},{16,17},{18,... | collective-permute-start | bytes 61448 | tf_op jit(solution)/shard_map/ppermute | solution.py:450
